TPU v7x, 512 devices: a whole 4x4x16 slice. The times are simulated.
512 devices in a mesh: seq: 32 (over x, y, z_hi), tp: 16 (over z_lo, core).
Axes of the slice: x: 4, y: 4, z: 16 (z_hi: 2, z_lo: 8; z = z_hi * 8 + z_lo), core: 2. Of those that a mesh axis runs over, the one named last changes fastest.
Arguments:
- query_rows: bfloat16 [8192, 6144], P('seq', 'tp'), may hold values from -6 to 6
- key_rows: bfloat16 [8192, 6144], P('seq', 'tp'), may hold values from -6 to 6
- value_rows: bfloat16 [8192, 6144], P('seq', 'tp'), may hold values from -6 to 6
- log_decay: float32 [48, 8192], P('tp', 'seq'), as said below
- doc_starts: int32 [32, 3], P('seq'), may hold values from 0 to 256, as said below
- residual_in: bfloat16 [8192, 4096], P(('seq', 'tp')), may hold values from -6 to 6
- out_weight: bfloat16 [6144, 4096], P('tp'), may hold values from -0.078125 to 0.078125
- norm_gain: float32 [4096], replicated, may hold values from 0.5 to 1.5
Outputs:
- hidden_state: bfloat16 [8192, 4096], P(('seq', 'tp'))
- normed_state: bfloat16 [8192, 4096], P(('seq', 'tp'))
Inputs may be any that keep to these rules, and one draw needn't show every extreme that they name: `doc_starts`: each entry is a document's start offset within its shard; 256 marks an unused slot; the last entry of every row is 256; the first entry of shard 0 is 0; entries may repeat and need not be sorted. `log_decay`: every entry is negative.
All inputs are finite; a program needn't handle non-finite values.
Results may differ from a plain program's by a relative error of at most 0.022.
Values may be sent and summed in bfloat16 or wider, within the bound.
No kernel may reach another device: no remote copies, remote signals or barrier semaphores. Data moves between devices by JAX's collectives and lax.ppermute only.
A program may use at most 64 MiB of HBM per device.

v0:
```python
import jax
import jax.numpy as jnp
from jax import lax
from jax.sharding import PartitionSpec as P


def carried_in(x, axis, combine, identity):
    devices, position = (lax.axis_size(axis), lax.axis_index(axis))
    everything = jax.tree.map(
        lambda part, kind: lax.all_gather(part.astype(kind), axis), x, (jnp.bfloat16, jnp.bfloat16)
    )
    start = jax.tree.map(
        lambda part, zero: jnp.broadcast_to(jnp.asarray(zero, part.dtype), part.shape), x, identity
    )

    def lap(k, before):
        reached = k < position
        new = combine(
            before, jax.tree.map(lambda part, own: part[k].astype(own.dtype), everything, x)
        )
        return jax.tree.map(lambda a, b: jnp.where(reached, a, b), new, before)

    return lax.fori_loop(0, devices, lap, start)


def join_states(earlier, later_part):
    return (earlier[0] * later_part[0], later_part[0][:, None, None] * earlier[1] + later_part[1])


def shards(
    query_rows, key_rows, value_rows, log_decay, doc_starts, residual_in, out_weight, norm_gain
):
    span_len = query_rows.shape[0]
    heads_local = log_decay.shape[0]
    head_dim = query_rows.shape[1] // heads_local
    query_c = query_rows.reshape(span_len, heads_local, head_dim)
    key_c = key_rows.reshape(span_len, heads_local, head_dim)
    value_c = value_rows.reshape(span_len, heads_local, head_dim)
    positions = lax.iota(jnp.int32, span_len)
    starts = doc_starts[0]
    segment = jnp.sum((starts[None, :] <= positions[:, None]).astype(jnp.int32), axis=1)
    lower_mask = positions[:, None] >= positions[None, :]
    cumulative = jnp.dot(
        log_decay, lower_mask.astype(jnp.float32).T, precision=lax.Precision.HIGHEST
    )
    last_seg = segment[span_len - 1]
    tail_weight = (
        jnp.exp(cumulative[:, span_len - 1 :] - cumulative)
        * (segment == last_seg).astype(jnp.float32)[None, :]
    )
    decayed_keys = (key_c.astype(jnp.float32) * tail_weight.T[:, :, None]).astype(jnp.bfloat16)
    local_state = jnp.einsum(
        "jhd,jhe->hde", decayed_keys, value_c, preferred_element_type=jnp.float32
    )
    through = jnp.exp(cumulative[:, span_len - 1]) * (last_seg == 0).astype(jnp.float32)
    identity = (jnp.ones_like(through), jnp.zeros_like(local_state))
    prefix_decay, state_in = carried_in((through, local_state), "seq", join_states, identity)
    state_low = state_in.astype(jnp.bfloat16)
    same_doc = lower_mask & (segment[:, None] == segment[None, :])
    spread = cumulative[:, :, None] - cumulative[:, None, :]
    decay_mat = jnp.exp(jnp.where(same_doc[None], spread, -jnp.inf))
    scores = jnp.einsum("ihd,jhd->hij", query_c, key_c, preferred_element_type=jnp.float32)
    weights = (scores * decay_mat).astype(jnp.bfloat16)
    intra_out = jnp.einsum("hij,jhd->ihd", weights, value_c, preferred_element_type=jnp.float32)
    carry_scale = jnp.exp(cumulative) * (segment == 0).astype(jnp.float32)[None, :]
    inter_out = (
        jnp.einsum("ihd,hde->ihe", query_c, state_low, preferred_element_type=jnp.float32)
        * carry_scale.T[:, :, None]
    )
    mixed = intra_out + inter_out
    attended = (mixed * lax.rsqrt(jnp.mean(mixed * mixed, axis=2, keepdims=True) + 1e-06)).astype(
        jnp.bfloat16
    )
    attended = attended.reshape(span_len, heads_local * head_dim)
    projected = lax.psum_scatter(
        jnp.dot(attended, out_weight, preferred_element_type=jnp.float32).astype(jnp.bfloat16),
        "tp",
        scatter_dimension=0,
        tiled=True,
    ).astype(jnp.float32)
    hidden = residual_in.astype(jnp.float32) + projected
    scale = lax.rsqrt(jnp.mean(hidden * hidden, axis=1, keepdims=True) + 1e-05)
    normed_state = (hidden * scale * norm_gain[None, :]).astype(jnp.bfloat16)
    return (hidden.astype(jnp.bfloat16), normed_state)


def solution(mesh):
    return jax.shard_map(
        shards,
        mesh=mesh,
        in_specs=(
            P("seq", "tp"),
            P("seq", "tp"),
            P("seq", "tp"),
            P("tp", "seq"),
            P("seq", None),
            P(("seq", "tp"), None),
            P("tp", None),
            P(),
        ),
        out_specs=(P(("seq", "tp"), None), P(("seq", "tp"), None)),
        check_vma=False,
    )
```

profile of v0, /device:TPU:4, one launch (start us, length us, event | category | flops | bytes accessed | tf_op | source)
XLA Modules:
  0.0 381.0 jit_solution(14685253051950224929)
XLA Ops:
  7.2 0.9 convert_reduce_fusion
  8.7 1.2 compare_convert_fusion.1
  9.9 0.9 fusion.13
  10.8 0.9 slice_reduce_fusion
  11.6 1.1 copy.30
  12.7 1.1 copy.33
  13.8 0.8 exponential_multiply_fusion.1
  14.6 0.9 convolution_convert_fusion.1
  16.2 1.3 dynamic-slice
  18.8 1.3 dynamic-update-slice
  20.1 180.3 %all-reduce = bf16[96]{0:T(256)(128)(2,1)S(1)} all-reduce(bf16[96]{0:T(256)(128)(2,1)} %dynamic-update-slice), channel_id=2, replica_groups=mesh['seq'=32,'tp'=16] {'seq'}, use_global_device_ids=true, to_apply=%add | all-reduce | flops 96 | bytes 384
  200.4 0.7 reshape.122
  201.1 1.7 copy.29
  202.9 0.7 fusion.14
  203.6 54.1 %while.14 = (s32[]{:T(128)}, f32[3,128,128]{2,1,0:T(8,128)S(1)}, s32[]{:T(128)}, bf16[32,3]{1,0:T(8,128)(2,1)}, bf16[32,3,128,128]{3,2,1,0:T(8,128)(2,1)}, /*index=5*/s32[]{:T(128)}, s32[]{:T(128)}) while((s32[]{:T(128)}, f32[3,128,128]{2,1,0:T(8,128)S(1)}, s32[]{:T(128)}, bf16[32,3]{1,0:T(8,128)(2,1)}, ...), condition=%wide.region_2.3_spmd.clone, body=%wide.region_1.2_spmd.clone.sunk | while | flops 245767 | bytes 491655 | solution.py:23
  204.3 1.0 fusion.29
  205.3 0.7 bitcast_convert_fusion.2
  206.0 1.0 fusion.29
  207.0 0.7 bitcast_convert_fusion.2
  207.7 1.0 fusion.29
  208.7 0.7 bitcast_convert_fusion.2
  209.4 1.0 fusion.29
  210.4 0.7 bitcast_convert_fusion.2
  211.1 1.0 fusion.29
  212.1 0.7 bitcast_convert_fusion.2
  212.8 1.0 fusion.29
  213.8 0.7 bitcast_convert_fusion.2
  214.5 1.0 fusion.29
  215.5 0.7 bitcast_convert_fusion.2
  216.2 1.0 fusion.29
  217.9 1.0 fusion.29
  219.6 1.0 fusion.29
  221.3 1.0 fusion.29
  222.9 1.0 fusion.29
  224.6 1.0 fusion.29
  226.3 1.0 fusion.29
  228.0 1.0 fusion.29
  229.7 1.0 fusion.29
  231.4 1.0 fusion.29
  233.1 1.0 fusion.29
  234.8 1.0 fusion.29
  236.5 1.0 fusion.29
  238.2 1.0 fusion.29
  239.2 0.7 bitcast_convert_fusion.2
  239.9 1.0 fusion.29
  240.9 0.7 bitcast_convert_fusion.2
  241.6 1.0 fusion.29
  242.6 0.7 bitcast_convert_fusion.2
  243.3 1.0 fusion.29
  244.9 1.0 fusion.29
  246.6 1.0 fusion.29
  248.3 1.0 fusion.29
  250.0 1.0 fusion.29
  251.7 1.0 fusion.29
  253.4 1.0 fusion.29
  255.0 1.0 fusion.29
  256.7 1.0 fusion.29
  257.7 1.9 fusion.5
  259.7 2.5 multiply_reduce_fusion
  262.1 1.0 multiply_convert_fusion
  263.2 2.6 convolution_convert_fusion
  265.9 105.6 %reduce-scatter.2.cloned.1.call-done = bf16[16,4096]{1,0:T(8,128)(2,1)} async-done(((bf16[256,4096]{1,0:T(8,128)(2,1)}), bf16[16,4096]{1,0:T(8,128)(2,1)}) %reduce-scatter.2.cloned.1.call-update) | async-done | bytes 131088 | tf_op jit(solution)/shard_map/reduce_scatter | solution.py:75
  371.4 1.1 multiply_reduce_fusion.1
  372.5 1.7 multiply_convert_fusion.2
  (41 shorter events, 16.5 us)
Async XLA Ops:
  7.2 256.0 %copy-start = (bf16[384,4096]{1,0:T(8,128)(2,1)S(1)}, bf16[384,4096]{1,0:T(8,128)(2,1)}, u32[]{:S(2)}) copy-start(bf16[384,4096]{1,0:T(8,128)(2,1)} %param.16) | copy-start | bytes 9437188
  7.2 196.4 %all-gather.4.cloned.1.call-start = ((), (), s32[]{:S(2)}) async-start(), calls=%async_computation.2 | async-start | bytes 3244032 | tf_op jit(solution)/shard_map/all_gather | solution.py:10
  13.8 1.8 copy-start.1
  15.5 356.0 %reduce-scatter.2.cloned.1.call-start = ((), (), s32[]{:S(2)}) async-start(), calls=%async_computation.1 | async-start | bytes 2228224 | tf_op jit(solution)/shard_map/reduce_scatter | solution.py:75
  263.2 108.2 %copy-start.2 = (bf16[16,4096]{1,0:T(8,128)(2,1)S(1)}, bf16[16,4096]{1,0:T(8,128)(2,1)}, u32[]{:S(2)}) copy-start(bf16[16,4096]{1,0:T(8,128)(2,1)} %param.15) | copy-start | bytes 393220
  263.2 109.3 %copy-start.3 = (f32[4096]{0:T(1024)S(1)}, f32[4096]{0:T(1024)}, u32[]{:S(2)}) copy-start(f32[4096]{0:T(1024)} %param.17) | copy-start | bytes 49156
Sparse Core Ops, SparseCore 0:
  15.6 158.2 all-gather.3
  266.0 105.3 reduce-scatter.1
where the time goes:
time: 383 us; the launch traced here: 381 us
  blocking collectives  180 us (47%)
  waiting for transfers between devices  106 us (28%)
  other arithmetic  61.1 us (16%)
  between operations  15.4 us (4%)
  local copies, waits for them, and re-layouts  9.09 us (2%)
  matrix products  8.75 us (2%)
    unnamed x1, blocking collectives  180 us
    reduce_scatter x1, waiting for transfers between devices, shards(): lax.psum_scatter(jnp.dot(attended, out_weight, preferred_element_type=jnp...  106 us
    select_n x32, other arithmetic, lap(): return jax.tree.map(lambda a, b: jnp.where(reached, a, b), new, before)  31.6 us
    convert_element_type x32, other arithmetic, lap(): part[k].astype(own.dtype)  21.9 us
  transfers between devices with their start and end apart: 2, of which 1 were waited for; matrix products, arithmetic and copies ran while one was open for 2% of the time, Pallas kernels for 0%

commit v1 on v0

v1 whole, which is shorter than its diff:
```python
import jax
import jax.numpy as jnp
from jax import lax
from jax.experimental import pallas as pl
from jax.experimental.pallas import tpu as pltpu
from jax.sharding import PartitionSpec as P

SPAN = 256
HEADS = 3
HDIM = 128
STATE = HEADS * HDIM
PAYLOAD = STATE + 8
D = 4096
F32 = jnp.float32
BF16 = jnp.bfloat16

SHARDS = 32
FLIP_Z = [(i, i ^ 1) for i in range(SHARDS)]
ROW_Y = [[g + 2 * k for k in range(4)] for g in range(SHARDS) if g & 6 == 0]
ROW_X = [[g + 8 * k for k in range(4)] for g in range(8)]

VMEM = pl.BlockSpec(memory_space=pltpu.VMEM)
SMEM = pl.BlockSpec(memory_space=pltpu.SMEM)


def segment_of(starts_ref, positions):
    total = jnp.zeros(positions.shape, jnp.int32)
    for slot in range(3):
        total = total + (positions >= starts_ref[0, slot]).astype(jnp.int32)
    return total


def running_sums(weights, decay, column):
    dims = (((1,), (1,)), ((), ()))
    a, b = (weights, decay) if column else (decay, weights)
    return lax.dot_general(a, b, dims, precision=lax.Precision.HIGHEST, preferred_element_type=F32)


def grid_iotas():
    row = lax.broadcasted_iota(jnp.int32, (SPAN, SPAN), 0)
    col = lax.broadcasted_iota(jnp.int32, (SPAN, SPAN), 1)
    return row, col


def state_kernel(starts_ref, decay_ref, key_ref, value_ref, out_ref):
    row, col = grid_iotas()
    later = (col > row).astype(F32)
    decay = decay_ref[...]
    tail = running_sums(later, decay, True)
    segment = segment_of(starts_ref, lax.broadcasted_iota(jnp.int32, (SPAN, 1), 0))
    last = segment_of(starts_ref, jnp.full((1, 1), SPAN - 1, jnp.int32))
    tail_weight = jnp.exp(tail) * (segment == last).astype(F32)
    through = jnp.exp(jnp.sum(decay, axis=1, keepdims=True)) * (last == 0).astype(F32)
    high = through.astype(BF16).astype(F32)
    low = (through - high).astype(BF16).astype(F32)
    rows = jnp.concatenate([high, low, jnp.zeros((2, 1), F32)], axis=0)
    out_ref[STATE:, :] = jnp.broadcast_to(rows, (8, HDIM)).astype(BF16)
    for h in range(HEADS):
        cut = slice(h * HDIM, (h + 1) * HDIM)
        decayed = (key_ref[:, cut].astype(F32) * tail_weight[:, h : h + 1]).astype(BF16)
        out_ref[cut, :] = lax.dot_general(
            decayed, value_ref[:, cut], (((0,), (0,)), ((), ())), preferred_element_type=F32
        ).astype(BF16)


def intra_kernel(starts_ref, decay_ref, query_ref, key_ref, value_ref, out_ref):
    row, col = grid_iotas()
    lower = row >= col
    lower_f = lower.astype(F32)
    decay = decay_ref[...]
    cum_col = running_sums(lower_f, decay, True)
    cum_row = running_sums(lower_f, decay, False)
    seg_col = segment_of(starts_ref, lax.broadcasted_iota(jnp.int32, (SPAN, 1), 0))
    seg_row = segment_of(starts_ref, lax.broadcasted_iota(jnp.int32, (1, SPAN), 1))
    same = lower & (seg_col == seg_row)
    for h in range(HEADS):
        cut = slice(h * HDIM, (h + 1) * HDIM)
        spread = cum_col[:, h : h + 1] - cum_row[h : h + 1, :]
        decay_mat = jnp.exp(jnp.where(same, spread, -jnp.inf))
        scores = lax.dot_general(
            query_ref[:, cut], key_ref[:, cut], (((1,), (1,)), ((), ())), preferred_element_type=F32
        )
        weights = (scores * decay_mat).astype(BF16)
        out_ref[:, cut] = jnp.dot(weights, value_ref[:, cut], preferred_element_type=F32)


def decays(rows):
    rows = rows.astype(F32)
    return rows[0:HEADS] + rows[HEADS : 2 * HEADS]


def split_decay(decay):
    high = decay.astype(BF16).astype(F32)
    low = (decay - high).astype(BF16).astype(F32)
    return jnp.concatenate([high, low, jnp.zeros((2, HDIM), F32)], axis=0).astype(BF16)


def pair_kernel(place_ref, own_ref, other_ref, out_ref):
    odd = place_ref[0] & 1 == 1
    own_a, other_a = decays(own_ref[STATE:, :]), decays(other_ref[STATE:, :])
    later_a = jnp.where(odd, own_a, other_a)
    scales = split_decay(own_a * other_a)
    for k in range(4):
        out_ref[k, STATE:, :] = scales
    for h in range(HEADS):
        cut = slice(h * HDIM, (h + 1) * HDIM)
        own, other = own_ref[cut, :].astype(F32), other_ref[cut, :].astype(F32)
        first, second = jnp.where(odd, other, own), jnp.where(odd, own, other)
        total = (later_a[h : h + 1] * first + second).astype(BF16)
        for k in range(4):
            out_ref[k, cut, :] = total


def row_kernel(parts_ref, out_ref):
    scale = [decays(parts_ref[k, STATE:, :]) for k in range(4)]
    scales = split_decay(scale[0] * scale[1] * scale[2] * scale[3])
    for k in range(4):
        out_ref[k, STATE:, :] = scales
    for h in range(HEADS):
        cut = slice(h * HDIM, (h + 1) * HDIM)
        total = parts_ref[0, cut, :].astype(F32)
        for k in range(1, 4):
            total = scale[k][h : h + 1] * total + parts_ref[k, cut, :].astype(F32)
        total = total.astype(BF16)
        for k in range(4):
            out_ref[k, cut, :] = total


def before(parts_ref, scale, reached, h):
    cut = slice(h * HDIM, (h + 1) * HDIM)
    state = jnp.zeros((HDIM, HDIM), F32)
    through = jnp.ones((1, HDIM), F32)
    for k in range(3):
        a = scale[k][h : h + 1]
        state = jnp.where(k < reached, a * state + parts_ref[k, cut, :].astype(F32), state)
        through = jnp.where(k < reached, a * through, through)
    return state, through


def attend_kernel(
    place_ref, starts_ref, decay_ref, query_ref, intra_ref, other_ref, row_ref, col_ref,
    send_ref, keep_ref, mixed_ref,
):
    odd = place_ref[0] & 1 == 1
    row, col = grid_iotas()
    lower_f = (row >= col).astype(F32)
    cumulative = running_sums(lower_f, decay_ref[...], True)
    segment = segment_of(starts_ref, lax.broadcasted_iota(jnp.int32, (SPAN, 1), 0))
    carry = jnp.exp(cumulative) * (segment == 0).astype(F32)
    row_scale = [decays(row_ref[k, STATE:, :]) for k in range(3)]
    col_scale = [decays(col_ref[k, STATE:, :]) for k in range(3)]
    other_a = decays(other_ref[STATE:, :])
    for h in range(HEADS):
        cut = slice(h * HDIM, (h + 1) * HDIM)
        inner, inner_a = before(row_ref, row_scale, (place_ref[0] >> 1) & 3, h)
        outer, _ = before(col_ref, col_scale, place_ref[0] >> 3, h)
        state = inner_a * outer + inner
        state = jnp.where(odd, other_a[h : h + 1] * state + other_ref[cut, :].astype(F32), state)
        inter = jnp.dot(query_ref[:, cut], state.astype(BF16), preferred_element_type=F32)
        mixed = intra_ref[:, cut] + inter * carry[:, h : h + 1]
        scale = lax.rsqrt(jnp.mean(mixed * mixed, axis=1, keepdims=True) + 1e-06)
        mixed_ref[:, cut] = (mixed * scale).astype(BF16)
    core, parity, group = place_ref[1] & 1, (place_ref[1] >> 1) & 1, place_ref[1] >> 2
    for u in range(2):
        for k in range(4):
            chip = ((group + k) & 3) * 2 + (parity if u else 1 - parity)
            at = (u * 4 + k) * 16
            keep_ref[at : at + 16, :] = mixed_ref[pl.ds(pl.multiple_of(chip * 32 + core * 16, 16), 16), :]
            send_ref[at : at + 16, :] = mixed_ref[pl.ds(pl.multiple_of(chip * 32 + (1 - core) * 16, 16), 16), :]


def project_kernel(own_ref, other_ref, own_w_ref, other_w_ref, send_ref, keep_ref):
    total = jnp.dot(own_ref[...], own_w_ref[...], preferred_element_type=F32)
    total = total + jnp.dot(other_ref[...], other_w_ref[...], preferred_element_type=F32)
    total = total.astype(BF16)
    send_ref[...] = total[:64]
    keep_ref[...] = total[64:]


def pair_sum_kernel(keep_ref, got_ref, own_ref, a_ref, b_ref, c_ref):
    for k, ref in enumerate((own_ref, a_ref, b_ref, c_ref)):
        cut = slice(k * 16, (k + 1) * 16)
        total = keep_ref[cut, :].astype(F32) + got_ref[cut, :].astype(F32)
        ref[...] = total.astype(ref.dtype)


def finish_kernel(own_ref, a_ref, b_ref, c_ref, residual_ref, gain_ref, hidden_ref, normed_ref):
    total = own_ref[...] + a_ref[...].astype(F32) + b_ref[...].astype(F32) + c_ref[...].astype(F32)
    hidden = residual_ref[...].astype(F32) + total
    scale = lax.rsqrt(jnp.mean(hidden * hidden, axis=1, keepdims=True) + 1e-05)
    hidden_ref[...] = hidden.astype(BF16)
    normed_ref[...] = (hidden * scale * gain_ref[...]).astype(BF16)


def call(body, shapes, specs, *args, scratch=()):
    return pl.pallas_call(
        body,
        out_shape=shapes,
        in_specs=specs,
        out_specs=jax.tree.map(lambda _: VMEM, shapes),
        scratch_shapes=list(scratch),
        compiler_params=pltpu.CompilerParams(vmem_limit_bytes=40 * 1024 * 1024),
    )(*args)


def of(shape, dtype):
    return jax.ShapeDtypeStruct(shape, dtype)


def shards(
    query_rows, key_rows, value_rows, log_decay, doc_starts, residual_in, out_weight, norm_gain
):
    place = jnp.stack([lax.axis_index("seq"), lax.axis_index("tp")]).astype(jnp.int32)

    local = call(
        state_kernel, of((PAYLOAD, HDIM), BF16), [SMEM, VMEM, VMEM, VMEM],
        doc_starts, log_decay, key_rows, value_rows,
    )
    other = lax.ppermute(local, "seq", FLIP_Z)
    intra = call(
        intra_kernel, of((SPAN, STATE), F32), [SMEM, VMEM, VMEM, VMEM, VMEM],
        doc_starts, log_decay, query_rows, key_rows, value_rows,
    )
    _, late_weight = lax.optimization_barrier((intra, out_weight))
    other_weight = lax.ppermute(late_weight, "tp", [(i, i ^ 1) for i in range(16)])
    other, intra = lax.optimization_barrier((other, intra))
    four = of((4, PAYLOAD, HDIM), BF16)
    pairs = call(pair_kernel, four, [SMEM, VMEM, VMEM], place, local, other)
    rows = lax.all_to_all(pairs, "seq", 0, 0, axis_index_groups=ROW_Y)
    totals = call(row_kernel, four, [VMEM], rows)
    cols = lax.all_to_all(totals, "seq", 0, 0, axis_index_groups=ROW_X)
    half = of((SPAN // 2, STATE), BF16)
    send, keep = call(
        attend_kernel, (half, half), [SMEM, SMEM] + [VMEM] * 6,
        place, doc_starts, log_decay, query_rows, intra, other, rows, cols,
        scratch=[pltpu.VMEM((SPAN, STATE), BF16)],
    )
    got = lax.ppermute(send, "tp", [(i, i ^ 1) for i in range(16)])

    block = 1024
    whole = pl.BlockSpec((SPAN // 2, STATE), lambda j: (0, 0))
    piece = pl.BlockSpec((STATE, block), lambda j: (0, j))
    out = pl.BlockSpec((64, block), lambda j: (0, j))
    quarter = of((64, D), BF16)
    send, keep = pl.pallas_call(
        project_kernel,
        grid=(D // block,),
        in_specs=[whole, whole, piece, piece],
        out_specs=(out, out),
        out_shape=(quarter, quarter),
        compiler_params=pltpu.CompilerParams(vmem_limit_bytes=40 * 1024 * 1024),
    )(keep, got, out_weight, other_weight)
    got = lax.ppermute(send, "tp", [(i, i ^ 2) for i in range(16)])
    chunk = of((16, D), BF16)
    own, *parts = call(
        pair_sum_kernel, (of((16, D), F32), chunk, chunk, chunk), [VMEM, VMEM], keep, got
    )
    parts = [
        lax.ppermute(part, "tp", [(i, (i + 4 * k) % 16) for i in range(16)])
        for k, part in enumerate(parts, 1)
    ]
    return call(
        finish_kernel, (chunk, chunk), [VMEM] * 6, own, *parts, residual_in, norm_gain[None, :]
    )


def solution(mesh):
    return jax.shard_map(
        shards,
        mesh=mesh,
        in_specs=(
            P("seq", "tp"),
            P("seq", "tp"),
            P("seq", "tp"),
            P("tp", "seq"),
            P("seq", None),
            P(("seq", "tp"), None),
            P("tp", None),
            P(),
        ),
        out_specs=(P(("seq", "tp"), None), P(("seq", "tp"), None)),
        check_vma=False,
    )
```

time: 383 us -> 117 us (0.31)
  the two profiles are of different devices: /device:TPU:4 before, /device:TPU:64 now
where the time goes in v1:
time: 117 us
  starting transfers between devices  37.5 us (32%)
  waiting for transfers between devices  35.1 us (30%)
  blocking collectives  25.9 us (22%)
  Pallas kernels  11 us (9%)
  local copies, waits for them, and re-layouts  6.14 us (5%)
    ppermute x3, starting transfers between devices, shards(): lax.ppermute(part, 'tp', [(i, (i + 4 * k) % 16) for i in range(16)])  17.9 us
    ppermute x3, waiting for transfers between devices, shards(): lax.ppermute(part, 'tp', [(i, (i + 4 * k) % 16) for i in range(16)])  16 us
    all_to_all x1, blocking collectives, shards(): rows = lax.all_to_all(pairs, 'seq', 0, 0, axis_index_groups=ROW_Y)  14.4 us
    ppermute x1, starting transfers between devices, shards(): other = lax.ppermute(local, 'seq', FLIP_Z)  13.9 us
    ppermute x1, waiting for transfers between devices, shards(): got = lax.ppermute(send, 'tp', [(i, i ^ 2) for i in range(16)])  13.9 us
    all_to_all x1, blocking collectives, shards(): cols = lax.all_to_all(totals, 'seq', 0, 0, axis_index_groups=ROW_X)  11.5 us
    pallas_call x7, Pallas kernels, call(): pl.pallas_call(body, out_shape=shapes, in_specs=specs, out_specs=jax.tree...  7.07 us
    unnamed x26, local copies, waits for them, and re-layouts  6.14 us
  transfers between devices with their start and end apart: 7, of which 5 were waited for; matrix products, arithmetic and copies ran while one was open for 0% of the time, Pallas kernels for 4%

profile of v1, /device:TPU:64, one launch (start us, length us, event | category | flops | bytes accessed | tf_op | source)
XLA Modules:
  0.0 116.6 jit_solution(5776224311073019823)
XLA Ops:
  0.6 0.0 copy-start
  0.6 0.0 copy-start.1
  0.7 1.1 copy-done.1
  1.7 0.0 copy-start.3
  1.7 0.9 copy-done.3
  2.6 0.0 copy-start.5
  2.7 0.9 copy-done.5
  3.6 0.0 copy-start.8
  3.6 0.7 copy-done.8
  4.3 0.0 copy-start.11
  4.3 0.7 copy-done.11
  4.9 1.4 %shard_map.96.intra_ref = f32[256,384]{1,0:T(8,128)S(1)} custom-call(s32[1,3]{1,0:T(1,128)S(1)} %copy-done.11, f32[3,256]{1,0:T(4,128)S(1)} %copy-done.8, bf16[256,384]{1,0:T(8,128)(2,1)S(1)} %copy-done.1, bf16[256,384]{1,0:T(8,128)(2,1)S(1)} %copy-done.3, bf16[256,384]{1,0:T(8,128)(2,1)S(1)} %copy-done.5), custom_call_target="tpu_custom_call" | custom-call | tf_op jit(solution)/shard_map/pallas_call | solution.py:196
  6.3 1.9 %collective-permute-start.2 = (bf16[384,4096]{1,0:T(8,128)(2,1)}, bf16[384,4096]{1,0:T(8,128)(2,1)}, u32[]{:S(2)}, u32[]{:S(2)}) collective-permute-start(bf16[384,4096]{1,0:T(8,128)(2,1)} %own_w_ref.1), channel_id=1, source_target_pairs={{0,1},{1,0},{2,3},{3,2},{4,5},{5,4},{6,7},{7,6},{8,9},{9,8},{10,11... | collective-permute-start | bytes 9437192 | tf_op jit(solution)/shard_map/ppermute | solution.py:225
  8.3 0.0 copy-start.4
  8.3 0.9 copy-done.4
  9.2 0.0 copy-start.6
  9.2 0.9 copy-done.6
  10.1 0.0 copy-start.9
  10.1 0.0 copy-start.12
  10.1 2.0 %shard_map.95.own_ref = bf16[392,128]{1,0:T(8,128)(2,1)} custom-call(s32[1,3]{1,0:T(1,128)S(1)} %copy-done.11, f32[3,256]{1,0:T(4,128)S(1)} %copy-done.8, bf16[256,384]{1,0:T(8,128)(2,1)S(1)} %copy-done.4, bf16[256,384]{1,0:T(8,128)(2,1)S(1)} %copy-done.6), custom_call_target="tpu_custom_call" | custom-call | tf_op jit(solution)/shard_map/pallas_call | solution.py:196
  12.1 13.9 %collective-permute-start = (bf16[392,128]{1,0:T(8,128)(2,1)}, bf16[392,128]{1,0:T(8,128)(2,1)}, u32[]{:S(2)}, u32[]{:S(2)}) collective-permute-start(bf16[392,128]{1,0:T(8,128)(2,1)} %shard_map.95.own_ref), channel_id=1, source_target_pairs={{0,16},{16,0},{32,48},{48,32},{64,80},{80,64},{96,112},{112,96},{1... | collective-permute-start | bytes 301064 | tf_op jit(solution)/shard_map/ppermute | solution.py:219
  26.0 0.0 copy-start.2
  26.1 0.1 pad_add_fusion.place_ref
  26.1 4.0 %collective-permute-done.other_ref = bf16[392,128]{1,0:T(8,128)(2,1)} collective-permute-done((bf16[392,128]{1,0:T(8,128)(2,1)}, bf16[392,128]{1,0:T(8,128)(2,1)}, u32[]{:S(2)}, u32[]{:S(2)}) %collective-permute-start) | collective-permute-done | bytes 100384 | tf_op jit(solution)/shard_map/ppermute | solution.py:219
  30.1 1.0 shard_map.97
  31.2 14.4 %all_to_all.10.parts_ref.row_ref = bf16[4,392,128]{2,1,0:T(8,128)(2,1)S(1)} all-to-all(bf16[4,392,128]{2,1,0:T(8,128)(2,1)S(1)} %shard_map.97), channel_id=1, replica_groups={{0,32,64,96},{16,48,80,112},{128,160,192,224},{144,176,208,240},{256,28..., dimensions={0} | all-to-all | bytes 802816 | tf_op jit(solution)/shard_map/all_to_all | solution.py:229
  45.5 0.1 shard_map.98
  45.6 11.5 %all_to_all.11.col_ref = bf16[4,392,128]{2,1,0:T(8,128)(2,1)S(1)} all-to-all(bf16[4,392,128]{2,1,0:T(8,128)(2,1)S(1)} %shard_map.98), channel_id=1, replica_groups={{0,128,256,384},{16,144,272,400},{32,160,288,416},{48,176,304,432},{64,..., dimensions={0} | all-to-all | bytes 802816 | tf_op jit(solution)/shard_map/all_to_all | solution.py:231
  57.1 0.0 copy-done.9
  57.1 0.0 copy-done.12
  57.1 0.0 copy-done.2
  57.1 1.6 %shard_map.99 = (bf16[128,384]{1,0:T(8,128)(2,1)S(1)}, bf16[128,384]{1,0:T(8,128)(2,1)S(1)}) custom-call(s32[2]{0:T(128)S(1)} %pad_add_fusion.place_ref, s32[1,3]{1,0:T(1,128)S(1)} %copy-done.12, f32[3,256]{1,0:T(4,128)S(1)} %copy-done.9, bf16[256,384]{1,0:T(8,128)(2,1)S(1)} %copy-done.2, f32[256,384]{1,0:T(8,128)S(1)} %shard_map.96.intra_ref, ...), custom_call_target="tpu_custom_call" | custom-call | tf_op jit(solution)/shard_map/pallas_call | solution.py:196
  58.8 1.9 %collective-permute-start.1 = (bf16[128,384]{1,0:T(8,128)(2,1)S(1)}, bf16[128,384]{1,0:T(8,128)(2,1)S(1)}, u32[]{:S(2)}, u32[]{:S(2)}) collective-permute-start(bf16[128,384]{1,0:T(8,128)(2,1)S(1)} %get-tuple-element.16), channel_id=1, source_target_pairs={{0,1},{1,0},{2,3},{3,2},{4,5},{5,4},{6,7},{7,6},{8,9},{9,8},{10,11... | collective-permute-start | bytes 294920 | tf_op jit(solution)/shard_map/ppermute | solution.py:238
  60.7 1.3 %collective-permute-done.1.other_ref = bf16[128,384]{1,0:T(8,128)(2,1)S(1)} collective-permute-done((bf16[128,384]{1,0:T(8,128)(2,1)S(1)}, bf16[128,384]{1,0:T(8,128)(2,1)S(1)}, u32[]{:S(2)}, u32[]{:S(2)}) %collective-permute-start.1) | collective-permute-done | bytes 98336 | tf_op jit(solution)/shard_map/ppermute | solution.py:238
  62.0 0.0 collective-permute-done.2.other_w_ref
  62.0 0.0 copy-done
  62.0 0.0 copy-start.7
  62.0 0.0 copy-start.10
  62.0 3.9 %shard_map.100 = (bf16[64,4096]{1,0:T(8,128)(2,1)S(1)}, bf16[64,4096]{1,0:T(8,128)(2,1)S(1)}) custom-call(bf16[128,384]{1,0:T(8,128)(2,1)S(1)} %get-tuple-element.15.own_ref, bf16[128,384]{1,0:T(8,128)(2,1)S(1)} %collective-permute-done.1.other_ref, bf16[384,4096]{1,0:T(8,128)(2,1)S(1)} %copy-done, bf16[384,4096]{1,0:T(8,128)(2,1)} %collective-permute-done.2.other_w_ref), custom_call_target="tpu_custom_call" | custom-call | tf_op jit(solution)/shard_map/pallas_call | solution.py:245
  65.9 1.9 %collective-permute-start.3 = (bf16[64,4096]{1,0:T(8,128)(2,1)S(1)}, bf16[64,4096]{1,0:T(8,128)(2,1)S(1)}, u32[]{:S(2)}, u32[]{:S(2)}) collective-permute-start(bf16[64,4096]{1,0:T(8,128)(2,1)S(1)} %get-tuple-element.19), channel_id=1, source_target_pairs={{0,2},{1,3},{2,0},{3,1},{4,6},{5,7},{6,4},{7,5},{8,10},{9,11},{10,... | collective-permute-start | bytes 1572872 | tf_op jit(solution)/shard_map/ppermute | solution.py:253
  67.8 13.9 %collective-permute-done.3.got_ref = bf16[64,4096]{1,0:T(8,128)(2,1)S(1)} collective-permute-done((bf16[64,4096]{1,0:T(8,128)(2,1)S(1)}, bf16[64,4096]{1,0:T(8,128)(2,1)S(1)}, u32[]{:S(2)}, u32[]{:S(2)}) %collective-permute-start.3) | collective-permute-done | bytes 524320 | tf_op jit(solution)/shard_map/ppermute | solution.py:253
  81.7 0.1 shard_map.101
  81.9 6.8 %collective-permute-start.4 = (bf16[16,4096]{1,0:T(8,128)(2,1)S(1)}, bf16[16,4096]{1,0:T(8,128)(2,1)S(1)}, u32[]{:S(2)}, u32[]{:S(2)}) collective-permute-start(bf16[16,4096]{1,0:T(8,128)(2,1)S(1)} %get-tuple-element.21), channel_id=1, source_target_pairs={{0,4},{1,5},{2,6},{3,7},{4,8},{5,9},{6,10},{7,11},{8,12},{9,13},{1... | collective-permute-start | bytes 393224 | tf_op jit(solution)/shard_map/ppermute | solution.py:259
  88.7 6.2 %collective-permute-start.5 = (bf16[16,4096]{1,0:T(8,128)(2,1)S(1)}, bf16[16,4096]{1,0:T(8,128)(2,1)S(1)}, u32[]{:S(2)}, u32[]{:S(2)}) collective-permute-start(bf16[16,4096]{1,0:T(8,128)(2,1)S(1)} %get-tuple-element.22), channel_id=1, source_target_pairs={{0,8},{1,9},{2,10},{3,11},{4,12},{5,13},{6,14},{7,15},{8,0},{9,1},... | collective-permute-start | bytes 393224 | tf_op jit(solution)/shard_map/ppermute | solution.py:259
  94.9 4.8 %collective-permute-start.6 = (bf16[16,4096]{1,0:T(8,128)(2,1)S(1)}, bf16[16,4096]{1,0:T(8,128)(2,1)S(1)}, u32[]{:S(2)}, u32[]{:S(2)}) collective-permute-start(bf16[16,4096]{1,0:T(8,128)(2,1)S(1)} %get-tuple-element.23), channel_id=1, source_target_pairs={{0,12},{1,13},{2,14},{3,15},{4,0},{5,1},{6,2},{7,3},{8,4},{9,5},{1... | collective-permute-start | bytes 393224 | tf_op jit(solution)/shard_map/ppermute | solution.py:259
  99.7 0.0 collective-permute-done.4.a_ref
  99.8 8.7 %collective-permute-done.5.b_ref = bf16[16,4096]{1,0:T(8,128)(2,1)S(1)} collective-permute-done((bf16[16,4096]{1,0:T(8,128)(2,1)S(1)}, bf16[16,4096]{1,0:T(8,128)(2,1)S(1)}, u32[]{:S(2)}, u32[]{:S(2)}) %collective-permute-start.5) | collective-permute-done | bytes 131104 | tf_op jit(solution)/shard_map/ppermute | solution.py:259
  108.5 7.2 %collective-permute-done.6.c_ref = bf16[16,4096]{1,0:T(8,128)(2,1)S(1)} collective-permute-done((bf16[16,4096]{1,0:T(8,128)(2,1)S(1)}, bf16[16,4096]{1,0:T(8,128)(2,1)S(1)}, u32[]{:S(2)}, u32[]{:S(2)}) %collective-permute-start.6) | collective-permute-done | bytes 131104 | tf_op jit(solution)/shard_map/ppermute | solution.py:259
  115.7 0.0 copy-done.7
  115.7 0.0 copy-done.10
  115.7 0.8 shard_map.102
Async XLA Ops:
  0.6 61.3 %copy-start = (bf16[384,4096]{1,0:T(8,128)(2,1)S(1)}, bf16[384,4096]{1,0:T(8,128)(2,1)}, u32[]{:S(2)}) copy-start(bf16[384,4096]{1,0:T(8,128)(2,1)} %own_w_ref.1) | copy-start | bytes 9437188
  0.6 1.1 copy-start.1
  1.7 0.9 copy-start.3
  2.6 0.9 copy-start.5
  3.6 0.7 copy-start.8
  4.3 0.7 copy-start.11
  6.3 55.6 %collective-permute-start.2 = (bf16[384,4096]{1,0:T(8,128)(2,1)}, bf16[384,4096]{1,0:T(8,128)(2,1)}, u32[]{:S(2)}, u32[]{:S(2)}) collective-permute-start(bf16[384,4096]{1,0:T(8,128)(2,1)} %own_w_ref.1), channel_id=1, source_target_pairs={{0,1},{1,0},{2,3},{3,2},{4,5},{5,4},{6,7},{7,6},{8,9},{9,8},{10,11... | collective-permute-start | bytes 9437192 | tf_op jit(solution)/shard_map/ppermute | solution.py:225
  8.3 0.9 copy-start.4
  9.2 0.9 copy-start.6
  10.1 47.0 %copy-start.9 = (f32[3,256]{1,0:T(4,128)S(1)}, f32[3,256]{1,0:T(4,128)}, u32[]{:S(2)}) copy-start(f32[3,256]{1,0:T(4,128)} %decay_ref.5) | copy-start | bytes 9220
  10.1 47.0 %copy-start.12 = (s32[1,3]{1,0:T(1,128)S(1)}, s32[1,3]{1,0:T(1,128)}, u32[]{:S(2)}) copy-start(s32[1,3]{1,0:T(1,128)} %starts_ref.5) | copy-start | bytes 40
  12.1 18.0 %collective-permute-start = (bf16[392,128]{1,0:T(8,128)(2,1)}, bf16[392,128]{1,0:T(8,128)(2,1)}, u32[]{:S(2)}, u32[]{:S(2)}) collective-permute-start(bf16[392,128]{1,0:T(8,128)(2,1)} %shard_map.95.own_ref), channel_id=1, source_target_pairs={{0,16},{16,0},{32,48},{48,32},{64,80},{80,64},{96,112},{112,96},{1... | collective-permute-start | bytes 301064 | tf_op jit(solution)/shard_map/ppermute | solution.py:219
  26.0 31.1 %copy-start.2 = (bf16[256,384]{1,0:T(8,128)(2,1)S(1)}, bf16[256,384]{1,0:T(8,128)(2,1)}, u32[]{:S(2)}) copy-start(bf16[256,384]{1,0:T(8,128)(2,1)} %query_ref.3) | copy-start | bytes 589828
  58.8 3.2 %collective-permute-start.1 = (bf16[128,384]{1,0:T(8,128)(2,1)S(1)}, bf16[128,384]{1,0:T(8,128)(2,1)S(1)}, u32[]{:S(2)}, u32[]{:S(2)}) collective-permute-start(bf16[128,384]{1,0:T(8,128)(2,1)S(1)} %get-tuple-element.16), channel_id=1, source_target_pairs={{0,1},{1,0},{2,3},{3,2},{4,5},{5,4},{6,7},{7,6},{8,9},{9,8},{10,11... | collective-permute-start | bytes 294920 | tf_op jit(solution)/shard_map/ppermute | solution.py:238
  62.0 53.8 %copy-start.7 = (bf16[16,4096]{1,0:T(8,128)(2,1)S(1)}, bf16[16,4096]{1,0:T(8,128)(2,1)}, u32[]{:S(2)}) copy-start(bf16[16,4096]{1,0:T(8,128)(2,1)} %residual_ref.1) | copy-start | bytes 393220
  62.0 53.8 %copy-start.10 = (f32[4096]{0:T(1024)S(1)}, f32[4096]{0:T(1024)}, u32[]{:S(2)}) copy-start(f32[4096]{0:T(1024)} %param.15) | copy-start | bytes 49156
  65.9 15.8 %collective-permute-start.3 = (bf16[64,4096]{1,0:T(8,128)(2,1)S(1)}, bf16[64,4096]{1,0:T(8,128)(2,1)S(1)}, u32[]{:S(2)}, u32[]{:S(2)}) collective-permute-start(bf16[64,4096]{1,0:T(8,128)(2,1)S(1)} %get-tuple-element.19), channel_id=1, source_target_pairs={{0,2},{1,3},{2,0},{3,1},{4,6},{5,7},{6,4},{7,5},{8,10},{9,11},{10,... | collective-permute-start | bytes 1572872 | tf_op jit(solution)/shard_map/ppermute | solution.py:253
  81.9 17.9 %collective-permute-start.4 = (bf16[16,4096]{1,0:T(8,128)(2,1)S(1)}, bf16[16,4096]{1,0:T(8,128)(2,1)S(1)}, u32[]{:S(2)}, u32[]{:S(2)}) collective-permute-start(bf16[16,4096]{1,0:T(8,128)(2,1)S(1)} %get-tuple-element.21), channel_id=1, source_target_pairs={{0,4},{1,5},{2,6},{3,7},{4,8},{5,9},{6,10},{7,11},{8,12},{9,13},{1... | collective-permute-start | bytes 393224 | tf_op jit(solution)/shard_map/ppermute | solution.py:259
  88.7 19.8 %collective-permute-start.5 = (bf16[16,4096]{1,0:T(8,128)(2,1)S(1)}, bf16[16,4096]{1,0:T(8,128)(2,1)S(1)}, u32[]{:S(2)}, u32[]{:S(2)}) collective-permute-start(bf16[16,4096]{1,0:T(8,128)(2,1)S(1)} %get-tuple-element.22), channel_id=1, source_target_pairs={{0,8},{1,9},{2,10},{3,11},{4,12},{5,13},{6,14},{7,15},{8,0},{9,1},... | collective-permute-start | bytes 393224 | tf_op jit(solution)/shard_map/ppermute | solution.py:259
  94.9 20.8 %collective-permute-start.6 = (bf16[16,4096]{1,0:T(8,128)(2,1)S(1)}, bf16[16,4096]{1,0:T(8,128)(2,1)S(1)}, u32[]{:S(2)}, u32[]{:S(2)}) collective-permute-start(bf16[16,4096]{1,0:T(8,128)(2,1)S(1)} %get-tuple-element.23), channel_id=1, source_target_pairs={{0,12},{1,13},{2,14},{3,15},{4,0},{5,1},{6,2},{7,3},{8,4},{9,5},{1... | collective-permute-start | bytes 393224 | tf_op jit(solution)/shard_map/ppermute | solution.py:259

commit v2 on v1

--- a/solution.py
+++ b/solution.py
@@ -20,6 +20,7 @@
 ROW_X = [[g + 8 * k for k in range(4)] for g in range(8)]
 
 VMEM = pl.BlockSpec(memory_space=pltpu.VMEM)
+HBM = pl.BlockSpec(memory_space=pltpu.HBM)
 SMEM = pl.BlockSpec(memory_space=pltpu.SMEM)
 
 
@@ -42,11 +43,24 @@
     return row, col
 
 
-def state_kernel(starts_ref, decay_ref, key_ref, value_ref, out_ref):
+def state_kernel(
+    starts_hbm, decay_hbm, key_hbm, value_hbm, out_ref,
+    starts_ref, decay_ref, key_ref, value_ref, sems,
+):
+    sources = (decay_hbm, starts_hbm, key_hbm, value_hbm)
+    targets = (decay_ref, starts_ref, key_ref, value_ref)
+    copies = [
+        pltpu.make_async_copy(source, target, sems.at[k])
+        for k, (source, target) in enumerate(zip(sources, targets))
+    ]
+    for copy in copies:
+        copy.start()
     row, col = grid_iotas()
     later = (col > row).astype(F32)
+    copies[0].wait()
     decay = decay_ref[...]
     tail = running_sums(later, decay, True)
+    copies[1].wait()
     segment = segment_of(starts_ref, lax.broadcasted_iota(jnp.int32, (SPAN, 1), 0))
     last = segment_of(starts_ref, jnp.full((1, 1), SPAN - 1, jnp.int32))
     tail_weight = jnp.exp(tail) * (segment == last).astype(F32)
@@ -55,6 +69,8 @@
     low = (through - high).astype(BF16).astype(F32)
     rows = jnp.concatenate([high, low, jnp.zeros((2, 1), F32)], axis=0)
     out_ref[STATE:, :] = jnp.broadcast_to(rows, (8, HDIM)).astype(BF16)
+    copies[2].wait()
+    copies[3].wait()
     for h in range(HEADS):
         cut = slice(h * HDIM, (h + 1) * HDIM)
         decayed = (key_ref[:, cut].astype(F32) * tail_weight[:, h : h + 1]).astype(BF16)
@@ -184,12 +200,22 @@
         ref[...] = total.astype(ref.dtype)
 
 
-def finish_kernel(own_ref, a_ref, b_ref, c_ref, residual_ref, gain_ref, hidden_ref, normed_ref):
-    total = own_ref[...] + a_ref[...].astype(F32) + b_ref[...].astype(F32) + c_ref[...].astype(F32)
-    hidden = residual_ref[...].astype(F32) + total
-    scale = lax.rsqrt(jnp.mean(hidden * hidden, axis=1, keepdims=True) + 1e-05)
-    hidden_ref[...] = hidden.astype(BF16)
-    normed_ref[...] = (hidden * scale * gain_ref[...]).astype(BF16)
+def finish_kernel(*refs):
+    *sums, residual_ref, gain_ref, hidden_ref, normed_ref = refs
+    width = D // 2
+    square = jnp.zeros((16, 1), F32)
+    sides = []
+    for side in range(2):
+        total = residual_ref[:, side * width : (side + 1) * width].astype(F32) + sums[side][...]
+        for part in sums[2 + 3 * side : 5 + 3 * side]:
+            total = total + part[...].astype(F32)
+        square = square + jnp.sum(total * total, axis=1, keepdims=True)
+        sides.append(total)
+    scale = lax.rsqrt(square / D + 1e-05)
+    for side, total in enumerate(sides):
+        cut = slice(side * width, (side + 1) * width)
+        hidden_ref[:, cut] = total.astype(BF16)
+        normed_ref[:, cut] = (total * scale * gain_ref[:, cut]).astype(BF16)
 
 
 def call(body, shapes, specs, *args, scratch=()):
@@ -199,8 +225,12 @@
         in_specs=specs,
         out_specs=jax.tree.map(lambda _: VMEM, shapes),
         scratch_shapes=list(scratch),
-        compiler_params=pltpu.CompilerParams(vmem_limit_bytes=40 * 1024 * 1024),
+        compiler_params=pltpu.CompilerParams(vmem_limit_bytes=16 * 1024 * 1024),
     )(*args)
+
+
+def whole(*shape):
+    return pl.BlockSpec(shape, lambda j: (0,) * len(shape))
 
 
 def of(shape, dtype):
@@ -213,15 +243,26 @@
     place = jnp.stack([lax.axis_index("seq"), lax.axis_index("tp")]).astype(jnp.int32)
 
     local = call(
-        state_kernel, of((PAYLOAD, HDIM), BF16), [SMEM, VMEM, VMEM, VMEM],
-        doc_starts, log_decay, key_rows, value_rows,
-    )
+        state_kernel, of((PAYLOAD, HDIM), BF16), [HBM] * 4,
+        *(
+            pltpu.with_memory_space_constraint(a, pltpu.HBM)
+            for a in (doc_starts, log_decay, key_rows, value_rows)
+        ),
+        scratch=[
+            pltpu.SMEM((1, 3), jnp.int32),
+            pltpu.VMEM((HEADS, SPAN), F32),
+            pltpu.VMEM((SPAN, STATE), BF16),
+            pltpu.VMEM((SPAN, STATE), BF16),
+            pltpu.SemaphoreType.DMA((4,)),
+        ],
+    )
+    late_query = lax.optimization_barrier((local, query_rows))[1]
     other = lax.ppermute(local, "seq", FLIP_Z)
     intra = call(
         intra_kernel, of((SPAN, STATE), F32), [SMEM, VMEM, VMEM, VMEM, VMEM],
-        doc_starts, log_decay, query_rows, key_rows, value_rows,
-    )
-    _, late_weight = lax.optimization_barrier((intra, out_weight))
+        doc_starts, log_decay, late_query, key_rows, value_rows,
+    )
+    late_weight = lax.optimization_barrier((local, out_weight))[1]
     other_weight = lax.ppermute(late_weight, "tp", [(i, i ^ 1) for i in range(16)])
     other, intra = lax.optimization_barrier((other, intra))
     four = of((4, PAYLOAD, HDIM), BF16)
@@ -237,30 +278,31 @@
     )
     got = lax.ppermute(send, "tp", [(i, i ^ 1) for i in range(16)])
 
-    block = 1024
-    whole = pl.BlockSpec((SPAN // 2, STATE), lambda j: (0, 0))
-    piece = pl.BlockSpec((STATE, block), lambda j: (0, j))
-    out = pl.BlockSpec((64, block), lambda j: (0, j))
-    quarter = of((64, D), BF16)
-    send, keep = pl.pallas_call(
-        project_kernel,
-        grid=(D // block,),
-        in_specs=[whole, whole, piece, piece],
-        out_specs=(out, out),
-        out_shape=(quarter, quarter),
-        compiler_params=pltpu.CompilerParams(vmem_limit_bytes=40 * 1024 * 1024),
-    )(keep, got, out_weight, other_weight)
-    got = lax.ppermute(send, "tp", [(i, i ^ 2) for i in range(16)])
-    chunk = of((16, D), BF16)
-    own, *parts = call(
-        pair_sum_kernel, (of((16, D), F32), chunk, chunk, chunk), [VMEM, VMEM], keep, got
-    )
-    parts = [
-        lax.ppermute(part, "tp", [(i, (i + 4 * k) % 16) for i in range(16)])
-        for k, part in enumerate(parts, 1)
-    ]
+    width = D // 2
+    quarter, chunk = of((64, width), BF16), of((16, width), BF16)
+    owned, others = [], []
+    for side in range(2):
+        piece = pl.BlockSpec((STATE, width), lambda j, side=side: (0, side))
+        sent, kept = pl.pallas_call(
+            project_kernel,
+            grid=(1,),
+            in_specs=[whole(SPAN // 2, STATE)] * 2 + [piece] * 2,
+            out_specs=(whole(64, width),) * 2,
+            out_shape=(quarter, quarter),
+            compiler_params=pltpu.CompilerParams(vmem_limit_bytes=16 * 1024 * 1024),
+        )(keep, got, out_weight, other_weight)
+        near = lax.ppermute(sent, "tp", [(i, i ^ 2) for i in range(16)])
+        own, *parts = call(
+            pair_sum_kernel, (of((16, width), F32), chunk, chunk, chunk), [VMEM, VMEM], kept, near
+        )
+        owned.append(own)
+        others += [
+            lax.ppermute(part, "tp", [(i, (i + 4 * k) % 16) for i in range(16)])
+            for k, part in enumerate(parts, 1)
+        ]
+    full = of((16, D), BF16)
     return call(
-        finish_kernel, (chunk, chunk), [VMEM] * 6, own, *parts, residual_in, norm_gain[None, :]
+        finish_kernel, (full, full), [VMEM] * 10, *owned, *others, residual_in, norm_gain[None, :]
     )
 
 

time: 117 us -> 111 us (0.949)
  the two profiles are of different devices: /device:TPU:64 before, /device:TPU:1 now
where the time goes in v2:
time: 111 us
  starting transfers between devices  62.5 us (56%)
  blocking collectives  21.8 us (20%)
  Pallas kernels  12.1 us (11%)
  waiting for transfers between devices  9.33 us (8%)
  local copies, waits for them, and re-layouts  4.15 us (4%)
    ppermute x6, starting transfers between devices, shards(): lax.ppermute(part, 'tp', [(i, (i + 4 * k) % 16) for i in range(16)])  32.6 us
    all_to_all x1, blocking collectives, shards(): rows = lax.all_to_all(pairs, 'seq', 0, 0, axis_index_groups=ROW_Y)  11.7 us
    all_to_all x1, blocking collectives, shards(): cols = lax.all_to_all(totals, 'seq', 0, 0, axis_index_groups=ROW_X)  10.1 us
    ppermute x1, starting transfers between devices, shards(): other = lax.ppermute(local, 'seq', FLIP_Z)  10.1 us
    ppermute x1, starting transfers between devices, shards(): lax.ppermute(late_weight, 'tp', [(i, i ^ 1) for i in range(16)])  8.79 us
    pallas_call x8, Pallas kernels, call(): pl.pallas_call(body, out_shape=shapes, in_specs=specs, out_specs=jax.tree...  7.64 us
    ppermute x2, starting transfers between devices, shards(): near = lax.ppermute(sent, 'tp', [(i, i ^ 2) for i in range(16)])  6.21 us
    ppermute x6, waiting for transfers between devices, shards(): lax.ppermute(part, 'tp', [(i, (i + 4 * k) % 16) for i in range(16)])  6.19 us
  transfers between devices with their start and end apart: 11, of which 3 were waited for; matrix products, arithmetic and copies ran while one was open for 0% of the time, Pallas kernels for 6%

profile of v2, /device:TPU:1, one launch (start us, length us, event | category | flops | bytes accessed | tf_op | source)
XLA Modules:
  0.0 110.8 jit_solution(1710008661164664357)
XLA Ops:
  0.6 0.0 copy-start
  0.6 2.5 %shard_map.95.own_ref = bf16[392,128]{1,0:T(8,128)(2,1)} custom-call(s32[1,3]{1,0:T(1,128)} %starts_ref.3, f32[3,256]{1,0:T(4,128)} %decay_ref.3, bf16[256,384]{1,0:T(8,128)(2,1)} %key_ref.1, bf16[256,384]{1,0:T(8,128)(2,1)} %value_ref.1), custom_call_target="tpu_custom_call" | custom-call | tf_op jit(solution)/shard_map/pallas_call | solution.py:222
  3.2 8.8 %collective-permute-start.2 = (bf16[384,4096]{1,0:T(8,128)(2,1)}, bf16[384,4096]{1,0:T(8,128)(2,1)}, u32[]{:S(2)}, u32[]{:S(2)}) collective-permute-start(bf16[384,4096]{1,0:T(8,128)(2,1)} %own_w_ref.3), channel_id=1, source_target_pairs={{0,1},{1,0},{2,3},{3,2},{4,5},{5,4},{6,7},{7,6},{8,9},{9,8},{10,11... | collective-permute-start | bytes 9437192 | tf_op jit(solution)/shard_map/ppermute | solution.py:266
  12.0 10.1 %collective-permute-start = (bf16[392,128]{1,0:T(8,128)(2,1)}, bf16[392,128]{1,0:T(8,128)(2,1)}, u32[]{:S(2)}, u32[]{:S(2)}) collective-permute-start(bf16[392,128]{1,0:T(8,128)(2,1)} %shard_map.95.own_ref), channel_id=1, source_target_pairs={{0,16},{16,0},{32,48},{48,32},{64,80},{80,64},{96,112},{112,96},{1... | collective-permute-start | bytes 301064 | tf_op jit(solution)/shard_map/ppermute | solution.py:260
  22.1 0.0 copy-start.1
  22.1 0.9 copy-done.1
  23.0 0.0 copy-start.3
  23.0 0.9 copy-done.3
  23.9 0.0 copy-start.4
  23.9 0.9 copy-done.4
  24.8 0.0 copy-start.6
  24.8 0.7 copy-done.6
  25.5 0.0 copy-start.9
  25.5 0.7 copy-done.9
  26.2 0.0 copy-start.7
  26.2 0.0 copy-start.10
  26.2 1.4 %shard_map.96.intra_ref = f32[256,384]{1,0:T(8,128)S(1)} custom-call(s32[1,3]{1,0:T(1,128)S(1)} %copy-done.9, f32[3,256]{1,0:T(4,128)S(1)} %copy-done.6, bf16[256,384]{1,0:T(8,128)(2,1)S(1)} %copy-done.1, bf16[256,384]{1,0:T(8,128)(2,1)S(1)} %copy-done.3, bf16[256,384]{1,0:T(8,128)(2,1)S(1)} %copy-done.4), custom_call_target="tpu_custom_call" | custom-call | tf_op jit(solution)/shard_map/pallas_call | solution.py:222
  27.6 0.0 copy-start.2
  27.6 0.1 pad_add_fusion.place_ref
  27.7 0.0 collective-permute-done.other_ref
  27.7 1.0 shard_map.97
  28.7 11.7 %all_to_all.10.parts_ref.row_ref = bf16[4,392,128]{2,1,0:T(8,128)(2,1)S(1)} all-to-all(bf16[4,392,128]{2,1,0:T(8,128)(2,1)S(1)} %shard_map.97), channel_id=1, replica_groups={{0,32,64,96},{16,48,80,112},{128,160,192,224},{144,176,208,240},{256,28..., dimensions={0} | all-to-all | bytes 802816 | tf_op jit(solution)/shard_map/all_to_all | solution.py:270
  40.4 0.1 shard_map.98
  40.5 10.1 %all_to_all.11.col_ref = bf16[4,392,128]{2,1,0:T(8,128)(2,1)S(1)} all-to-all(bf16[4,392,128]{2,1,0:T(8,128)(2,1)S(1)} %shard_map.98), channel_id=1, replica_groups={{0,128,256,384},{16,144,272,400},{32,160,288,416},{48,176,304,432},{64,..., dimensions={0} | all-to-all | bytes 802816 | tf_op jit(solution)/shard_map/all_to_all | solution.py:272
  50.6 0.0 copy-done.7
  50.6 0.0 copy-done.10
  50.6 0.0 copy-done.2
  50.6 1.6 %shard_map.99 = (bf16[128,384]{1,0:T(8,128)(2,1)S(1)}, bf16[128,384]{1,0:T(8,128)(2,1)S(1)}) custom-call(s32[2]{0:T(128)S(1)} %pad_add_fusion.place_ref, s32[1,3]{1,0:T(1,128)S(1)} %copy-done.10, f32[3,256]{1,0:T(4,128)S(1)} %copy-done.7, bf16[256,384]{1,0:T(8,128)(2,1)S(1)} %copy-done.2, f32[256,384]{1,0:T(8,128)S(1)} %shard_map.96.intra_ref, ...), custom_call_target="tpu_custom_call" | custom-call | tf_op jit(solution)/shard_map/pallas_call | solution.py:222
  52.2 4.8 %collective-permute-start.1 = (bf16[128,384]{1,0:T(8,128)(2,1)S(1)}, bf16[128,384]{1,0:T(8,128)(2,1)S(1)}, u32[]{:S(2)}, u32[]{:S(2)}) collective-permute-start(bf16[128,384]{1,0:T(8,128)(2,1)S(1)} %get-tuple-element.24), channel_id=1, source_target_pairs={{0,1},{1,0},{2,3},{3,2},{4,5},{5,4},{6,7},{7,6},{8,9},{9,8},{10,11... | collective-permute-start | bytes 294920 | tf_op jit(solution)/shard_map/ppermute | solution.py:279
  57.0 0.9 collective-permute-done.1.other_ref
  57.9 0.0 collective-permute-done.2.other_w_ref
  57.9 0.0 copy-done
  57.9 2.2 %shard_map.102 = (bf16[64,2048]{1,0:T(8,128)(2,1)S(1)}, bf16[64,2048]{1,0:T(8,128)(2,1)S(1)}) custom-call(bf16[128,384]{1,0:T(8,128)(2,1)S(1)} %get-tuple-element.23.own_ref, bf16[128,384]{1,0:T(8,128)(2,1)S(1)} %collective-permute-done.1.other_ref, bf16[384,4096]{1,0:T(8,128)(2,1)S(1)} %copy-done, bf16[384,4096]{1,0:T(8,128)(2,1)} %collective-permute-done.2.other_w_ref), custom_call_target="tpu_custom_call" | custom-call | tf_op jit(solution)/shard_map/pallas_call | solution.py:286
  60.2 0.0 copy-start.5
  60.2 0.0 copy-start.8
  60.2 4.3 %collective-permute-start.4 = (bf16[64,2048]{1,0:T(8,128)(2,1)S(1)}, bf16[64,2048]{1,0:T(8,128)(2,1)S(1)}, u32[]{:S(2)}, u32[]{:S(2)}) collective-permute-start(bf16[64,2048]{1,0:T(8,128)(2,1)S(1)} %get-tuple-element.30), channel_id=1, source_target_pairs={{0,2},{1,3},{2,0},{3,1},{4,6},{5,7},{6,4},{7,5},{8,10},{9,11},{10,... | collective-permute-start | bytes 786440 | tf_op jit(solution)/shard_map/ppermute | solution.py:294
  64.5 2.2 %shard_map.100 = (bf16[64,2048]{1,0:T(8,128)(2,1)S(1)}, bf16[64,2048]{1,0:T(8,128)(2,1)S(1)}) custom-call(bf16[128,384]{1,0:T(8,128)(2,1)S(1)} %get-tuple-element.23.own_ref, bf16[128,384]{1,0:T(8,128)(2,1)S(1)} %collective-permute-done.1.other_ref, bf16[384,4096]{1,0:T(8,128)(2,1)S(1)} %copy-done, bf16[384,4096]{1,0:T(8,128)(2,1)} %collective-permute-done.2.other_w_ref), custom_call_target="tpu_custom_call" | custom-call | tf_op jit(solution)/shard_map/pallas_call | solution.py:286
  66.7 1.9 %collective-permute-start.3 = (bf16[64,2048]{1,0:T(8,128)(2,1)S(1)}, bf16[64,2048]{1,0:T(8,128)(2,1)S(1)}, u32[]{:S(2)}, u32[]{:S(2)}) collective-permute-start(bf16[64,2048]{1,0:T(8,128)(2,1)S(1)} %get-tuple-element.27), channel_id=1, source_target_pairs={{0,2},{1,3},{2,0},{3,1},{4,6},{5,7},{6,4},{7,5},{8,10},{9,11},{10,... | collective-permute-start | bytes 786440 | tf_op jit(solution)/shard_map/ppermute | solution.py:294
  68.7 2.2 %collective-permute-done.4.got_ref = bf16[64,2048]{1,0:T(8,128)(2,1)S(1)} collective-permute-done((bf16[64,2048]{1,0:T(8,128)(2,1)S(1)}, bf16[64,2048]{1,0:T(8,128)(2,1)S(1)}, u32[]{:S(2)}, u32[]{:S(2)}) %collective-permute-start.4) | collective-permute-done | bytes 262176 | tf_op jit(solution)/shard_map/ppermute | solution.py:294
  70.9 0.1 shard_map.103
  70.9 10.5 %collective-permute-start.10 = (bf16[16,2048]{1,0:T(8,128)(2,1)S(1)}, bf16[16,2048]{1,0:T(8,128)(2,1)S(1)}, u32[]{:S(2)}, u32[]{:S(2)}) collective-permute-start(bf16[16,2048]{1,0:T(8,128)(2,1)S(1)} %get-tuple-element.37), channel_id=1, source_target_pairs={{0,12},{1,13},{2,14},{3,15},{4,0},{5,1},{6,2},{7,3},{8,4},{9,5},{1... | collective-permute-start | bytes 196616 | tf_op jit(solution)/shard_map/ppermute | solution.py:300
  81.5 1.9 %collective-permute-start.8 = (bf16[16,2048]{1,0:T(8,128)(2,1)S(1)}, bf16[16,2048]{1,0:T(8,128)(2,1)S(1)}, u32[]{:S(2)}, u32[]{:S(2)}) collective-permute-start(bf16[16,2048]{1,0:T(8,128)(2,1)S(1)} %get-tuple-element.35), channel_id=1, source_target_pairs={{0,4},{1,5},{2,6},{3,7},{4,8},{5,9},{6,10},{7,11},{8,12},{9,13},{1... | collective-permute-start | bytes 196616 | tf_op jit(solution)/shard_map/ppermute | solution.py:300
  83.4 2.2 %collective-permute-start.9 = (bf16[16,2048]{1,0:T(8,128)(2,1)S(1)}, bf16[16,2048]{1,0:T(8,128)(2,1)S(1)}, u32[]{:S(2)}, u32[]{:S(2)}) collective-permute-start(bf16[16,2048]{1,0:T(8,128)(2,1)S(1)} %get-tuple-element.36), channel_id=1, source_target_pairs={{0,8},{1,9},{2,10},{3,11},{4,12},{5,13},{6,14},{7,15},{8,0},{9,1},... | collective-permute-start | bytes 196616 | tf_op jit(solution)/shard_map/ppermute | solution.py:300
  85.6 0.0 collective-permute-done.3.got_ref
  85.6 0.1 shard_map.101
  85.7 9.1 %collective-permute-start.5 = (bf16[16,2048]{1,0:T(8,128)(2,1)S(1)}, bf16[16,2048]{1,0:T(8,128)(2,1)S(1)}, u32[]{:S(2)}, u32[]{:S(2)}) collective-permute-start(bf16[16,2048]{1,0:T(8,128)(2,1)S(1)} %get-tuple-element.32), channel_id=1, source_target_pairs={{0,4},{1,5},{2,6},{3,7},{4,8},{5,9},{6,10},{7,11},{8,12},{9,13},{1... | collective-permute-start | bytes 196616 | tf_op jit(solution)/shard_map/ppermute | solution.py:300
  94.8 1.9 %collective-permute-start.6 = (bf16[16,2048]{1,0:T(8,128)(2,1)S(1)}, bf16[16,2048]{1,0:T(8,128)(2,1)S(1)}, u32[]{:S(2)}, u32[]{:S(2)}) collective-permute-start(bf16[16,2048]{1,0:T(8,128)(2,1)S(1)} %get-tuple-element.33), channel_id=1, source_target_pairs={{0,8},{1,9},{2,10},{3,11},{4,12},{5,13},{6,14},{7,15},{8,0},{9,1},... | collective-permute-start | bytes 196616 | tf_op jit(solution)/shard_map/ppermute | solution.py:300
  96.7 0.0 collective-permute-done.10.refs_7_
  96.7 7.0 %collective-permute-start.7 = (bf16[16,2048]{1,0:T(8,128)(2,1)S(1)}, bf16[16,2048]{1,0:T(8,128)(2,1)S(1)}, u32[]{:S(2)}, u32[]{:S(2)}) collective-permute-start(bf16[16,2048]{1,0:T(8,128)(2,1)S(1)} %get-tuple-element.34), channel_id=1, source_target_pairs={{0,12},{1,13},{2,14},{3,15},{4,0},{5,1},{6,2},{7,3},{8,4},{9,5},{1... | collective-permute-start | bytes 196616 | tf_op jit(solution)/shard_map/ppermute | solution.py:300
  103.7 0.0 collective-permute-done.8.refs_5_
  103.7 0.0 collective-permute-done.9.refs_6_
  103.7 0.0 collective-permute-done.5.refs_2_
  103.7 6.2 %collective-permute-done.6.refs_3_ = bf16[16,2048]{1,0:T(8,128)(2,1)S(1)} collective-permute-done((bf16[16,2048]{1,0:T(8,128)(2,1)S(1)}, bf16[16,2048]{1,0:T(8,128)(2,1)S(1)}, u32[]{:S(2)}, u32[]{:S(2)}) %collective-permute-start.6) | collective-permute-done | bytes 65568 | tf_op jit(solution)/shard_map/ppermute | solution.py:300
  109.9 0.0 collective-permute-done.7.refs_4_
  109.9 0.0 copy-done.5
  109.9 0.0 copy-done.8
  109.9 0.8 shard_map.104
Async XLA Ops:
  0.6 57.3 %copy-start = (bf16[384,4096]{1,0:T(8,128)(2,1)S(1)}, bf16[384,4096]{1,0:T(8,128)(2,1)}, u32[]{:S(2)}) copy-start(bf16[384,4096]{1,0:T(8,128)(2,1)} %own_w_ref.3) | copy-start | bytes 9437188
  3.2 54.7 %collective-permute-start.2 = (bf16[384,4096]{1,0:T(8,128)(2,1)}, bf16[384,4096]{1,0:T(8,128)(2,1)}, u32[]{:S(2)}, u32[]{:S(2)}) collective-permute-start(bf16[384,4096]{1,0:T(8,128)(2,1)} %own_w_ref.3), channel_id=1, source_target_pairs={{0,1},{1,0},{2,3},{3,2},{4,5},{5,4},{6,7},{7,6},{8,9},{9,8},{10,11... | collective-permute-start | bytes 9437192 | tf_op jit(solution)/shard_map/ppermute | solution.py:266
  12.0 15.7 %collective-permute-start = (bf16[392,128]{1,0:T(8,128)(2,1)}, bf16[392,128]{1,0:T(8,128)(2,1)}, u32[]{:S(2)}, u32[]{:S(2)}) collective-permute-start(bf16[392,128]{1,0:T(8,128)(2,1)} %shard_map.95.own_ref), channel_id=1, source_target_pairs={{0,16},{16,0},{32,48},{48,32},{64,80},{80,64},{96,112},{112,96},{1... | collective-permute-start | bytes 301064 | tf_op jit(solution)/shard_map/ppermute | solution.py:260
  22.1 0.9 copy-start.1
  23.0 0.9 copy-start.3
  23.9 0.9 copy-start.4
  24.8 0.7 copy-start.6
  25.5 0.7 copy-start.9
  26.2 24.4 %copy-start.7 = (f32[3,256]{1,0:T(4,128)S(1)}, f32[3,256]{1,0:T(4,128)}, u32[]{:S(2)}) copy-start(f32[3,256]{1,0:T(4,128)} %decay_ref.3) | copy-start | bytes 9220
  26.2 24.4 %copy-start.10 = (s32[1,3]{1,0:T(1,128)S(1)}, s32[1,3]{1,0:T(1,128)}, u32[]{:S(2)}) copy-start(s32[1,3]{1,0:T(1,128)} %starts_ref.3) | copy-start | bytes 40
  27.6 23.0 %copy-start.2 = (bf16[256,384]{1,0:T(8,128)(2,1)S(1)}, bf16[256,384]{1,0:T(8,128)(2,1)}, u32[]{:S(2)}) copy-start(bf16[256,384]{1,0:T(8,128)(2,1)} %query_ref.2) | copy-start | bytes 589828
  52.2 5.7 %collective-permute-start.1 = (bf16[128,384]{1,0:T(8,128)(2,1)S(1)}, bf16[128,384]{1,0:T(8,128)(2,1)S(1)}, u32[]{:S(2)}, u32[]{:S(2)}) collective-permute-start(bf16[128,384]{1,0:T(8,128)(2,1)S(1)} %get-tuple-element.24), channel_id=1, source_target_pairs={{0,1},{1,0},{2,3},{3,2},{4,5},{5,4},{6,7},{7,6},{8,9},{9,8},{10,11... | collective-permute-start | bytes 294920 | tf_op jit(solution)/shard_map/ppermute | solution.py:279
  60.2 49.8 %copy-start.5 = (bf16[16,4096]{1,0:T(8,128)(2,1)S(1)}, bf16[16,4096]{1,0:T(8,128)(2,1)}, u32[]{:S(2)}) copy-start(bf16[16,4096]{1,0:T(8,128)(2,1)} %refs_8_.1) | copy-start | bytes 393220
  60.2 49.8 %copy-start.8 = (f32[4096]{0:T(1024)S(1)}, f32[4096]{0:T(1024)}, u32[]{:S(2)}) copy-start(f32[4096]{0:T(1024)} %param.15) | copy-start | bytes 49156
  60.2 10.7 %collective-permute-start.4 = (bf16[64,2048]{1,0:T(8,128)(2,1)S(1)}, bf16[64,2048]{1,0:T(8,128)(2,1)S(1)}, u32[]{:S(2)}, u32[]{:S(2)}) collective-permute-start(bf16[64,2048]{1,0:T(8,128)(2,1)S(1)} %get-tuple-element.30), channel_id=1, source_target_pairs={{0,2},{1,3},{2,0},{3,1},{4,6},{5,7},{6,4},{7,5},{8,10},{9,11},{10,... | collective-permute-start | bytes 786440 | tf_op jit(solution)/shard_map/ppermute | solution.py:294
  66.7 18.9 %collective-permute-start.3 = (bf16[64,2048]{1,0:T(8,128)(2,1)S(1)}, bf16[64,2048]{1,0:T(8,128)(2,1)S(1)}, u32[]{:S(2)}, u32[]{:S(2)}) collective-permute-start(bf16[64,2048]{1,0:T(8,128)(2,1)S(1)} %get-tuple-element.27), channel_id=1, source_target_pairs={{0,2},{1,3},{2,0},{3,1},{4,6},{5,7},{6,4},{7,5},{8,10},{9,11},{10,... | collective-permute-start | bytes 786440 | tf_op jit(solution)/shard_map/ppermute | solution.py:294
  70.9 25.8 %collective-permute-start.10 = (bf16[16,2048]{1,0:T(8,128)(2,1)S(1)}, bf16[16,2048]{1,0:T(8,128)(2,1)S(1)}, u32[]{:S(2)}, u32[]{:S(2)}) collective-permute-start(bf16[16,2048]{1,0:T(8,128)(2,1)S(1)} %get-tuple-element.37), channel_id=1, source_target_pairs={{0,12},{1,13},{2,14},{3,15},{4,0},{5,1},{6,2},{7,3},{8,4},{9,5},{1... | collective-permute-start | bytes 196616 | tf_op jit(solution)/shard_map/ppermute | solution.py:300
  81.5 22.2 %collective-permute-start.8 = (bf16[16,2048]{1,0:T(8,128)(2,1)S(1)}, bf16[16,2048]{1,0:T(8,128)(2,1)S(1)}, u32[]{:S(2)}, u32[]{:S(2)}) collective-permute-start(bf16[16,2048]{1,0:T(8,128)(2,1)S(1)} %get-tuple-element.35), channel_id=1, source_target_pairs={{0,4},{1,5},{2,6},{3,7},{4,8},{5,9},{6,10},{7,11},{8,12},{9,13},{1... | collective-permute-start | bytes 196616 | tf_op jit(solution)/shard_map/ppermute | solution.py:300
  83.4 20.3 %collective-permute-start.9 = (bf16[16,2048]{1,0:T(8,128)(2,1)S(1)}, bf16[16,2048]{1,0:T(8,128)(2,1)S(1)}, u32[]{:S(2)}, u32[]{:S(2)}) collective-permute-start(bf16[16,2048]{1,0:T(8,128)(2,1)S(1)} %get-tuple-element.36), channel_id=1, source_target_pairs={{0,8},{1,9},{2,10},{3,11},{4,12},{5,13},{6,14},{7,15},{8,0},{9,1},... | collective-permute-start | bytes 196616 | tf_op jit(solution)/shard_map/ppermute | solution.py:300
  85.7 18.0 %collective-permute-start.5 = (bf16[16,2048]{1,0:T(8,128)(2,1)S(1)}, bf16[16,2048]{1,0:T(8,128)(2,1)S(1)}, u32[]{:S(2)}, u32[]{:S(2)}) collective-permute-start(bf16[16,2048]{1,0:T(8,128)(2,1)S(1)} %get-tuple-element.32), channel_id=1, source_target_pairs={{0,4},{1,5},{2,6},{3,7},{4,8},{5,9},{6,10},{7,11},{8,12},{9,13},{1... | collective-permute-start | bytes 196616 | tf_op jit(solution)/shard_map/ppermute | solution.py:300
  94.8 15.2 %collective-permute-start.6 = (bf16[16,2048]{1,0:T(8,128)(2,1)S(1)}, bf16[16,2048]{1,0:T(8,128)(2,1)S(1)}, u32[]{:S(2)}, u32[]{:S(2)}) collective-permute-start(bf16[16,2048]{1,0:T(8,128)(2,1)S(1)} %get-tuple-element.33), channel_id=1, source_target_pairs={{0,8},{1,9},{2,10},{3,11},{4,12},{5,13},{6,14},{7,15},{8,0},{9,1},... | collective-permute-start | bytes 196616 | tf_op jit(solution)/shard_map/ppermute | solution.py:300
  96.7 13.2 %collective-permute-start.7 = (bf16[16,2048]{1,0:T(8,128)(2,1)S(1)}, bf16[16,2048]{1,0:T(8,128)(2,1)S(1)}, u32[]{:S(2)}, u32[]{:S(2)}) collective-permute-start(bf16[16,2048]{1,0:T(8,128)(2,1)S(1)} %get-tuple-element.34), channel_id=1, source_target_pairs={{0,12},{1,13},{2,14},{3,15},{4,0},{5,1},{6,2},{7,3},{8,4},{9,5},{1... | collective-permute-start | bytes 196616 | tf_op jit(solution)/shard_map/ppermute | solution.py:300

commit v3 on v2

--- a/solution.py
+++ b/solution.py
@@ -176,46 +176,35 @@
         mixed = intra_ref[:, cut] + inter * carry[:, h : h + 1]
         scale = lax.rsqrt(jnp.mean(mixed * mixed, axis=1, keepdims=True) + 1e-06)
         mixed_ref[:, cut] = (mixed * scale).astype(BF16)
-    core, parity, group = place_ref[1] & 1, (place_ref[1] >> 1) & 1, place_ref[1] >> 2
-    for u in range(2):
-        for k in range(4):
-            chip = ((group + k) & 3) * 2 + (parity if u else 1 - parity)
-            at = (u * 4 + k) * 16
-            keep_ref[at : at + 16, :] = mixed_ref[pl.ds(pl.multiple_of(chip * 32 + core * 16, 16), 16), :]
-            send_ref[at : at + 16, :] = mixed_ref[pl.ds(pl.multiple_of(chip * 32 + (1 - core) * 16, 16), 16), :]
-
-
-def project_kernel(own_ref, other_ref, own_w_ref, other_w_ref, send_ref, keep_ref):
+    core, chip = place_ref[1] & 1, place_ref[1] >> 1
+    for k in range(8):
+        start = (chip ^ (k & 3) ^ (0 if k & 4 else 4)) * 32
+        cut = slice(k * 16, (k + 1) * 16)
+        own, sibling = start + core * 16, start + (1 - core) * 16
+        keep_ref[cut, :] = mixed_ref[pl.ds(pl.multiple_of(own, 16), 16), :]
+        send_ref[cut, :] = mixed_ref[pl.ds(pl.multiple_of(sibling, 16), 16), :]
+
+
+def project_kernel(own_ref, other_ref, own_w_ref, other_w_ref, *out_refs):
     total = jnp.dot(own_ref[...], own_w_ref[...], preferred_element_type=F32)
     total = total + jnp.dot(other_ref[...], other_w_ref[...], preferred_element_type=F32)
-    total = total.astype(BF16)
-    send_ref[...] = total[:64]
-    keep_ref[...] = total[64:]
-
-
-def pair_sum_kernel(keep_ref, got_ref, own_ref, a_ref, b_ref, c_ref):
-    for k, ref in enumerate((own_ref, a_ref, b_ref, c_ref)):
-        cut = slice(k * 16, (k + 1) * 16)
-        total = keep_ref[cut, :].astype(F32) + got_ref[cut, :].astype(F32)
-        ref[...] = total.astype(ref.dtype)
-
-
-def finish_kernel(*refs):
-    *sums, residual_ref, gain_ref, hidden_ref, normed_ref = refs
-    width = D // 2
-    square = jnp.zeros((16, 1), F32)
-    sides = []
-    for side in range(2):
-        total = residual_ref[:, side * width : (side + 1) * width].astype(F32) + sums[side][...]
-        for part in sums[2 + 3 * side : 5 + 3 * side]:
-            total = total + part[...].astype(F32)
-        square = square + jnp.sum(total * total, axis=1, keepdims=True)
-        sides.append(total)
-    scale = lax.rsqrt(square / D + 1e-05)
-    for side, total in enumerate(sides):
-        cut = slice(side * width, (side + 1) * width)
-        hidden_ref[:, cut] = total.astype(BF16)
-        normed_ref[:, cut] = (total * scale * gain_ref[:, cut]).astype(BF16)
+    for k, ref in enumerate(out_refs):
+        ref[...] = total[k * 16 : (k + 1) * 16].astype(ref.dtype)
+
+
+def sum_kernel(own_ref, a_ref, b_ref, c_ref, out_ref):
+    total = own_ref[...] + a_ref[...].astype(F32) + b_ref[...].astype(F32) + c_ref[...].astype(F32)
+    out_ref[...] = total.astype(BF16)
+
+
+def finish_kernel(own_ref, *refs):
+    *part_refs, residual_ref, gain_ref, hidden_ref, normed_ref = refs
+    hidden = residual_ref[...].astype(F32) + own_ref[...]
+    for ref in part_refs:
+        hidden = hidden + ref[...].astype(F32)
+    scale = lax.rsqrt(jnp.mean(hidden * hidden, axis=1, keepdims=True) + 1e-05)
+    hidden_ref[...] = hidden.astype(BF16)
+    normed_ref[...] = (hidden * scale * gain_ref[...]).astype(BF16)
 
 
 def call(body, shapes, specs, *args, scratch=()):
@@ -278,31 +267,28 @@
     )
     got = lax.ppermute(send, "tp", [(i, i ^ 1) for i in range(16)])
 
-    width = D // 2
-    quarter, chunk = of((64, width), BF16), of((16, width), BF16)
-    owned, others = [], []
-    for side in range(2):
-        piece = pl.BlockSpec((STATE, width), lambda j, side=side: (0, side))
-        sent, kept = pl.pallas_call(
+    full, block = of((16, D), BF16), D // 2
+    piece = pl.BlockSpec((STATE, block), lambda j: (0, j))
+    halves = []
+    for part in range(2):
+        rows = pl.BlockSpec((SPAN // 4, STATE), lambda j, part=part: (part, 0))
+        own, *parts = pl.pallas_call(
             project_kernel,
-            grid=(1,),
-            in_specs=[whole(SPAN // 2, STATE)] * 2 + [piece] * 2,
-            out_specs=(whole(64, width),) * 2,
-            out_shape=(quarter, quarter),
+            grid=(D // block,),
+            in_specs=[rows, rows, piece, piece],
+            out_specs=(pl.BlockSpec((16, block), lambda j: (0, j)),) * 4,
+            out_shape=(of((16, D), F32), full, full, full),
             compiler_params=pltpu.CompilerParams(vmem_limit_bytes=16 * 1024 * 1024),
         )(keep, got, out_weight, other_weight)
-        near = lax.ppermute(sent, "tp", [(i, i ^ 2) for i in range(16)])
-        own, *parts = call(
-            pair_sum_kernel, (of((16, width), F32), chunk, chunk, chunk), [VMEM, VMEM], kept, near
-        )
-        owned.append(own)
-        others += [
-            lax.ppermute(part, "tp", [(i, (i + 4 * k) % 16) for i in range(16)])
-            for k, part in enumerate(parts, 1)
+        near = [
+            lax.ppermute(sent, "tp", [(i, i ^ (2 * k)) for i in range(16)])
+            for k, sent in enumerate(parts, 1)
         ]
-    full = of((16, D), BF16)
+        halves.append((own, *near))
+    away = call(sum_kernel, full, [VMEM] * 4, *halves[0])
+    far = lax.ppermute(away, "tp", [(i, i ^ 8) for i in range(16)])
     return call(
-        finish_kernel, (full, full), [VMEM] * 10, *owned, *others, residual_in, norm_gain[None, :]
+        finish_kernel, (full, full), [VMEM] * 7, *halves[1], far, residual_in, norm_gain[None, :]
     )
 
 

time: 111 us -> 104 us (0.937)
  the two profiles are of different devices: /device:TPU:1 before, /device:TPU:32 now
where the time goes in v3:
time: 104 us
  starting transfers between devices  45.8 us (44%)
  blocking collectives  23.2 us (22%)
  waiting for transfers between devices  16.2 us (16%)
  Pallas kernels  13.5 us (13%)
  local copies, waits for them, and re-layouts  4.15 us (4%)
    ppermute x6, starting transfers between devices, shards(): lax.ppermute(sent, 'tp', [(i, i ^ 2 * k) for i in range(16)])  18.6 us
    ppermute x1, starting transfers between devices, shards(): other = lax.ppermute(local, 'seq', FLIP_Z)  14.8 us
    all_to_all x1, blocking collectives, shards(): rows = lax.all_to_all(pairs, 'seq', 0, 0, axis_index_groups=ROW_Y)  11.7 us
    all_to_all x1, blocking collectives, shards(): cols = lax.all_to_all(totals, 'seq', 0, 0, axis_index_groups=ROW_X)  11.5 us
    ppermute x1, waiting for transfers between devices, shards(): far = lax.ppermute(away, 'tp', [(i, i ^ 8) for i in range(16)])  10 us
    ppermute x1, starting transfers between devices, shards(): far = lax.ppermute(away, 'tp', [(i, i ^ 8) for i in range(16)])  8.52 us
    pallas_call x7, Pallas kernels, call(): pl.pallas_call(body, out_shape=shapes, in_specs=specs, out_specs=jax.tree...  7.57 us
    pallas_call x2, Pallas kernels, shards(): pl.pallas_call(project_kernel, grid=(D // block,), in_specs=[rows, rows,...  5.89 us
  transfers between devices with their start and end apart: 10, of which 4 were waited for; matrix products, arithmetic and copies ran while one was open for 0% of the time, Pallas kernels for 7%

profile of v3, /device:TPU:32, one launch (start us, length us, event | category | flops | bytes accessed | tf_op | source)
XLA Modules:
  0.0 103.7 jit_solution(11134711973618575641)
XLA Ops:
  0.6 0.0 copy-start
  0.6 2.5 %shard_map.95.own_ref = bf16[392,128]{1,0:T(8,128)(2,1)} custom-call(s32[1,3]{1,0:T(1,128)} %starts_ref.3, f32[3,256]{1,0:T(4,128)} %decay_ref.3, bf16[256,384]{1,0:T(8,128)(2,1)} %key_ref.1, bf16[256,384]{1,0:T(8,128)(2,1)} %value_ref.1), custom_call_target="tpu_custom_call" | custom-call | tf_op jit(solution)/shard_map/pallas_call | solution.py:211
  3.2 1.9 %collective-permute-start.2 = (bf16[384,4096]{1,0:T(8,128)(2,1)}, bf16[384,4096]{1,0:T(8,128)(2,1)}, u32[]{:S(2)}, u32[]{:S(2)}) collective-permute-start(bf16[384,4096]{1,0:T(8,128)(2,1)} %own_w_ref.3), channel_id=1, source_target_pairs={{0,1},{1,0},{2,3},{3,2},{4,5},{5,4},{6,7},{7,6},{8,9},{9,8},{10,11... | collective-permute-start | bytes 9437192 | tf_op jit(solution)/shard_map/ppermute | solution.py:255
  5.1 14.8 %collective-permute-start = (bf16[392,128]{1,0:T(8,128)(2,1)}, bf16[392,128]{1,0:T(8,128)(2,1)}, u32[]{:S(2)}, u32[]{:S(2)}) collective-permute-start(bf16[392,128]{1,0:T(8,128)(2,1)} %shard_map.95.own_ref), channel_id=1, source_target_pairs={{0,16},{16,0},{32,48},{48,32},{64,80},{80,64},{96,112},{112,96},{1... | collective-permute-start | bytes 301064 | tf_op jit(solution)/shard_map/ppermute | solution.py:249
  19.9 0.0 copy-start.1
  20.0 0.9 copy-done.1
  20.9 0.0 copy-start.3
  20.9 0.9 copy-done.3
  21.8 0.0 copy-start.4
  21.8 0.9 copy-done.4
  22.7 0.0 copy-start.6
  22.7 0.7 copy-done.6
  23.4 0.0 copy-start.9
  23.4 0.7 copy-done.9
  24.1 0.0 copy-start.7
  24.1 0.0 copy-start.10
  24.1 1.4 %shard_map.96.intra_ref = f32[256,384]{1,0:T(8,128)S(1)} custom-call(s32[1,3]{1,0:T(1,128)S(1)} %copy-done.9, f32[3,256]{1,0:T(4,128)S(1)} %copy-done.6, bf16[256,384]{1,0:T(8,128)(2,1)S(1)} %copy-done.1, bf16[256,384]{1,0:T(8,128)(2,1)S(1)} %copy-done.3, bf16[256,384]{1,0:T(8,128)(2,1)S(1)} %copy-done.4), custom_call_target="tpu_custom_call" | custom-call | tf_op jit(solution)/shard_map/pallas_call | solution.py:211
  25.5 0.0 copy-start.2
  25.5 0.1 pad_add_fusion.place_ref
  25.6 2.7 %collective-permute-done.other_ref = bf16[392,128]{1,0:T(8,128)(2,1)} collective-permute-done((bf16[392,128]{1,0:T(8,128)(2,1)}, bf16[392,128]{1,0:T(8,128)(2,1)}, u32[]{:S(2)}, u32[]{:S(2)}) %collective-permute-start) | collective-permute-done | bytes 100384 | tf_op jit(solution)/shard_map/ppermute | solution.py:249
  28.3 1.0 shard_map.97
  29.3 11.7 %all_to_all.10.parts_ref.row_ref = bf16[4,392,128]{2,1,0:T(8,128)(2,1)S(1)} all-to-all(bf16[4,392,128]{2,1,0:T(8,128)(2,1)S(1)} %shard_map.97), channel_id=1, replica_groups={{0,32,64,96},{16,48,80,112},{128,160,192,224},{144,176,208,240},{256,28..., dimensions={0} | all-to-all | bytes 802816 | tf_op jit(solution)/shard_map/all_to_all | solution.py:259
  41.0 0.1 shard_map.98
  41.0 11.5 %all_to_all.11.col_ref = bf16[4,392,128]{2,1,0:T(8,128)(2,1)S(1)} all-to-all(bf16[4,392,128]{2,1,0:T(8,128)(2,1)S(1)} %shard_map.98), channel_id=1, replica_groups={{0,128,256,384},{16,144,272,400},{32,160,288,416},{48,176,304,432},{64,..., dimensions={0} | all-to-all | bytes 802816 | tf_op jit(solution)/shard_map/all_to_all | solution.py:261
  52.6 0.0 copy-done.7
  52.6 0.0 copy-done.10
  52.6 0.0 copy-done.2
  52.6 1.6 %shard_map.99 = (bf16[128,384]{1,0:T(8,128)(2,1)S(1)}, bf16[128,384]{1,0:T(8,128)(2,1)S(1)}) custom-call(s32[2]{0:T(128)S(1)} %pad_add_fusion.place_ref, s32[1,3]{1,0:T(1,128)S(1)} %copy-done.10, f32[3,256]{1,0:T(4,128)S(1)} %copy-done.7, bf16[256,384]{1,0:T(8,128)(2,1)S(1)} %copy-done.2, f32[256,384]{1,0:T(8,128)S(1)} %shard_map.96.intra_ref, ...), custom_call_target="tpu_custom_call" | custom-call | tf_op jit(solution)/shard_map/pallas_call | solution.py:211
  54.2 1.9 %collective-permute-start.1 = (bf16[128,384]{1,0:T(8,128)(2,1)S(1)}, bf16[128,384]{1,0:T(8,128)(2,1)S(1)}, u32[]{:S(2)}, u32[]{:S(2)}) collective-permute-start(bf16[128,384]{1,0:T(8,128)(2,1)S(1)} %get-tuple-element.20), channel_id=1, source_target_pairs={{0,1},{1,0},{2,3},{3,2},{4,5},{5,4},{6,7},{7,6},{8,9},{9,8},{10,11... | collective-permute-start | bytes 294920 | tf_op jit(solution)/shard_map/ppermute | solution.py:268
  56.1 1.3 %collective-permute-done.1.other_ref = bf16[128,384]{1,0:T(8,128)(2,1)S(1)} collective-permute-done((bf16[128,384]{1,0:T(8,128)(2,1)S(1)}, bf16[128,384]{1,0:T(8,128)(2,1)S(1)}, u32[]{:S(2)}, u32[]{:S(2)}) %collective-permute-start.1) | collective-permute-done | bytes 98336 | tf_op jit(solution)/shard_map/ppermute | solution.py:268
  57.4 0.0 collective-permute-done.2.other_w_ref
  57.4 0.0 copy-done
  57.4 2.9 %shard_map.101 = (f32[16,4096]{1,0:T(8,128)S(1)}, bf16[16,4096]{1,0:T(8,128)(2,1)S(1)}, bf16[16,4096]{1,0:T(8,128)(2,1)S(1)}, bf16[16,4096]{1,0:T(8,128)(2,1)S(1)}) custom-call(bf16[128,384]{1,0:T(8,128)(2,1)S(1)} %get-tuple-element.19.own_ref, bf16[128,384]{1,0:T(8,128)(2,1)S(1)} %collective-permute-done.1.other_ref, bf16[384,4096]{1,0:T(8,128)(2,1)S(1)} %copy-done, ...), custom_call_target="tpu_custom_call" | custom-call | tf_op jit(solution)/shard_map/pallas_call | solution.py:275
  60.4 1.9 %collective-permute-start.6 = (bf16[16,4096]{1,0:T(8,128)(2,1)S(1)}, bf16[16,4096]{1,0:T(8,128)(2,1)S(1)}, u32[]{:S(2)}, u32[]{:S(2)}) collective-permute-start(bf16[16,4096]{1,0:T(8,128)(2,1)S(1)} %get-tuple-element.27), channel_id=1, source_target_pairs={{0,2},{1,3},{2,0},{3,1},{4,6},{5,7},{6,4},{7,5},{8,10},{9,11},{10,... | collective-permute-start | bytes 393224 | tf_op jit(solution)/shard_map/ppermute | solution.py:284
  62.3 2.8 %collective-permute-start.7 = (bf16[16,4096]{1,0:T(8,128)(2,1)S(1)}, bf16[16,4096]{1,0:T(8,128)(2,1)S(1)}, u32[]{:S(2)}, u32[]{:S(2)}) collective-permute-start(bf16[16,4096]{1,0:T(8,128)(2,1)S(1)} %get-tuple-element.28), channel_id=1, source_target_pairs={{0,4},{1,5},{2,6},{3,7},{4,0},{5,1},{6,2},{7,3},{8,12},{9,13},{10,... | collective-permute-start | bytes 393224 | tf_op jit(solution)/shard_map/ppermute | solution.py:284
  65.1 0.0 copy-start.5
  65.2 0.0 copy-start.8
  65.2 4.6 %collective-permute-start.8 = (bf16[16,4096]{1,0:T(8,128)(2,1)S(1)}, bf16[16,4096]{1,0:T(8,128)(2,1)S(1)}, u32[]{:S(2)}, u32[]{:S(2)}) collective-permute-start(bf16[16,4096]{1,0:T(8,128)(2,1)S(1)} %get-tuple-element.29), channel_id=1, source_target_pairs={{0,6},{1,7},{2,4},{3,5},{4,2},{5,3},{6,0},{7,1},{8,14},{9,15},{10,... | collective-permute-start | bytes 393224 | tf_op jit(solution)/shard_map/ppermute | solution.py:284
  69.8 3.0 %shard_map.100 = (f32[16,4096]{1,0:T(8,128)S(1)}, bf16[16,4096]{1,0:T(8,128)(2,1)S(1)}, bf16[16,4096]{1,0:T(8,128)(2,1)S(1)}, bf16[16,4096]{1,0:T(8,128)(2,1)S(1)}) custom-call(bf16[128,384]{1,0:T(8,128)(2,1)S(1)} %get-tuple-element.19.own_ref, bf16[128,384]{1,0:T(8,128)(2,1)S(1)} %collective-permute-done.1.other_ref, bf16[384,4096]{1,0:T(8,128)(2,1)S(1)} %copy-done, ...), custom_call_target="tpu_custom_call" | custom-call | tf_op jit(solution)/shard_map/pallas_call | solution.py:275
  72.7 2.8 %collective-permute-start.3 = (bf16[16,4096]{1,0:T(8,128)(2,1)S(1)}, bf16[16,4096]{1,0:T(8,128)(2,1)S(1)}, u32[]{:S(2)}, u32[]{:S(2)}) collective-permute-start(bf16[16,4096]{1,0:T(8,128)(2,1)S(1)} %get-tuple-element.23), channel_id=1, source_target_pairs={{0,2},{1,3},{2,0},{3,1},{4,6},{5,7},{6,4},{7,5},{8,10},{9,11},{10,... | collective-permute-start | bytes 393224 | tf_op jit(solution)/shard_map/ppermute | solution.py:284
  75.5 2.5 %collective-permute-start.4 = (bf16[16,4096]{1,0:T(8,128)(2,1)S(1)}, bf16[16,4096]{1,0:T(8,128)(2,1)S(1)}, u32[]{:S(2)}, u32[]{:S(2)}) collective-permute-start(bf16[16,4096]{1,0:T(8,128)(2,1)S(1)} %get-tuple-element.24), channel_id=1, source_target_pairs={{0,4},{1,5},{2,6},{3,7},{4,0},{5,1},{6,2},{7,3},{8,12},{9,13},{10,... | collective-permute-start | bytes 393224 | tf_op jit(solution)/shard_map/ppermute | solution.py:284
  78.0 0.0 collective-permute-done.6.a_ref
  78.0 3.9 %collective-permute-start.5 = (bf16[16,4096]{1,0:T(8,128)(2,1)S(1)}, bf16[16,4096]{1,0:T(8,128)(2,1)S(1)}, u32[]{:S(2)}, u32[]{:S(2)}) collective-permute-start(bf16[16,4096]{1,0:T(8,128)(2,1)S(1)} %get-tuple-element.25), channel_id=1, source_target_pairs={{0,6},{1,7},{2,4},{3,5},{4,2},{5,3},{6,0},{7,1},{8,14},{9,15},{10,... | collective-permute-start | bytes 393224 | tf_op jit(solution)/shard_map/ppermute | solution.py:284
  82.0 0.0 collective-permute-done.7.b_ref
  82.0 0.0 collective-permute-done.8.c_ref
  82.0 0.1 shard_map.102
  82.0 8.5 %collective-permute-start.9 = (bf16[16,4096]{1,0:T(8,128)(2,1)S(1)}, bf16[16,4096]{1,0:T(8,128)(2,1)S(1)}, u32[]{:S(2)}, u32[]{:S(2)}) collective-permute-start(bf16[16,4096]{1,0:T(8,128)(2,1)S(1)} %shard_map.102), channel_id=1, source_target_pairs={{0,8},{1,9},{2,10},{3,11},{4,12},{5,13},{6,14},{7,15},{8,0},{9,1},... | collective-permute-start | bytes 393224 | tf_op jit(solution)/shard_map/ppermute | solution.py:289
  90.6 0.0 collective-permute-done.3.refs_0_
  90.6 0.0 collective-permute-done.4.refs_1_
  90.6 2.2 %collective-permute-done.5.refs_2_ = bf16[16,4096]{1,0:T(8,128)(2,1)S(1)} collective-permute-done((bf16[16,4096]{1,0:T(8,128)(2,1)S(1)}, bf16[16,4096]{1,0:T(8,128)(2,1)S(1)}, u32[]{:S(2)}, u32[]{:S(2)}) %collective-permute-start.5) | collective-permute-done | bytes 131104 | tf_op jit(solution)/shard_map/ppermute | solution.py:284
  92.8 10.0 %collective-permute-done.9.refs_3_ = bf16[16,4096]{1,0:T(8,128)(2,1)S(1)} collective-permute-done((bf16[16,4096]{1,0:T(8,128)(2,1)S(1)}, bf16[16,4096]{1,0:T(8,128)(2,1)S(1)}, u32[]{:S(2)}, u32[]{:S(2)}) %collective-permute-start.9) | collective-permute-done | bytes 131104 | tf_op jit(solution)/shard_map/ppermute | solution.py:289
  102.8 0.0 copy-done.5
  102.8 0.0 copy-done.8
  102.8 0.9 shard_map.103
Async XLA Ops:
  0.6 56.8 %copy-start = (bf16[384,4096]{1,0:T(8,128)(2,1)S(1)}, bf16[384,4096]{1,0:T(8,128)(2,1)}, u32[]{:S(2)}) copy-start(bf16[384,4096]{1,0:T(8,128)(2,1)} %own_w_ref.3) | copy-start | bytes 9437188
  3.2 54.2 %collective-permute-start.2 = (bf16[384,4096]{1,0:T(8,128)(2,1)}, bf16[384,4096]{1,0:T(8,128)(2,1)}, u32[]{:S(2)}, u32[]{:S(2)}) collective-permute-start(bf16[384,4096]{1,0:T(8,128)(2,1)} %own_w_ref.3), channel_id=1, source_target_pairs={{0,1},{1,0},{2,3},{3,2},{4,5},{5,4},{6,7},{7,6},{8,9},{9,8},{10,11... | collective-permute-start | bytes 9437192 | tf_op jit(solution)/shard_map/ppermute | solution.py:255
  5.1 23.2 %collective-permute-start = (bf16[392,128]{1,0:T(8,128)(2,1)}, bf16[392,128]{1,0:T(8,128)(2,1)}, u32[]{:S(2)}, u32[]{:S(2)}) collective-permute-start(bf16[392,128]{1,0:T(8,128)(2,1)} %shard_map.95.own_ref), channel_id=1, source_target_pairs={{0,16},{16,0},{32,48},{48,32},{64,80},{80,64},{96,112},{112,96},{1... | collective-permute-start | bytes 301064 | tf_op jit(solution)/shard_map/ppermute | solution.py:249
  19.9 0.9 copy-start.1
  20.9 0.9 copy-start.3
  21.8 0.9 copy-start.4
  22.7 0.7 copy-start.6
  23.4 0.7 copy-start.9
  24.1 28.5 %copy-start.7 = (f32[3,256]{1,0:T(4,128)S(1)}, f32[3,256]{1,0:T(4,128)}, u32[]{:S(2)}) copy-start(f32[3,256]{1,0:T(4,128)} %decay_ref.3) | copy-start | bytes 9220
  24.1 28.5 %copy-start.10 = (s32[1,3]{1,0:T(1,128)S(1)}, s32[1,3]{1,0:T(1,128)}, u32[]{:S(2)}) copy-start(s32[1,3]{1,0:T(1,128)} %starts_ref.3) | copy-start | bytes 40
  25.5 27.1 %copy-start.2 = (bf16[256,384]{1,0:T(8,128)(2,1)S(1)}, bf16[256,384]{1,0:T(8,128)(2,1)}, u32[]{:S(2)}) copy-start(bf16[256,384]{1,0:T(8,128)(2,1)} %query_ref.2) | copy-start | bytes 589828
  54.2 3.2 %collective-permute-start.1 = (bf16[128,384]{1,0:T(8,128)(2,1)S(1)}, bf16[128,384]{1,0:T(8,128)(2,1)S(1)}, u32[]{:S(2)}, u32[]{:S(2)}) collective-permute-start(bf16[128,384]{1,0:T(8,128)(2,1)S(1)} %get-tuple-element.20), channel_id=1, source_target_pairs={{0,1},{1,0},{2,3},{3,2},{4,5},{5,4},{6,7},{7,6},{8,9},{9,8},{10,11... | collective-permute-start | bytes 294920 | tf_op jit(solution)/shard_map/ppermute | solution.py:268
  60.4 17.7 %collective-permute-start.6 = (bf16[16,4096]{1,0:T(8,128)(2,1)S(1)}, bf16[16,4096]{1,0:T(8,128)(2,1)S(1)}, u32[]{:S(2)}, u32[]{:S(2)}) collective-permute-start(bf16[16,4096]{1,0:T(8,128)(2,1)S(1)} %get-tuple-element.27), channel_id=1, source_target_pairs={{0,2},{1,3},{2,0},{3,1},{4,6},{5,7},{6,4},{7,5},{8,10},{9,11},{10,... | collective-permute-start | bytes 393224 | tf_op jit(solution)/shard_map/ppermute | solution.py:284
  62.3 19.7 %collective-permute-start.7 = (bf16[16,4096]{1,0:T(8,128)(2,1)S(1)}, bf16[16,4096]{1,0:T(8,128)(2,1)S(1)}, u32[]{:S(2)}, u32[]{:S(2)}) collective-permute-start(bf16[16,4096]{1,0:T(8,128)(2,1)S(1)} %get-tuple-element.28), channel_id=1, source_target_pairs={{0,4},{1,5},{2,6},{3,7},{4,0},{5,1},{6,2},{7,3},{8,12},{9,13},{10,... | collective-permute-start | bytes 393224 | tf_op jit(solution)/shard_map/ppermute | solution.py:284
  65.1 37.7 %copy-start.5 = (bf16[16,4096]{1,0:T(8,128)(2,1)S(1)}, bf16[16,4096]{1,0:T(8,128)(2,1)}, u32[]{:S(2)}) copy-start(bf16[16,4096]{1,0:T(8,128)(2,1)} %refs_4_.1) | copy-start | bytes 393220
  65.2 37.7 %copy-start.8 = (f32[4096]{0:T(1024)S(1)}, f32[4096]{0:T(1024)}, u32[]{:S(2)}) copy-start(f32[4096]{0:T(1024)} %param.15) | copy-start | bytes 49156
  65.2 16.8 %collective-permute-start.8 = (bf16[16,4096]{1,0:T(8,128)(2,1)S(1)}, bf16[16,4096]{1,0:T(8,128)(2,1)S(1)}, u32[]{:S(2)}, u32[]{:S(2)}) collective-permute-start(bf16[16,4096]{1,0:T(8,128)(2,1)S(1)} %get-tuple-element.29), channel_id=1, source_target_pairs={{0,6},{1,7},{2,4},{3,5},{4,2},{5,3},{6,0},{7,1},{8,14},{9,15},{10,... | collective-permute-start | bytes 393224 | tf_op jit(solution)/shard_map/ppermute | solution.py:284
  72.7 17.9 %collective-permute-start.3 = (bf16[16,4096]{1,0:T(8,128)(2,1)S(1)}, bf16[16,4096]{1,0:T(8,128)(2,1)S(1)}, u32[]{:S(2)}, u32[]{:S(2)}) collective-permute-start(bf16[16,4096]{1,0:T(8,128)(2,1)S(1)} %get-tuple-element.23), channel_id=1, source_target_pairs={{0,2},{1,3},{2,0},{3,1},{4,6},{5,7},{6,4},{7,5},{8,10},{9,11},{10,... | collective-permute-start | bytes 393224 | tf_op jit(solution)/shard_map/ppermute | solution.py:284
  75.5 15.1 %collective-permute-start.4 = (bf16[16,4096]{1,0:T(8,128)(2,1)S(1)}, bf16[16,4096]{1,0:T(8,128)(2,1)S(1)}, u32[]{:S(2)}, u32[]{:S(2)}) collective-permute-start(bf16[16,4096]{1,0:T(8,128)(2,1)S(1)} %get-tuple-element.24), channel_id=1, source_target_pairs={{0,4},{1,5},{2,6},{3,7},{4,0},{5,1},{6,2},{7,3},{8,12},{9,13},{10,... | collective-permute-start | bytes 393224 | tf_op jit(solution)/shard_map/ppermute | solution.py:284
  78.0 14.8 %collective-permute-start.5 = (bf16[16,4096]{1,0:T(8,128)(2,1)S(1)}, bf16[16,4096]{1,0:T(8,128)(2,1)S(1)}, u32[]{:S(2)}, u32[]{:S(2)}) collective-permute-start(bf16[16,4096]{1,0:T(8,128)(2,1)S(1)} %get-tuple-element.25), channel_id=1, source_target_pairs={{0,6},{1,7},{2,4},{3,5},{4,2},{5,3},{6,0},{7,1},{8,14},{9,15},{10,... | collective-permute-start | bytes 393224 | tf_op jit(solution)/shard_map/ppermute | solution.py:284
  82.0 20.8 %collective-permute-start.9 = (bf16[16,4096]{1,0:T(8,128)(2,1)S(1)}, bf16[16,4096]{1,0:T(8,128)(2,1)S(1)}, u32[]{:S(2)}, u32[]{:S(2)}) collective-permute-start(bf16[16,4096]{1,0:T(8,128)(2,1)S(1)} %shard_map.102), channel_id=1, source_target_pairs={{0,8},{1,9},{2,10},{3,11},{4,12},{5,13},{6,14},{7,15},{8,0},{9,1},... | collective-permute-start | bytes 393224 | tf_op jit(solution)/shard_map/ppermute | solution.py:289

commit v4 on v3

--- a/solution.py
+++ b/solution.py
@@ -18,6 +18,7 @@
 FLIP_Z = [(i, i ^ 1) for i in range(SHARDS)]
 ROW_Y = [[g + 2 * k for k in range(4)] for g in range(SHARDS) if g & 6 == 0]
 ROW_X = [[g + 8 * k for k in range(4)] for g in range(8)]
+NEAR_CHIPS = [[8 * g + 2 * k + core for k in range(4)] for g in range(2) for core in range(2)]
 
 VMEM = pl.BlockSpec(memory_space=pltpu.VMEM)
 HBM = pl.BlockSpec(memory_space=pltpu.HBM)
@@ -178,22 +179,35 @@
         mixed_ref[:, cut] = (mixed * scale).astype(BF16)
     core, chip = place_ref[1] & 1, place_ref[1] >> 1
     for k in range(8):
-        start = (chip ^ (k & 3) ^ (0 if k & 4 else 4)) * 32
+        start = (chip ^ (k & 3) if k & 4 else ((chip & 4) ^ 4) + k) * 32
         cut = slice(k * 16, (k + 1) * 16)
         own, sibling = start + core * 16, start + (1 - core) * 16
         keep_ref[cut, :] = mixed_ref[pl.ds(pl.multiple_of(own, 16), 16), :]
         send_ref[cut, :] = mixed_ref[pl.ds(pl.multiple_of(sibling, 16), 16), :]
 
 
-def project_kernel(own_ref, other_ref, own_w_ref, other_w_ref, *out_refs):
-    total = jnp.dot(own_ref[...], own_w_ref[...], preferred_element_type=F32)
-    total = total + jnp.dot(other_ref[...], other_w_ref[...], preferred_element_type=F32)
+def base_kernel(own_ref, weight_ref, out_ref):
+    out_ref[...] = jnp.dot(own_ref[...], weight_ref[...], preferred_element_type=F32)
+
+
+def far_project_kernel(base_ref, other_ref, weight_ref, out_ref):
+    total = jnp.dot(other_ref[...], weight_ref[...], preferred_element_type=F32)
+    total = (total + base_ref[...]).astype(BF16)
+    for k in range(4):
+        out_ref[k] = total[k * 16 : (k + 1) * 16]
+
+
+def near_project_kernel(base_ref, other_ref, weight_ref, *out_refs):
+    total = jnp.dot(other_ref[...], weight_ref[...], preferred_element_type=F32)
+    total = total + base_ref[...]
     for k, ref in enumerate(out_refs):
         ref[...] = total[k * 16 : (k + 1) * 16].astype(ref.dtype)
 
 
-def sum_kernel(own_ref, a_ref, b_ref, c_ref, out_ref):
-    total = own_ref[...] + a_ref[...].astype(F32) + b_ref[...].astype(F32) + c_ref[...].astype(F32)
+def sum_kernel(parts_ref, out_ref):
+    total = parts_ref[0].astype(F32)
+    for k in range(1, 4):
+        total = total + parts_ref[k].astype(F32)
     out_ref[...] = total.astype(BF16)
 
 
@@ -220,6 +234,17 @@
 
 def whole(*shape):
     return pl.BlockSpec(shape, lambda j: (0,) * len(shape))
+
+
+def blocked(body, shapes, specs, out_specs, *args):
+    return pl.pallas_call(
+        body,
+        grid=(2,),
+        in_specs=specs,
+        out_specs=out_specs,
+        out_shape=shapes,
+        compiler_params=pltpu.CompilerParams(vmem_limit_bytes=16 * 1024 * 1024),
+    )(*args)
 
 
 def of(shape, dtype):
@@ -267,28 +292,38 @@
     )
     got = lax.ppermute(send, "tp", [(i, i ^ 1) for i in range(16)])
 
-    full, block = of((16, D), BF16), D // 2
+    block = D // 2
+    full = of((16, D), BF16)
     piece = pl.BlockSpec((STATE, block), lambda j: (0, j))
-    halves = []
-    for part in range(2):
-        rows = pl.BlockSpec((SPAN // 4, STATE), lambda j, part=part: (part, 0))
-        own, *parts = pl.pallas_call(
-            project_kernel,
-            grid=(D // block,),
-            in_specs=[rows, rows, piece, piece],
-            out_specs=(pl.BlockSpec((16, block), lambda j: (0, j)),) * 4,
-            out_shape=(of((16, D), F32), full, full, full),
-            compiler_params=pltpu.CompilerParams(vmem_limit_bytes=16 * 1024 * 1024),
-        )(keep, got, out_weight, other_weight)
-        near = [
-            lax.ppermute(sent, "tp", [(i, i ^ (2 * k)) for i in range(16)])
-            for k, sent in enumerate(parts, 1)
+    base = blocked(
+        base_kernel, of((SPAN // 2, D), F32), [whole(SPAN // 2, STATE), piece],
+        pl.BlockSpec((SPAN // 2, block), lambda j: (0, j)), keep, out_weight,
+    )
+
+    def inputs(part):
+        return [
+            pl.BlockSpec((SPAN // 4, block), lambda j: (part, j)),
+            pl.BlockSpec((SPAN // 4, STATE), lambda j: (part, 0)),
+            piece,
         ]
-        halves.append((own, *near))
-    away = call(sum_kernel, full, [VMEM] * 4, *halves[0])
+
+    away = blocked(
+        far_project_kernel, of((4, 16, D), BF16), inputs(0),
+        pl.BlockSpec((4, 16, block), lambda j: (0, 0, j)), base, got, other_weight,
+    )
+    away = lax.all_to_all(away, "tp", 0, 0, axis_index_groups=NEAR_CHIPS)
+    own, *parts = blocked(
+        near_project_kernel, (of((16, D), F32), full, full, full), inputs(1),
+        (pl.BlockSpec((16, block), lambda j: (0, j)),) * 4, base, got, other_weight,
+    )
+    near = [
+        lax.ppermute(sent, "tp", [(i, i ^ (2 * k)) for i in range(16)])
+        for k, sent in enumerate(parts, 1)
+    ]
+    away = call(sum_kernel, full, [VMEM], away)
     far = lax.ppermute(away, "tp", [(i, i ^ 8) for i in range(16)])
     return call(
-        finish_kernel, (full, full), [VMEM] * 7, *halves[1], far, residual_in, norm_gain[None, :]
+        finish_kernel, (full, full), [VMEM] * 7, own, *near, far, residual_in, norm_gain[None, :]
     )
 
 

time: 104 us -> 100 us (0.962)
  the two profiles are of different devices: /device:TPU:32 before, /device:TPU:64 now
where the time goes in v4:
time: 100 us; the launch traced here: 99.5 us
  starting transfers between devices  41.8 us (42%)
  blocking collectives  24.5 us (24%)
  waiting for transfers between devices  15.4 us (15%)
  Pallas kernels  12.8 us (13%)
  local copies, waits for them, and re-layouts  4.15 us (4%)
    ppermute x1, starting transfers between devices, shards(): other = lax.ppermute(local, 'seq', FLIP_Z)  13.9 us
    all_to_all x1, blocking collectives, shards(): rows = lax.all_to_all(pairs, 'seq', 0, 0, axis_index_groups=ROW_Y)  12.9 us
    all_to_all x1, blocking collectives, shards(): cols = lax.all_to_all(totals, 'seq', 0, 0, axis_index_groups=ROW_X)  11.5 us
    ppermute x1, starting transfers between devices, shards(): far = lax.ppermute(away, 'tp', [(i, i ^ 8) for i in range(16)])  10 us
    ppermute x1, waiting for transfers between devices, shards(): far = lax.ppermute(away, 'tp', [(i, i ^ 8) for i in range(16)])  9.6 us
    ppermute x3, starting transfers between devices, shards(): lax.ppermute(sent, 'tp', [(i, i ^ 2 * k) for i in range(16)])  9.21 us
    pallas_call x3, Pallas kernels, blocked(): pl.pallas_call(body, grid=(2,), in_specs=specs, out_specs=out_specs, out_...  6.73 us
    pallas_call x7, Pallas kernels, call(): pl.pallas_call(body, out_shape=shapes, in_specs=specs, out_specs=jax.tree...  6.04 us
  transfers between devices with their start and end apart: 8, of which 3 were waited for; matrix products, arithmetic and copies ran while one was open for 0% of the time, Pallas kernels for 7%

profile of v4, /device:TPU:64, one launch (start us, length us, event | category | flops | bytes accessed | tf_op | source)
XLA Modules:
  0.0 99.5 jit_solution(6076582312067378422)
XLA Ops:
  0.6 0.0 copy-start.7
  0.6 0.0 copy-start.10
  0.7 0.0 copy-start.2
  0.7 1.8 %shard_map.95.own_ref = bf16[392,128]{1,0:T(8,128)(2,1)S(1)} custom-call(s32[1,3]{1,0:T(1,128)} %starts_ref.3, f32[3,256]{1,0:T(4,128)} %decay_ref.3, bf16[256,384]{1,0:T(8,128)(2,1)} %key_ref.1, bf16[256,384]{1,0:T(8,128)(2,1)} %value_ref.1), custom_call_target="tpu_custom_call" | custom-call | tf_op jit(solution)/shard_map/pallas_call | solution.py:225
  2.4 1.9 %collective-permute-start.2 = (bf16[384,4096]{1,0:T(8,128)(2,1)}, bf16[384,4096]{1,0:T(8,128)(2,1)}, u32[]{:S(2)}, u32[]{:S(2)}) collective-permute-start(bf16[384,4096]{1,0:T(8,128)(2,1)} %weight_ref.1), channel_id=1, source_target_pairs={{0,1},{1,0},{2,3},{3,2},{4,5},{5,4},{6,7},{7,6},{8,9},{9,8},{10,11... | collective-permute-start | bytes 9437192 | tf_op jit(solution)/shard_map/ppermute | solution.py:280
  4.4 13.9 %collective-permute-start = (bf16[392,128]{1,0:T(8,128)(2,1)S(1)}, bf16[392,128]{1,0:T(8,128)(2,1)S(1)}, u32[]{:S(2)}, u32[]{:S(2)}) collective-permute-start(bf16[392,128]{1,0:T(8,128)(2,1)S(1)} %shard_map.95.own_ref), channel_id=1, source_target_pairs={{0,16},{16,0},{32,48},{48,32},{64,80},{80,64},{96,112},{112,96},{1... | collective-permute-start | bytes 301064 | tf_op jit(solution)/shard_map/ppermute | solution.py:274
  18.3 0.0 copy-start.1
  18.3 0.9 copy-done.1
  19.2 0.0 copy-start.3
  19.2 0.9 copy-done.3
  20.2 0.0 copy-start.4
  20.2 0.9 copy-done.4
  21.1 0.0 copy-start.6
  21.1 0.7 copy-done.6
  21.8 0.0 copy-start.9
  21.8 0.7 copy-done.9
  22.4 1.4 %shard_map.96.intra_ref = f32[256,384]{1,0:T(8,128)S(1)} custom-call(s32[1,3]{1,0:T(1,128)S(1)} %copy-done.9, f32[3,256]{1,0:T(4,128)S(1)} %copy-done.6, bf16[256,384]{1,0:T(8,128)(2,1)S(1)} %copy-done.1, bf16[256,384]{1,0:T(8,128)(2,1)S(1)} %copy-done.3, bf16[256,384]{1,0:T(8,128)(2,1)S(1)} %copy-done.4), custom_call_target="tpu_custom_call" | custom-call | tf_op jit(solution)/shard_map/pallas_call | solution.py:225
  23.9 0.0 copy-start
  23.9 0.1 pad_add_fusion.place_ref
  24.0 0.0 collective-permute-done.other_ref
  24.0 0.6 shard_map.97
  24.6 12.9 %all_to_all.15.parts_ref.row_ref = bf16[4,392,128]{2,1,0:T(8,128)(2,1)S(1)} all-to-all(bf16[4,392,128]{2,1,0:T(8,128)(2,1)S(1)} %shard_map.97), channel_id=1, replica_groups={{0,32,64,96},{16,48,80,112},{128,160,192,224},{144,176,208,240},{256,28..., dimensions={0} | all-to-all | bytes 802816 | tf_op jit(solution)/shard_map/all_to_all | solution.py:284
  37.5 0.1 shard_map.98
  37.6 11.5 %all_to_all.16.col_ref = bf16[4,392,128]{2,1,0:T(8,128)(2,1)S(1)} all-to-all(bf16[4,392,128]{2,1,0:T(8,128)(2,1)S(1)} %shard_map.98), channel_id=1, replica_groups={{0,128,256,384},{16,144,272,400},{32,160,288,416},{48,176,304,432},{64,..., dimensions={0} | all-to-all | bytes 802816 | tf_op jit(solution)/shard_map/all_to_all | solution.py:286
  49.1 0.0 copy-done.7
  49.1 0.0 copy-done.10
  49.1 0.0 copy-done.2
  49.1 1.3 %shard_map.99 = (bf16[128,384]{1,0:T(8,128)(2,1)S(1)}, bf16[128,384]{1,0:T(8,128)(2,1)S(1)}) custom-call(s32[2]{0:T(128)S(1)} %pad_add_fusion.place_ref, s32[1,3]{1,0:T(1,128)S(1)} %copy-done.10, f32[3,256]{1,0:T(4,128)S(1)} %copy-done.7, bf16[256,384]{1,0:T(8,128)(2,1)S(1)} %copy-done.2, f32[256,384]{1,0:T(8,128)S(1)} %shard_map.96.intra_ref, ...), custom_call_target="tpu_custom_call" | custom-call | tf_op jit(solution)/shard_map/pallas_call | solution.py:225
  50.4 1.9 %collective-permute-start.1 = (bf16[128,384]{1,0:T(8,128)(2,1)S(1)}, bf16[128,384]{1,0:T(8,128)(2,1)S(1)}, u32[]{:S(2)}, u32[]{:S(2)}) collective-permute-start(bf16[128,384]{1,0:T(8,128)(2,1)S(1)} %get-tuple-element.16), channel_id=1, source_target_pairs={{0,1},{1,0},{2,3},{3,2},{4,5},{5,4},{6,7},{7,6},{8,9},{9,8},{10,11... | collective-permute-start | bytes 294920 | tf_op jit(solution)/shard_map/ppermute | solution.py:293
  52.3 0.0 copy-done
  52.3 1.3 %shard_map.100.base_ref = f32[128,4096]{1,0:T(8,128)S(1)} custom-call(bf16[128,384]{1,0:T(8,128)(2,1)S(1)} %get-tuple-element.15.own_ref, bf16[384,4096]{1,0:T(8,128)(2,1)S(1)} %copy-done), custom_call_target="tpu_custom_call" | custom-call | tf_op jit(solution)/shard_map/pallas_call | solution.py:240
  53.6 0.0 collective-permute-done.1.other_ref
  53.6 0.0 collective-permute-done.2.weight_ref
  53.6 3.0 %shard_map.102 = bf16[4,16,4096]{2,1,0:T(8,128)(2,1)} custom-call(f32[128,4096]{1,0:T(8,128)S(1)} %shard_map.100.base_ref, bf16[128,384]{1,0:T(8,128)(2,1)S(1)} %collective-permute-done.1.other_ref, bf16[384,4096]{1,0:T(8,128)(2,1)} %collective-permute-done.2.weight_ref), custom_call_target="tpu_custom_call" | custom-call | tf_op jit(solution)/shard_map/pallas_call | solution.py:240
  56.7 4.9 %all-to-all-start.2 = ((bf16[4,16,4096]{2,1,0:T(8,128)(2,1)}), bf16[4,16,4096]{2,1,0:T(8,128)(2,1)S(1)}, u32[]{:S(2)}, u32[]{:S(2)}) async-start(bf16[4,16,4096]{2,1,0:T(8,128)(2,1)} %shard_map.102), calls=%async_computation.2 | async-start | bytes 1048576 | tf_op jit(solution)/shard_map/all_to_all | solution.py:314
  61.5 0.0 copy-start.5
  61.5 0.0 copy-start.8
  61.5 2.4 %shard_map.101 = (f32[16,4096]{1,0:T(8,128)S(1)}, bf16[16,4096]{1,0:T(8,128)(2,1)S(1)}, bf16[16,4096]{1,0:T(8,128)(2,1)S(1)}, bf16[16,4096]{1,0:T(8,128)(2,1)S(1)}) custom-call(f32[128,4096]{1,0:T(8,128)S(1)} %shard_map.100.base_ref, bf16[128,384]{1,0:T(8,128)(2,1)S(1)} %collective-permute-done.1.other_ref, bf16[384,4096]{1,0:T(8,128)(2,1)} %collective-permute-done.2.weight_ref), custom_call_target="tpu_custom_call" | custom-call | tf_op jit(solution)/shard_map/pallas_call | solution.py:240
  63.9 3.4 %collective-permute-start.3 = (bf16[16,4096]{1,0:T(8,128)(2,1)S(1)}, bf16[16,4096]{1,0:T(8,128)(2,1)S(1)}, u32[]{:S(2)}, u32[]{:S(2)}) collective-permute-start(bf16[16,4096]{1,0:T(8,128)(2,1)S(1)} %get-tuple-element.19), channel_id=1, source_target_pairs={{0,2},{1,3},{2,0},{3,1},{4,6},{5,7},{6,4},{7,5},{8,10},{9,11},{10,... | collective-permute-start | bytes 393224 | tf_op jit(solution)/shard_map/ppermute | solution.py:320
  67.3 2.6 %collective-permute-start.4 = (bf16[16,4096]{1,0:T(8,128)(2,1)S(1)}, bf16[16,4096]{1,0:T(8,128)(2,1)S(1)}, u32[]{:S(2)}, u32[]{:S(2)}) collective-permute-start(bf16[16,4096]{1,0:T(8,128)(2,1)S(1)} %get-tuple-element.20), channel_id=1, source_target_pairs={{0,4},{1,5},{2,6},{3,7},{4,0},{5,1},{6,2},{7,3},{8,12},{9,13},{10,... | collective-permute-start | bytes 393224 | tf_op jit(solution)/shard_map/ppermute | solution.py:320
  69.9 3.2 %collective-permute-start.5 = (bf16[16,4096]{1,0:T(8,128)(2,1)S(1)}, bf16[16,4096]{1,0:T(8,128)(2,1)S(1)}, u32[]{:S(2)}, u32[]{:S(2)}) collective-permute-start(bf16[16,4096]{1,0:T(8,128)(2,1)S(1)} %get-tuple-element.21), channel_id=1, source_target_pairs={{0,6},{1,7},{2,4},{3,5},{4,2},{5,3},{6,0},{7,1},{8,14},{9,15},{10,... | collective-permute-start | bytes 393224 | tf_op jit(solution)/shard_map/ppermute | solution.py:320
  73.2 0.9 all-to-all-done.2.parts_ref
  74.1 0.1 shard_map.103
  74.2 10.0 %collective-permute-start.6 = (bf16[16,4096]{1,0:T(8,128)(2,1)S(1)}, bf16[16,4096]{1,0:T(8,128)(2,1)S(1)}, u32[]{:S(2)}, u32[]{:S(2)}) collective-permute-start(bf16[16,4096]{1,0:T(8,128)(2,1)S(1)} %shard_map.103), channel_id=1, source_target_pairs={{0,8},{1,9},{2,10},{3,11},{4,12},{5,13},{6,14},{7,15},{8,0},{9,1},... | collective-permute-start | bytes 393224 | tf_op jit(solution)/shard_map/ppermute | solution.py:324
  84.2 0.0 collective-permute-done.3.refs_0_
  84.2 0.0 collective-permute-done.4.refs_1_
  84.2 4.9 %collective-permute-done.5.refs_2_ = bf16[16,4096]{1,0:T(8,128)(2,1)S(1)} collective-permute-done((bf16[16,4096]{1,0:T(8,128)(2,1)S(1)}, bf16[16,4096]{1,0:T(8,128)(2,1)S(1)}, u32[]{:S(2)}, u32[]{:S(2)}) %collective-permute-start.5) | collective-permute-done | bytes 131104 | tf_op jit(solution)/shard_map/ppermute | solution.py:320
  89.0 9.6 %collective-permute-done.6.refs_3_ = bf16[16,4096]{1,0:T(8,128)(2,1)S(1)} collective-permute-done((bf16[16,4096]{1,0:T(8,128)(2,1)S(1)}, bf16[16,4096]{1,0:T(8,128)(2,1)S(1)}, u32[]{:S(2)}, u32[]{:S(2)}) %collective-permute-start.6) | collective-permute-done | bytes 131104 | tf_op jit(solution)/shard_map/ppermute | solution.py:324
  98.6 0.0 copy-done.5
  98.6 0.0 copy-done.8
  98.6 0.9 shard_map.104
Async XLA Ops:
  0.6 48.5 %copy-start.7 = (f32[3,256]{1,0:T(4,128)S(1)}, f32[3,256]{1,0:T(4,128)}, u32[]{:S(2)}) copy-start(f32[3,256]{1,0:T(4,128)} %decay_ref.3) | copy-start | bytes 9220
  0.6 48.5 %copy-start.10 = (s32[1,3]{1,0:T(1,128)S(1)}, s32[1,3]{1,0:T(1,128)}, u32[]{:S(2)}) copy-start(s32[1,3]{1,0:T(1,128)} %starts_ref.3) | copy-start | bytes 40
  0.7 48.5 %copy-start.2 = (bf16[256,384]{1,0:T(8,128)(2,1)S(1)}, bf16[256,384]{1,0:T(8,128)(2,1)}, u32[]{:S(2)}) copy-start(bf16[256,384]{1,0:T(8,128)(2,1)} %query_ref.2) | copy-start | bytes 589828
  2.4 51.2 %collective-permute-start.2 = (bf16[384,4096]{1,0:T(8,128)(2,1)}, bf16[384,4096]{1,0:T(8,128)(2,1)}, u32[]{:S(2)}, u32[]{:S(2)}) collective-permute-start(bf16[384,4096]{1,0:T(8,128)(2,1)} %weight_ref.1), channel_id=1, source_target_pairs={{0,1},{1,0},{2,3},{3,2},{4,5},{5,4},{6,7},{7,6},{8,9},{9,8},{10,11... | collective-permute-start | bytes 9437192 | tf_op jit(solution)/shard_map/ppermute | solution.py:280
  4.4 19.6 %collective-permute-start = (bf16[392,128]{1,0:T(8,128)(2,1)S(1)}, bf16[392,128]{1,0:T(8,128)(2,1)S(1)}, u32[]{:S(2)}, u32[]{:S(2)}) collective-permute-start(bf16[392,128]{1,0:T(8,128)(2,1)S(1)} %shard_map.95.own_ref), channel_id=1, source_target_pairs={{0,16},{16,0},{32,48},{48,32},{64,80},{80,64},{96,112},{112,96},{1... | collective-permute-start | bytes 301064 | tf_op jit(solution)/shard_map/ppermute | solution.py:274
  18.3 0.9 copy-start.1
  19.2 0.9 copy-start.3
  20.2 0.9 copy-start.4
  21.1 0.7 copy-start.6
  21.8 0.7 copy-start.9
  23.9 28.4 %copy-start = (bf16[384,4096]{1,0:T(8,128)(2,1)S(1)}, bf16[384,4096]{1,0:T(8,128)(2,1)}, u32[]{:S(2)}) copy-start(bf16[384,4096]{1,0:T(8,128)(2,1)} %weight_ref.1) | copy-start | bytes 9437188
  50.4 3.2 %collective-permute-start.1 = (bf16[128,384]{1,0:T(8,128)(2,1)S(1)}, bf16[128,384]{1,0:T(8,128)(2,1)S(1)}, u32[]{:S(2)}, u32[]{:S(2)}) collective-permute-start(bf16[128,384]{1,0:T(8,128)(2,1)S(1)} %get-tuple-element.16), channel_id=1, source_target_pairs={{0,1},{1,0},{2,3},{3,2},{4,5},{5,4},{6,7},{7,6},{8,9},{9,8},{10,11... | collective-permute-start | bytes 294920 | tf_op jit(solution)/shard_map/ppermute | solution.py:293
  56.7 17.4 %all-to-all-start.2 = ((bf16[4,16,4096]{2,1,0:T(8,128)(2,1)}), bf16[4,16,4096]{2,1,0:T(8,128)(2,1)S(1)}, u32[]{:S(2)}, u32[]{:S(2)}) async-start(bf16[4,16,4096]{2,1,0:T(8,128)(2,1)} %shard_map.102), calls=%async_computation.2 | async-start | bytes 1048576 | tf_op jit(solution)/shard_map/all_to_all | solution.py:314
  61.5 37.1 %copy-start.5 = (bf16[16,4096]{1,0:T(8,128)(2,1)S(1)}, bf16[16,4096]{1,0:T(8,128)(2,1)}, u32[]{:S(2)}) copy-start(bf16[16,4096]{1,0:T(8,128)(2,1)} %refs_4_.1) | copy-start | bytes 393220
  61.5 37.1 %copy-start.8 = (f32[4096]{0:T(1024)S(1)}, f32[4096]{0:T(1024)}, u32[]{:S(2)}) copy-start(f32[4096]{0:T(1024)} %param.15) | copy-start | bytes 49156
  63.9 20.2 %collective-permute-start.3 = (bf16[16,4096]{1,0:T(8,128)(2,1)S(1)}, bf16[16,4096]{1,0:T(8,128)(2,1)S(1)}, u32[]{:S(2)}, u32[]{:S(2)}) collective-permute-start(bf16[16,4096]{1,0:T(8,128)(2,1)S(1)} %get-tuple-element.19), channel_id=1, source_target_pairs={{0,2},{1,3},{2,0},{3,1},{4,6},{5,7},{6,4},{7,5},{8,10},{9,11},{10,... | collective-permute-start | bytes 393224 | tf_op jit(solution)/shard_map/ppermute | solution.py:320
  67.3 16.9 %collective-permute-start.4 = (bf16[16,4096]{1,0:T(8,128)(2,1)S(1)}, bf16[16,4096]{1,0:T(8,128)(2,1)S(1)}, u32[]{:S(2)}, u32[]{:S(2)}) collective-permute-start(bf16[16,4096]{1,0:T(8,128)(2,1)S(1)} %get-tuple-element.20), channel_id=1, source_target_pairs={{0,4},{1,5},{2,6},{3,7},{4,0},{5,1},{6,2},{7,3},{8,12},{9,13},{10,... | collective-permute-start | bytes 393224 | tf_op jit(solution)/shard_map/ppermute | solution.py:320
  69.9 19.1 %collective-permute-start.5 = (bf16[16,4096]{1,0:T(8,128)(2,1)S(1)}, bf16[16,4096]{1,0:T(8,128)(2,1)S(1)}, u32[]{:S(2)}, u32[]{:S(2)}) collective-permute-start(bf16[16,4096]{1,0:T(8,128)(2,1)S(1)} %get-tuple-element.21), channel_id=1, source_target_pairs={{0,6},{1,7},{2,4},{3,5},{4,2},{5,3},{6,0},{7,1},{8,14},{9,15},{10,... | collective-permute-start | bytes 393224 | tf_op jit(solution)/shard_map/ppermute | solution.py:320
  74.2 24.5 %collective-permute-start.6 = (bf16[16,4096]{1,0:T(8,128)(2,1)S(1)}, bf16[16,4096]{1,0:T(8,128)(2,1)S(1)}, u32[]{:S(2)}, u32[]{:S(2)}) collective-permute-start(bf16[16,4096]{1,0:T(8,128)(2,1)S(1)} %shard_map.103), channel_id=1, source_target_pairs={{0,8},{1,9},{2,10},{3,11},{4,12},{5,13},{6,14},{7,15},{8,0},{9,1},... | collective-permute-start | bytes 393224 | tf_op jit(solution)/shard_map/ppermute | solution.py:324

commit v5 on v4

--- a/solution.py
+++ b/solution.py
@@ -156,7 +156,7 @@
 
 def attend_kernel(
     place_ref, starts_ref, decay_ref, query_ref, intra_ref, other_ref, row_ref, col_ref,
-    send_ref, keep_ref, mixed_ref,
+    weight_ref, send_ref, keep_ref, mixed_ref, sibling_ref,
 ):
     odd = place_ref[0] & 1 == 1
     row, col = grid_iotas()
@@ -183,25 +183,31 @@
         cut = slice(k * 16, (k + 1) * 16)
         own, sibling = start + core * 16, start + (1 - core) * 16
         keep_ref[cut, :] = mixed_ref[pl.ds(pl.multiple_of(own, 16), 16), :]
-        send_ref[cut, :] = mixed_ref[pl.ds(pl.multiple_of(sibling, 16), 16), :]
-
-
-def base_kernel(own_ref, weight_ref, out_ref):
+        sibling_ref[cut, :] = mixed_ref[pl.ds(pl.multiple_of(sibling, 16), 16), :]
+    send_ref[...] = jnp.dot(
+        sibling_ref[...], weight_ref[...], preferred_element_type=F32
+    ).astype(BF16)
+
+
+def keep_kernel(own_ref, weight_ref, out_ref):
     out_ref[...] = jnp.dot(own_ref[...], weight_ref[...], preferred_element_type=F32)
 
 
-def far_project_kernel(base_ref, other_ref, weight_ref, out_ref):
-    total = jnp.dot(other_ref[...], weight_ref[...], preferred_element_type=F32)
-    total = (total + base_ref[...]).astype(BF16)
+def far_kernel(keep_ref, got_ref, out_ref, sum_ref, sems):
+    copies = []
     for k in range(4):
-        out_ref[k] = total[k * 16 : (k + 1) * 16]
-
-
-def near_project_kernel(base_ref, other_ref, weight_ref, *out_refs):
-    total = jnp.dot(other_ref[...], weight_ref[...], preferred_element_type=F32)
-    total = total + base_ref[...]
+        cut = slice(k * 16, (k + 1) * 16)
+        sum_ref[k] = (keep_ref[cut, :] + got_ref[cut, :].astype(F32)).astype(BF16)
+        copies.append(pltpu.make_async_copy(sum_ref.at[k], out_ref.at[k], sems.at[k]))
+        copies[-1].start()
+    for copy in copies:
+        copy.wait()
+
+
+def near_kernel(keep_ref, got_ref, *out_refs):
     for k, ref in enumerate(out_refs):
-        ref[...] = total[k * 16 : (k + 1) * 16].astype(ref.dtype)
+        cut = slice(64 + k * 16, 80 + k * 16)
+        ref[...] = (keep_ref[cut, :] + got_ref[cut, :].astype(F32)).astype(ref.dtype)
 
 
 def sum_kernel(parts_ref, out_ref):
@@ -221,28 +227,13 @@
     normed_ref[...] = (hidden * scale * gain_ref[...]).astype(BF16)
 
 
-def call(body, shapes, specs, *args, scratch=()):
+def call(body, shapes, specs, *args, scratch=(), outs=VMEM):
     return pl.pallas_call(
         body,
         out_shape=shapes,
         in_specs=specs,
-        out_specs=jax.tree.map(lambda _: VMEM, shapes),
+        out_specs=jax.tree.map(lambda _: outs, shapes),
         scratch_shapes=list(scratch),
-        compiler_params=pltpu.CompilerParams(vmem_limit_bytes=16 * 1024 * 1024),
-    )(*args)
-
-
-def whole(*shape):
-    return pl.BlockSpec(shape, lambda j: (0,) * len(shape))
-
-
-def blocked(body, shapes, specs, out_specs, *args):
-    return pl.pallas_call(
-        body,
-        grid=(2,),
-        in_specs=specs,
-        out_specs=out_specs,
-        out_shape=shapes,
         compiler_params=pltpu.CompilerParams(vmem_limit_bytes=16 * 1024 * 1024),
     )(*args)
 
@@ -276,45 +267,28 @@
         intra_kernel, of((SPAN, STATE), F32), [SMEM, VMEM, VMEM, VMEM, VMEM],
         doc_starts, log_decay, late_query, key_rows, value_rows,
     )
-    late_weight = lax.optimization_barrier((local, out_weight))[1]
-    other_weight = lax.ppermute(late_weight, "tp", [(i, i ^ 1) for i in range(16)])
     other, intra = lax.optimization_barrier((other, intra))
     four = of((4, PAYLOAD, HDIM), BF16)
     pairs = call(pair_kernel, four, [SMEM, VMEM, VMEM], place, local, other)
     rows = lax.all_to_all(pairs, "seq", 0, 0, axis_index_groups=ROW_Y)
     totals = call(row_kernel, four, [VMEM], rows)
     cols = lax.all_to_all(totals, "seq", 0, 0, axis_index_groups=ROW_X)
-    half = of((SPAN // 2, STATE), BF16)
     send, keep = call(
-        attend_kernel, (half, half), [SMEM, SMEM] + [VMEM] * 6,
-        place, doc_starts, log_decay, query_rows, intra, other, rows, cols,
-        scratch=[pltpu.VMEM((SPAN, STATE), BF16)],
+        attend_kernel, (of((SPAN // 2, D), BF16), of((SPAN // 2, STATE), BF16)),
+        [SMEM, SMEM] + [VMEM] * 7,
+        place, doc_starts, log_decay, query_rows, intra, other, rows, cols, out_weight,
+        scratch=[pltpu.VMEM((SPAN, STATE), BF16), pltpu.VMEM((SPAN // 2, STATE), BF16)],
     )
     got = lax.ppermute(send, "tp", [(i, i ^ 1) for i in range(16)])
-
-    block = D // 2
+    keep = call(keep_kernel, of((SPAN // 2, D), F32), [VMEM, VMEM], keep, out_weight)
     full = of((16, D), BF16)
-    piece = pl.BlockSpec((STATE, block), lambda j: (0, j))
-    base = blocked(
-        base_kernel, of((SPAN // 2, D), F32), [whole(SPAN // 2, STATE), piece],
-        pl.BlockSpec((SPAN // 2, block), lambda j: (0, j)), keep, out_weight,
-    )
-
-    def inputs(part):
-        return [
-            pl.BlockSpec((SPAN // 4, block), lambda j: (part, j)),
-            pl.BlockSpec((SPAN // 4, STATE), lambda j: (part, 0)),
-            piece,
-        ]
-
-    away = blocked(
-        far_project_kernel, of((4, 16, D), BF16), inputs(0),
-        pl.BlockSpec((4, 16, block), lambda j: (0, 0, j)), base, got, other_weight,
+    away = call(
+        far_kernel, pltpu.HBM((4, 16, D), BF16), [VMEM, VMEM], keep, got,
+        scratch=[pltpu.VMEM((4, 16, D), BF16), pltpu.SemaphoreType.DMA((4,))], outs=HBM,
     )
     away = lax.all_to_all(away, "tp", 0, 0, axis_index_groups=NEAR_CHIPS)
-    own, *parts = blocked(
-        near_project_kernel, (of((16, D), F32), full, full, full), inputs(1),
-        (pl.BlockSpec((16, block), lambda j: (0, j)),) * 4, base, got, other_weight,
+    own, *parts = call(
+        near_kernel, (of((16, D), F32), full, full, full), [VMEM, VMEM], keep, got
     )
     near = [
         lax.ppermute(sent, "tp", [(i, i ^ (2 * k)) for i in range(16)])

time: 100 us -> 99.9 us (level)
  waiting for transfers between devices: 15.4 us -> 17.8 us
  starting transfers between devices: 41.8 us -> 40.7 us
    pallas_call x3 -> x0, Pallas kernels: 6.73 us -> none  [blocked(): pl.pallas_call(body, grid=(2,), in_specs=specs, out_specs=out_specs, out_...]
    pallas_call x7 -> x10, Pallas kernels: 6.04 us -> 11.9 us  [call(): pl.pallas_call(body, out_shape=shapes, in_specs=specs, out_specs=jax.tree...]
    ppermute x3, waiting for transfers between devices: 4.86 us -> 1.39 us  [shards(): lax.ppermute(sent, 'tp', [(i, i ^ 2 * k) for i in range(16)])]
    ppermute x1, waiting for transfers between devices: 9.6 us -> 11.8 us  [shards(): far = lax.ppermute(away, 'tp', [(i, i ^ 8) for i in range(16)])]
    ppermute x1 -> x0, starting transfers between devices: 1.92 us -> none  [shards(): lax.ppermute(late_weight, 'tp', [(i, i ^ 1) for i in range(16)])]
    ppermute x1, waiting for transfers between devices: 0.01 us -> 1.9 us  [shards(): got = lax.ppermute(send, 'tp', [(i, i ^ 1) for i in range(16)])]
    all_to_all x1, waiting for transfers between devices: 0.91 us -> 2.7 us  [shards(): away = lax.all_to_all(away, 'tp', 0, 0, axis_index_groups=NEAR_CHIPS)]
    unnamed x22 -> x24, local copies, waits for them, and re-layouts: 4.15 us -> 4.15 us
  transfers between devices with their start and end apart: 8 -> 7, of which waited for: 3 -> 4; matrix products, arithmetic and copies ran while one was open for 0% -> 0% of each run, Pallas kernels for 7% -> 4%
where the time goes in v5:
time: 99.9 us; the launch traced here: 99.3 us
  starting transfers between devices  40.7 us (41%)
  blocking collectives  23.9 us (24%)
  waiting for transfers between devices  17.8 us (18%)
  Pallas kernels  11.9 us (12%)
  local copies, waits for them, and re-layouts  4.15 us (4%)
    ppermute x1, starting transfers between devices, shards(): other = lax.ppermute(local, 'seq', FLIP_Z)  13.9 us
    all_to_all x1, blocking collectives, shards(): rows = lax.all_to_all(pairs, 'seq', 0, 0, axis_index_groups=ROW_Y)  12.1 us
    pallas_call x10, Pallas kernels, call(): pl.pallas_call(body, out_shape=shapes, in_specs=specs, out_specs=jax.tree...  11.9 us
    all_to_all x1, blocking collectives, shards(): cols = lax.all_to_all(totals, 'seq', 0, 0, axis_index_groups=ROW_X)  11.8 us
    ppermute x1, waiting for transfers between devices, shards(): far = lax.ppermute(away, 'tp', [(i, i ^ 8) for i in range(16)])  11.8 us
    ppermute x1, starting transfers between devices, shards(): far = lax.ppermute(away, 'tp', [(i, i ^ 8) for i in range(16)])  9.97 us
    ppermute x3, starting transfers between devices, shards(): lax.ppermute(sent, 'tp', [(i, i ^ 2 * k) for i in range(16)])  9.2 us
    all_to_all x1, starting transfers between devices, shards(): away = lax.all_to_all(away, 'tp', 0, 0, axis_index_groups=NEAR_CHIPS)  5.69 us
  transfers between devices with their start and end apart: 7, of which 4 were waited for; matrix products, arithmetic and copies ran while one was open for 0% of the time, Pallas kernels for 4%

profile of v5, /device:TPU:64, one launch (start us, length us, event | category | flops | bytes accessed | tf_op | source)
XLA Modules:
  0.0 99.3 jit_solution(7998037493155603853)
XLA Ops:
  0.6 0.0 copy-start
  0.6 2.5 %shard_map.95.own_ref = bf16[392,128]{1,0:T(8,128)(2,1)} custom-call(s32[1,3]{1,0:T(1,128)} %starts_ref.3, f32[3,256]{1,0:T(4,128)} %decay_ref.3, bf16[256,384]{1,0:T(8,128)(2,1)} %key_ref.1, bf16[256,384]{1,0:T(8,128)(2,1)} %value_ref.1), custom_call_target="tpu_custom_call" | custom-call | tf_op jit(solution)/shard_map/pallas_call | solution.py:231
  3.2 13.9 %collective-permute-start = (bf16[392,128]{1,0:T(8,128)(2,1)}, bf16[392,128]{1,0:T(8,128)(2,1)}, u32[]{:S(2)}, u32[]{:S(2)}) collective-permute-start(bf16[392,128]{1,0:T(8,128)(2,1)} %shard_map.95.own_ref), channel_id=1, source_target_pairs={{0,16},{16,0},{32,48},{48,32},{64,80},{80,64},{96,112},{112,96},{1... | collective-permute-start | bytes 301064 | tf_op jit(solution)/shard_map/ppermute | solution.py:265
  17.1 0.0 copy-start.2
  17.1 0.9 copy-done.2
  18.0 0.0 copy-start.4
  18.0 0.9 copy-done.4
  19.0 0.0 copy-start.5
  19.0 0.9 copy-done.5
  19.9 0.0 copy-start.7
  19.9 0.7 copy-done.7
  20.6 0.0 copy-start.10
  20.6 0.7 copy-done.10
  21.2 0.0 copy-start.8
  21.2 0.0 copy-start.11
  21.2 1.4 %shard_map.96.intra_ref = f32[256,384]{1,0:T(8,128)S(1)} custom-call(s32[1,3]{1,0:T(1,128)S(1)} %copy-done.10, f32[3,256]{1,0:T(4,128)S(1)} %copy-done.7, bf16[256,384]{1,0:T(8,128)(2,1)S(1)} %copy-done.2, bf16[256,384]{1,0:T(8,128)(2,1)S(1)} %copy-done.4, bf16[256,384]{1,0:T(8,128)(2,1)S(1)} %copy-done.5), custom_call_target="tpu_custom_call" | custom-call | tf_op jit(solution)/shard_map/pallas_call | solution.py:231
  22.7 0.0 copy-start.3
  22.7 0.1 pad_add_fusion.place_ref
  22.7 0.0 collective-permute-done.other_ref
  22.8 1.0 %shard_map.97 = bf16[4,392,128]{2,1,0:T(8,128)(2,1)S(1)} custom-call(s32[2]{0:T(128)S(1)} %pad_add_fusion.place_ref, bf16[392,128]{1,0:T(8,128)(2,1)} %shard_map.95.own_ref, bf16[392,128]{1,0:T(8,128)(2,1)} %collective-permute-done.other_ref), custom_call_target="tpu_custom_call" | custom-call | tf_op jit(solution)/shard_map/pallas_call | solution.py:231
  23.8 12.1 %all_to_all.15.parts_ref.row_ref = bf16[4,392,128]{2,1,0:T(8,128)(2,1)S(1)} all-to-all(bf16[4,392,128]{2,1,0:T(8,128)(2,1)S(1)} %shard_map.97), channel_id=1, replica_groups={{0,32,64,96},{16,48,80,112},{128,160,192,224},{144,176,208,240},{256,28..., dimensions={0} | all-to-all | bytes 802816 | tf_op jit(solution)/shard_map/all_to_all | solution.py:273
  35.9 0.0 copy-start.1
  35.9 0.1 shard_map.98
  36.0 11.8 %all_to_all.16.col_ref = bf16[4,392,128]{2,1,0:T(8,128)(2,1)S(1)} all-to-all(bf16[4,392,128]{2,1,0:T(8,128)(2,1)S(1)} %shard_map.98), channel_id=1, replica_groups={{0,128,256,384},{16,144,272,400},{32,160,288,416},{48,176,304,432},{64,..., dimensions={0} | all-to-all | bytes 802816 | tf_op jit(solution)/shard_map/all_to_all | solution.py:275
  47.8 0.0 copy-done
  47.8 0.0 copy-done.8
  47.8 0.0 copy-done.11
  47.8 0.0 copy-done.3
  47.8 2.5 %shard_map.99 = (bf16[128,4096]{1,0:T(8,128)(2,1)S(1)}, bf16[128,384]{1,0:T(8,128)(2,1)S(1)}) custom-call(s32[2]{0:T(128)S(1)} %pad_add_fusion.place_ref, s32[1,3]{1,0:T(1,128)S(1)} %copy-done.11, f32[3,256]{1,0:T(4,128)S(1)} %copy-done.8, bf16[256,384]{1,0:T(8,128)(2,1)S(1)} %copy-done.3, f32[256,384]{1,0:T(8,128)S(1)} %shard_map.96.intra_ref, ...), custom_call_target="tpu_custom_call" | custom-call | tf_op jit(solution)/shard_map/pallas_call | solution.py:231
  50.3 1.9 %collective-permute-start.1 = (bf16[128,4096]{1,0:T(8,128)(2,1)S(1)}, bf16[128,4096]{1,0:T(8,128)(2,1)S(1)}, u32[]{:S(2)}, u32[]{:S(2)}) collective-permute-start(bf16[128,4096]{1,0:T(8,128)(2,1)S(1)} %get-tuple-element.15), channel_id=1, source_target_pairs={{0,1},{1,0},{2,3},{3,2},{4,5},{5,4},{6,7},{7,6},{8,9},{9,8},{10,11... | collective-permute-start | bytes 3145736 | tf_op jit(solution)/shard_map/ppermute | solution.py:282
  52.3 0.0 copy-done.1
  52.3 0.7 shard_map.100.keep_ref
  53.0 1.9 %collective-permute-done.1.got_ref = bf16[128,4096]{1,0:T(8,128)(2,1)S(1)} collective-permute-done((bf16[128,4096]{1,0:T(8,128)(2,1)S(1)}, bf16[128,4096]{1,0:T(8,128)(2,1)S(1)}, u32[]{:S(2)}, u32[]{:S(2)}) %collective-permute-start.1) | collective-permute-done | bytes 1048608 | tf_op jit(solution)/shard_map/ppermute | solution.py:282
  54.9 0.8 shard_map.102
  55.8 0.0 copy-start.6
  55.8 0.0 copy-start.9
  55.8 5.7 %all-to-all-start.2 = ((bf16[4,16,4096]{2,1,0:T(8,128)(2,1)}), bf16[4,16,4096]{2,1,0:T(8,128)(2,1)}, u32[]{:S(2)}, u32[]{:S(2)}) async-start(bf16[4,16,4096]{2,1,0:T(8,128)(2,1)} %shard_map.102), calls=%async_computation.2 | async-start | bytes 1048576 | tf_op jit(solution)/shard_map/all_to_all | solution.py:289
  61.5 0.8 shard_map.101
  62.3 3.4 %collective-permute-start.2 = (bf16[16,4096]{1,0:T(8,128)(2,1)}, bf16[16,4096]{1,0:T(8,128)(2,1)S(1)}, u32[]{:S(2)}, u32[]{:S(2)}) collective-permute-start(bf16[16,4096]{1,0:T(8,128)(2,1)} %get-tuple-element.17), channel_id=1, source_target_pairs={{0,2},{1,3},{2,0},{3,1},{4,6},{5,7},{6,4},{7,5},{8,10},{9,11},{10,... | collective-permute-start | bytes 393224 | tf_op jit(solution)/shard_map/ppermute | solution.py:294
  65.6 3.0 %collective-permute-start.3 = (bf16[16,4096]{1,0:T(8,128)(2,1)}, bf16[16,4096]{1,0:T(8,128)(2,1)S(1)}, u32[]{:S(2)}, u32[]{:S(2)}) collective-permute-start(bf16[16,4096]{1,0:T(8,128)(2,1)} %get-tuple-element.18), channel_id=1, source_target_pairs={{0,4},{1,5},{2,6},{3,7},{4,0},{5,1},{6,2},{7,3},{8,12},{9,13},{10,... | collective-permute-start | bytes 393224 | tf_op jit(solution)/shard_map/ppermute | solution.py:294
  68.6 2.8 %collective-permute-start.4 = (bf16[16,4096]{1,0:T(8,128)(2,1)}, bf16[16,4096]{1,0:T(8,128)(2,1)S(1)}, u32[]{:S(2)}, u32[]{:S(2)}) collective-permute-start(bf16[16,4096]{1,0:T(8,128)(2,1)} %get-tuple-element.19), channel_id=1, source_target_pairs={{0,6},{1,7},{2,4},{3,5},{4,2},{5,3},{6,0},{7,1},{8,14},{9,15},{10,... | collective-permute-start | bytes 393224 | tf_op jit(solution)/shard_map/ppermute | solution.py:294
  71.5 2.7 %all-to-all-done.2.parts_ref = bf16[4,16,4096]{2,1,0:T(8,128)(2,1)} async-done(((bf16[4,16,4096]{2,1,0:T(8,128)(2,1)}), bf16[4,16,4096]{2,1,0:T(8,128)(2,1)}, u32[]{:S(2)}, u32[]{:S(2)}) %all-to-all-start.2) | async-done | bytes 524320 | tf_op jit(solution)/shard_map/all_to_all | solution.py:289
  74.2 1.1 %shard_map.103 = bf16[16,4096]{1,0:T(8,128)(2,1)S(1)} custom-call(bf16[4,16,4096]{2,1,0:T(8,128)(2,1)} %all-to-all-done.2.parts_ref), custom_call_target="tpu_custom_call" | custom-call | tf_op jit(solution)/shard_map/pallas_call | solution.py:231
  75.3 10.0 %collective-permute-start.5 = (bf16[16,4096]{1,0:T(8,128)(2,1)S(1)}, bf16[16,4096]{1,0:T(8,128)(2,1)S(1)}, u32[]{:S(2)}, u32[]{:S(2)}) collective-permute-start(bf16[16,4096]{1,0:T(8,128)(2,1)S(1)} %shard_map.103), channel_id=1, source_target_pairs={{0,8},{1,9},{2,10},{3,11},{4,12},{5,13},{6,14},{7,15},{8,0},{9,1},... | collective-permute-start | bytes 393224 | tf_op jit(solution)/shard_map/ppermute | solution.py:298
  85.3 0.0 collective-permute-done.2.refs_0_
  85.3 0.0 collective-permute-done.3.refs_1_
  85.3 1.4 %collective-permute-done.4.refs_2_ = bf16[16,4096]{1,0:T(8,128)(2,1)S(1)} collective-permute-done((bf16[16,4096]{1,0:T(8,128)(2,1)}, bf16[16,4096]{1,0:T(8,128)(2,1)S(1)}, u32[]{:S(2)}, u32[]{:S(2)}) %collective-permute-start.4) | collective-permute-done | bytes 131104 | tf_op jit(solution)/shard_map/ppermute | solution.py:294
  86.7 11.8 %collective-permute-done.5.refs_3_ = bf16[16,4096]{1,0:T(8,128)(2,1)S(1)} collective-permute-done((bf16[16,4096]{1,0:T(8,128)(2,1)S(1)}, bf16[16,4096]{1,0:T(8,128)(2,1)S(1)}, u32[]{:S(2)}, u32[]{:S(2)}) %collective-permute-start.5) | collective-permute-done | bytes 131104 | tf_op jit(solution)/shard_map/ppermute | solution.py:298
  98.4 0.0 copy-done.6
  98.4 0.0 copy-done.9
  98.5 0.9 shard_map.104
Async XLA Ops:
  0.6 47.2 %copy-start = (bf16[384,4096]{1,0:T(8,128)(2,1)S(1)}, bf16[384,4096]{1,0:T(8,128)(2,1)}, u32[]{:S(2)}) copy-start(bf16[384,4096]{1,0:T(8,128)(2,1)} %weight_ref.3) | copy-start | bytes 9437188
  3.2 19.6 %collective-permute-start = (bf16[392,128]{1,0:T(8,128)(2,1)}, bf16[392,128]{1,0:T(8,128)(2,1)}, u32[]{:S(2)}, u32[]{:S(2)}) collective-permute-start(bf16[392,128]{1,0:T(8,128)(2,1)} %shard_map.95.own_ref), channel_id=1, source_target_pairs={{0,16},{16,0},{32,48},{48,32},{64,80},{80,64},{96,112},{112,96},{1... | collective-permute-start | bytes 301064 | tf_op jit(solution)/shard_map/ppermute | solution.py:265
  17.1 0.9 copy-start.2
  18.0 0.9 copy-start.4
  19.0 0.9 copy-start.5
  19.9 0.7 copy-start.7
  20.6 0.7 copy-start.10
  21.2 26.6 %copy-start.8 = (f32[3,256]{1,0:T(4,128)S(1)}, f32[3,256]{1,0:T(4,128)}, u32[]{:S(2)}) copy-start(f32[3,256]{1,0:T(4,128)} %decay_ref.3) | copy-start | bytes 9220
  21.2 26.6 %copy-start.11 = (s32[1,3]{1,0:T(1,128)S(1)}, s32[1,3]{1,0:T(1,128)}, u32[]{:S(2)}) copy-start(s32[1,3]{1,0:T(1,128)} %starts_ref.3) | copy-start | bytes 40
  22.7 25.2 %copy-start.3 = (bf16[256,384]{1,0:T(8,128)(2,1)S(1)}, bf16[256,384]{1,0:T(8,128)(2,1)}, u32[]{:S(2)}) copy-start(bf16[256,384]{1,0:T(8,128)(2,1)} %query_ref.2) | copy-start | bytes 589828
  35.9 16.3 %copy-start.1 = (bf16[384,4096]{1,0:T(8,128)(2,1)S(1)}, bf16[384,4096]{1,0:T(8,128)(2,1)}, u32[]{:S(2)}) copy-start(bf16[384,4096]{1,0:T(8,128)(2,1)} %weight_ref.3) | copy-start | bytes 9437188
  50.3 4.6 %collective-permute-start.1 = (bf16[128,4096]{1,0:T(8,128)(2,1)S(1)}, bf16[128,4096]{1,0:T(8,128)(2,1)S(1)}, u32[]{:S(2)}, u32[]{:S(2)}) collective-permute-start(bf16[128,4096]{1,0:T(8,128)(2,1)S(1)} %get-tuple-element.15), channel_id=1, source_target_pairs={{0,1},{1,0},{2,3},{3,2},{4,5},{5,4},{6,7},{7,6},{8,9},{9,8},{10,11... | collective-permute-start | bytes 3145736 | tf_op jit(solution)/shard_map/ppermute | solution.py:282
  55.8 42.7 %copy-start.6 = (bf16[16,4096]{1,0:T(8,128)(2,1)S(1)}, bf16[16,4096]{1,0:T(8,128)(2,1)}, u32[]{:S(2)}) copy-start(bf16[16,4096]{1,0:T(8,128)(2,1)} %refs_4_.1) | copy-start | bytes 393220
  55.8 42.7 %copy-start.9 = (f32[4096]{0:T(1024)S(1)}, f32[4096]{0:T(1024)}, u32[]{:S(2)}) copy-start(f32[4096]{0:T(1024)} %param.15) | copy-start | bytes 49156
  55.8 18.4 %all-to-all-start.2 = ((bf16[4,16,4096]{2,1,0:T(8,128)(2,1)}), bf16[4,16,4096]{2,1,0:T(8,128)(2,1)}, u32[]{:S(2)}, u32[]{:S(2)}) async-start(bf16[4,16,4096]{2,1,0:T(8,128)(2,1)} %shard_map.102), calls=%async_computation.2 | async-start | bytes 1048576 | tf_op jit(solution)/shard_map/all_to_all | solution.py:289
  62.3 23.0 %collective-permute-start.2 = (bf16[16,4096]{1,0:T(8,128)(2,1)}, bf16[16,4096]{1,0:T(8,128)(2,1)S(1)}, u32[]{:S(2)}, u32[]{:S(2)}) collective-permute-start(bf16[16,4096]{1,0:T(8,128)(2,1)} %get-tuple-element.17), channel_id=1, source_target_pairs={{0,2},{1,3},{2,0},{3,1},{4,6},{5,7},{6,4},{7,5},{8,10},{9,11},{10,... | collective-permute-start | bytes 393224 | tf_op jit(solution)/shard_map/ppermute | solution.py:294
  65.6 19.7 %collective-permute-start.3 = (bf16[16,4096]{1,0:T(8,128)(2,1)}, bf16[16,4096]{1,0:T(8,128)(2,1)S(1)}, u32[]{:S(2)}, u32[]{:S(2)}) collective-permute-start(bf16[16,4096]{1,0:T(8,128)(2,1)} %get-tuple-element.18), channel_id=1, source_target_pairs={{0,4},{1,5},{2,6},{3,7},{4,0},{5,1},{6,2},{7,3},{8,12},{9,13},{10,... | collective-permute-start | bytes 393224 | tf_op jit(solution)/shard_map/ppermute | solution.py:294
  68.6 18.0 %collective-permute-start.4 = (bf16[16,4096]{1,0:T(8,128)(2,1)}, bf16[16,4096]{1,0:T(8,128)(2,1)S(1)}, u32[]{:S(2)}, u32[]{:S(2)}) collective-permute-start(bf16[16,4096]{1,0:T(8,128)(2,1)} %get-tuple-element.19), channel_id=1, source_target_pairs={{0,6},{1,7},{2,4},{3,5},{4,2},{5,3},{6,0},{7,1},{8,14},{9,15},{10,... | collective-permute-start | bytes 393224 | tf_op jit(solution)/shard_map/ppermute | solution.py:294
  75.3 23.1 %collective-permute-start.5 = (bf16[16,4096]{1,0:T(8,128)(2,1)S(1)}, bf16[16,4096]{1,0:T(8,128)(2,1)S(1)}, u32[]{:S(2)}, u32[]{:S(2)}) collective-permute-start(bf16[16,4096]{1,0:T(8,128)(2,1)S(1)} %shard_map.103), channel_id=1, source_target_pairs={{0,8},{1,9},{2,10},{3,11},{4,12},{5,13},{6,14},{7,15},{8,0},{9,1},... | collective-permute-start | bytes 393224 | tf_op jit(solution)/shard_map/ppermute | solution.py:298

commit v6 on v5

--- a/solution.py
+++ b/solution.py
@@ -19,6 +19,7 @@
 ROW_Y = [[g + 2 * k for k in range(4)] for g in range(SHARDS) if g & 6 == 0]
 ROW_X = [[g + 8 * k for k in range(4)] for g in range(8)]
 NEAR_CHIPS = [[8 * g + 2 * k + core for k in range(4)] for g in range(2) for core in range(2)]
+NEAR_ORDER = (0, 2, 1, 3)
 
 VMEM = pl.BlockSpec(memory_space=pltpu.VMEM)
 HBM = pl.BlockSpec(memory_space=pltpu.HBM)
@@ -179,7 +180,7 @@
         mixed_ref[:, cut] = (mixed * scale).astype(BF16)
     core, chip = place_ref[1] & 1, place_ref[1] >> 1
     for k in range(8):
-        start = (chip ^ (k & 3) if k & 4 else ((chip & 4) ^ 4) + k) * 32
+        start = (chip ^ NEAR_ORDER[k - 4] if k & 4 else ((chip & 4) ^ 4) + k) * 32
         cut = slice(k * 16, (k + 1) * 16)
         own, sibling = start + core * 16, start + (1 - core) * 16
         keep_ref[cut, :] = mixed_ref[pl.ds(pl.multiple_of(own, 16), 16), :]
@@ -204,10 +205,17 @@
         copy.wait()
 
 
-def near_kernel(keep_ref, got_ref, *out_refs):
-    for k, ref in enumerate(out_refs):
-        cut = slice(64 + k * 16, 80 + k * 16)
-        ref[...] = (keep_ref[cut, :] + got_ref[cut, :].astype(F32)).astype(ref.dtype)
+def near_kernel(keep_ref, got_ref, own_ref, next_ref, sent_ref):
+    def rows(start, stop):
+        return keep_ref[start:stop, :] + got_ref[start:stop, :].astype(F32)
+
+    sent_ref[...] = rows(96, 128).astype(BF16)
+    own_ref[...] = rows(64, 80)
+    next_ref[...] = rows(80, 96)
+
+
+def next_kernel(next_ref, got_ref, out_ref):
+    out_ref[...] = (next_ref[...] + got_ref[16:, :].astype(F32)).astype(BF16)
 
 
 def sum_kernel(parts_ref, out_ref):
@@ -217,11 +225,11 @@
     out_ref[...] = total.astype(BF16)
 
 
-def finish_kernel(own_ref, *refs):
-    *part_refs, residual_ref, gain_ref, hidden_ref, normed_ref = refs
-    hidden = residual_ref[...].astype(F32) + own_ref[...]
-    for ref in part_refs:
-        hidden = hidden + ref[...].astype(F32)
+def finish_kernel(
+    own_ref, first_ref, far_ref, second_ref, residual_ref, gain_ref, hidden_ref, normed_ref
+):
+    hidden = residual_ref[...].astype(F32) + own_ref[...] + first_ref[:16, :].astype(F32)
+    hidden = hidden + second_ref[...].astype(F32) + far_ref[...].astype(F32)
     scale = lax.rsqrt(jnp.mean(hidden * hidden, axis=1, keepdims=True) + 1e-05)
     hidden_ref[...] = hidden.astype(BF16)
     normed_ref[...] = (hidden * scale * gain_ref[...]).astype(BF16)
@@ -287,17 +295,18 @@
         scratch=[pltpu.VMEM((4, 16, D), BF16), pltpu.SemaphoreType.DMA((4,))], outs=HBM,
     )
     away = lax.all_to_all(away, "tp", 0, 0, axis_index_groups=NEAR_CHIPS)
-    own, *parts = call(
-        near_kernel, (of((16, D), F32), full, full, full), [VMEM, VMEM], keep, got
-    )
-    near = [
-        lax.ppermute(sent, "tp", [(i, i ^ (2 * k)) for i in range(16)])
-        for k, sent in enumerate(parts, 1)
-    ]
+    own, following, sent = call(
+        near_kernel, (of((16, D), F32), of((16, D), F32), of((32, D), BF16)), [VMEM, VMEM],
+        keep, got,
+    )
+    first = lax.ppermute(sent, "tp", [(i, i ^ 2) for i in range(16)])
     away = call(sum_kernel, full, [VMEM], away)
+    following = call(next_kernel, full, [VMEM, VMEM], following, first)
+    second = lax.ppermute(following, "tp", [(i, i ^ 4) for i in range(16)])
     far = lax.ppermute(away, "tp", [(i, i ^ 8) for i in range(16)])
     return call(
-        finish_kernel, (full, full), [VMEM] * 7, own, *near, far, residual_in, norm_gain[None, :]
+        finish_kernel, (full, full), [VMEM] * 6,
+        own, first, far, second, residual_in, norm_gain[None, :],
     )
 
 

time: 99.9 us -> 105 us (1.051)
  the two profiles are of different devices: /device:TPU:64 before, /device:TPU:2 now
where the time goes in v6:
time: 105 us; the launch traced here: 104 us
  starting transfers between devices  39.2 us (37%)
  waiting for transfers between devices  25.9 us (25%)
  blocking collectives  23 us (22%)
  Pallas kernels  11.2 us (11%)
  local copies, waits for them, and re-layouts  4.15 us (4%)
    ppermute x1, starting transfers between devices, shards(): other = lax.ppermute(local, 'seq', FLIP_Z)  15.7 us
    ppermute x1, waiting for transfers between devices, shards(): first = lax.ppermute(sent, 'tp', [(i, i ^ 2) for i in range(16)])  13.2 us
    all_to_all x1, blocking collectives, shards(): rows = lax.all_to_all(pairs, 'seq', 0, 0, axis_index_groups=ROW_Y)  12.1 us
    pallas_call x11, Pallas kernels, call(): pl.pallas_call(body, out_shape=shapes, in_specs=specs, out_specs=jax.tree...  11.2 us
    all_to_all x1, blocking collectives, shards(): cols = lax.all_to_all(totals, 'seq', 0, 0, axis_index_groups=ROW_X)  10.9 us
    ppermute x1, waiting for transfers between devices, shards(): far = lax.ppermute(away, 'tp', [(i, i ^ 8) for i in range(16)])  10.8 us
    ppermute x1, starting transfers between devices, shards(): far = lax.ppermute(away, 'tp', [(i, i ^ 8) for i in range(16)])  9.31 us
    ppermute x1, starting transfers between devices, shards(): first = lax.ppermute(sent, 'tp', [(i, i ^ 2) for i in range(16)])  4.43 us
  transfers between devices with their start and end apart: 6, of which 3 were waited for; matrix products, arithmetic and copies ran while one was open for 0% of the time, Pallas kernels for 3%

profile of v6, /device:TPU:2, one launch (start us, length us, event | category | flops | bytes accessed | tf_op | source)
XLA Modules:
  0.0 104.4 jit_solution(16021151985428786105)
XLA Ops:
  0.6 0.0 copy-start
  0.6 2.5 %shard_map.95.own_ref = bf16[392,128]{1,0:T(8,128)(2,1)} custom-call(s32[1,3]{1,0:T(1,128)} %starts_ref.3, f32[3,256]{1,0:T(4,128)} %decay_ref.3, bf16[256,384]{1,0:T(8,128)(2,1)} %key_ref.1, bf16[256,384]{1,0:T(8,128)(2,1)} %value_ref.1), custom_call_target="tpu_custom_call" | custom-call | tf_op jit(solution)/shard_map/pallas_call | solution.py:239
  3.2 15.7 %collective-permute-start = (bf16[392,128]{1,0:T(8,128)(2,1)}, bf16[392,128]{1,0:T(8,128)(2,1)}, u32[]{:S(2)}, u32[]{:S(2)}) collective-permute-start(bf16[392,128]{1,0:T(8,128)(2,1)} %shard_map.95.own_ref), channel_id=1, source_target_pairs={{0,16},{16,0},{32,48},{48,32},{64,80},{80,64},{96,112},{112,96},{1... | collective-permute-start | bytes 301064 | tf_op jit(solution)/shard_map/ppermute | solution.py:273
  18.9 0.0 copy-start.2
  18.9 0.9 copy-done.2
  19.8 0.0 copy-start.4
  19.8 0.9 copy-done.4
  20.8 0.0 copy-start.5
  20.8 0.9 copy-done.5
  21.7 0.0 copy-start.7
  21.7 0.7 copy-done.7
  22.4 0.0 copy-start.10
  22.4 0.7 copy-done.10
  23.0 0.0 copy-start.8
  23.0 0.0 copy-start.11
  23.0 1.4 %shard_map.96.intra_ref = f32[256,384]{1,0:T(8,128)S(1)} custom-call(s32[1,3]{1,0:T(1,128)S(1)} %copy-done.10, f32[3,256]{1,0:T(4,128)S(1)} %copy-done.7, bf16[256,384]{1,0:T(8,128)(2,1)S(1)} %copy-done.2, bf16[256,384]{1,0:T(8,128)(2,1)S(1)} %copy-done.4, bf16[256,384]{1,0:T(8,128)(2,1)S(1)} %copy-done.5), custom_call_target="tpu_custom_call" | custom-call | tf_op jit(solution)/shard_map/pallas_call | solution.py:239
  24.5 0.0 copy-start.3
  24.5 0.1 pad_add_fusion.place_ref
  24.5 0.0 collective-permute-done.other_ref
  24.6 1.0 shard_map.97
  25.6 12.1 %all_to_all.15.parts_ref.row_ref = bf16[4,392,128]{2,1,0:T(8,128)(2,1)S(1)} all-to-all(bf16[4,392,128]{2,1,0:T(8,128)(2,1)S(1)} %shard_map.97), channel_id=1, replica_groups={{0,32,64,96},{16,48,80,112},{128,160,192,224},{144,176,208,240},{256,28..., dimensions={0} | all-to-all | bytes 802816 | tf_op jit(solution)/shard_map/all_to_all | solution.py:281
  37.7 0.0 copy-start.1
  37.7 0.1 shard_map.98
  37.8 10.9 %all_to_all.16.col_ref = bf16[4,392,128]{2,1,0:T(8,128)(2,1)S(1)} all-to-all(bf16[4,392,128]{2,1,0:T(8,128)(2,1)S(1)} %shard_map.98), channel_id=1, replica_groups={{0,128,256,384},{16,144,272,400},{32,160,288,416},{48,176,304,432},{64,..., dimensions={0} | all-to-all | bytes 802816 | tf_op jit(solution)/shard_map/all_to_all | solution.py:283
  48.7 0.0 copy-done
  48.7 0.0 copy-done.8
  48.7 0.0 copy-done.11
  48.7 0.0 copy-done.3
  48.7 2.5 %shard_map.99 = (bf16[128,4096]{1,0:T(8,128)(2,1)S(1)}, bf16[128,384]{1,0:T(8,128)(2,1)S(1)}) custom-call(s32[2]{0:T(128)S(1)} %pad_add_fusion.place_ref, s32[1,3]{1,0:T(1,128)S(1)} %copy-done.11, f32[3,256]{1,0:T(4,128)S(1)} %copy-done.8, bf16[256,384]{1,0:T(8,128)(2,1)S(1)} %copy-done.3, f32[256,384]{1,0:T(8,128)S(1)} %shard_map.96.intra_ref, ...), custom_call_target="tpu_custom_call" | custom-call | tf_op jit(solution)/shard_map/pallas_call | solution.py:239
  51.2 1.9 %collective-permute-start.1 = (bf16[128,4096]{1,0:T(8,128)(2,1)S(1)}, bf16[128,4096]{1,0:T(8,128)(2,1)S(1)}, u32[]{:S(2)}, u32[]{:S(2)}) collective-permute-start(bf16[128,4096]{1,0:T(8,128)(2,1)S(1)} %get-tuple-element.14), channel_id=1, source_target_pairs={{0,1},{1,0},{2,3},{3,2},{4,5},{5,4},{6,7},{7,6},{8,9},{9,8},{10,11... | collective-permute-start | bytes 3145736 | tf_op jit(solution)/shard_map/ppermute | solution.py:290
  53.2 0.0 copy-done.1
  53.2 0.7 shard_map.100.keep_ref
  53.9 1.9 %collective-permute-done.1.got_ref = bf16[128,4096]{1,0:T(8,128)(2,1)S(1)} collective-permute-done((bf16[128,4096]{1,0:T(8,128)(2,1)S(1)}, bf16[128,4096]{1,0:T(8,128)(2,1)S(1)}, u32[]{:S(2)}, u32[]{:S(2)}) %collective-permute-start.1) | collective-permute-done | bytes 1048608 | tf_op jit(solution)/shard_map/ppermute | solution.py:290
  55.8 0.9 shard_map.102
  56.6 0.0 copy-start.6
  56.7 0.0 copy-start.9
  56.7 4.3 %all-to-all-start.2 = ((bf16[4,16,4096]{2,1,0:T(8,128)(2,1)}), bf16[4,16,4096]{2,1,0:T(8,128)(2,1)}, u32[]{:S(2)}, u32[]{:S(2)}) async-start(bf16[4,16,4096]{2,1,0:T(8,128)(2,1)} %shard_map.102), calls=%async_computation.2 | async-start | bytes 1048576 | tf_op jit(solution)/shard_map/all_to_all | solution.py:297
  61.0 0.1 shard_map.101
  61.1 4.4 %collective-permute-start.2 = (bf16[32,4096]{1,0:T(8,128)(2,1)S(1)}, bf16[32,4096]{1,0:T(8,128)(2,1)S(1)}, u32[]{:S(2)}, u32[]{:S(2)}) collective-permute-start(bf16[32,4096]{1,0:T(8,128)(2,1)S(1)} %get-tuple-element.16), channel_id=1, source_target_pairs={{0,2},{1,3},{2,0},{3,1},{4,6},{5,7},{6,4},{7,5},{8,10},{9,11},{10,... | collective-permute-start | bytes 786440 | tf_op jit(solution)/shard_map/ppermute | solution.py:302
  65.5 13.2 %collective-permute-done.2.got_ref.first_ref = bf16[32,4096]{1,0:T(8,128)(2,1)S(1)} collective-permute-done((bf16[32,4096]{1,0:T(8,128)(2,1)S(1)}, bf16[32,4096]{1,0:T(8,128)(2,1)S(1)}, u32[]{:S(2)}, u32[]{:S(2)}) %collective-permute-start.2) | collective-permute-done | bytes 262176 | tf_op jit(solution)/shard_map/ppermute | solution.py:302
  78.7 3.6 %collective-permute-start.4 = (bf16[16,4096]{1,0:T(8,128)(2,1)S(1)}, bf16[16,4096]{1,0:T(8,128)(2,1)S(1)}, u32[]{:S(2)}, u32[]{:S(2)}) collective-permute-start(bf16[16,4096]{1,0:T(8,128)(2,1)S(1)} %shard_map.104), channel_id=1, source_target_pairs={{0,4},{1,5},{2,6},{3,7},{4,0},{5,1},{6,2},{7,3},{8,12},{9,13},{10,... | collective-permute-start | bytes 393224 | tf_op jit(solution)/shard_map/ppermute | solution.py:305
  82.3 0.0 all-to-all-done.2.parts_ref
  82.3 1.1 %shard_map.103 = bf16[16,4096]{1,0:T(8,128)(2,1)S(1)} custom-call(bf16[4,16,4096]{2,1,0:T(8,128)(2,1)} %all-to-all-done.2.parts_ref), custom_call_target="tpu_custom_call" | custom-call | tf_op jit(solution)/shard_map/pallas_call | solution.py:239
  83.4 9.3 %collective-permute-start.3 = (bf16[16,4096]{1,0:T(8,128)(2,1)S(1)}, bf16[16,4096]{1,0:T(8,128)(2,1)S(1)}, u32[]{:S(2)}, u32[]{:S(2)}) collective-permute-start(bf16[16,4096]{1,0:T(8,128)(2,1)S(1)} %shard_map.103), channel_id=1, source_target_pairs={{0,8},{1,9},{2,10},{3,11},{4,12},{5,13},{6,14},{7,15},{8,0},{9,1},... | collective-permute-start | bytes 393224 | tf_op jit(solution)/shard_map/ppermute | solution.py:306
  92.7 0.0 collective-permute-done.4.second_ref
  92.7 10.8 %collective-permute-done.3.far_ref = bf16[16,4096]{1,0:T(8,128)(2,1)S(1)} collective-permute-done((bf16[16,4096]{1,0:T(8,128)(2,1)S(1)}, bf16[16,4096]{1,0:T(8,128)(2,1)S(1)}, u32[]{:S(2)}, u32[]{:S(2)}) %collective-permute-start.3) | collective-permute-done | bytes 131104 | tf_op jit(solution)/shard_map/ppermute | solution.py:306
  103.6 0.0 copy-done.6
  103.6 0.0 copy-done.9
  103.6 0.8 shard_map.105
  (1 shorter events, 0.0 us)
Async XLA Ops:
  0.6 48.1 %copy-start = (bf16[384,4096]{1,0:T(8,128)(2,1)S(1)}, bf16[384,4096]{1,0:T(8,128)(2,1)}, u32[]{:S(2)}) copy-start(bf16[384,4096]{1,0:T(8,128)(2,1)} %weight_ref.3) | copy-start | bytes 9437188
  3.2 21.4 %collective-permute-start = (bf16[392,128]{1,0:T(8,128)(2,1)}, bf16[392,128]{1,0:T(8,128)(2,1)}, u32[]{:S(2)}, u32[]{:S(2)}) collective-permute-start(bf16[392,128]{1,0:T(8,128)(2,1)} %shard_map.95.own_ref), channel_id=1, source_target_pairs={{0,16},{16,0},{32,48},{48,32},{64,80},{80,64},{96,112},{112,96},{1... | collective-permute-start | bytes 301064 | tf_op jit(solution)/shard_map/ppermute | solution.py:273
  18.9 0.9 copy-start.2
  19.8 0.9 copy-start.4
  20.8 0.9 copy-start.5
  21.7 0.7 copy-start.7
  22.4 0.7 copy-start.10
  23.0 25.7 %copy-start.8 = (f32[3,256]{1,0:T(4,128)S(1)}, f32[3,256]{1,0:T(4,128)}, u32[]{:S(2)}) copy-start(f32[3,256]{1,0:T(4,128)} %decay_ref.3) | copy-start | bytes 9220
  23.0 25.7 %copy-start.11 = (s32[1,3]{1,0:T(1,128)S(1)}, s32[1,3]{1,0:T(1,128)}, u32[]{:S(2)}) copy-start(s32[1,3]{1,0:T(1,128)} %starts_ref.3) | copy-start | bytes 40
  24.5 24.2 %copy-start.3 = (bf16[256,384]{1,0:T(8,128)(2,1)S(1)}, bf16[256,384]{1,0:T(8,128)(2,1)}, u32[]{:S(2)}) copy-start(bf16[256,384]{1,0:T(8,128)(2,1)} %query_ref.2) | copy-start | bytes 589828
  37.7 15.4 %copy-start.1 = (bf16[384,4096]{1,0:T(8,128)(2,1)S(1)}, bf16[384,4096]{1,0:T(8,128)(2,1)}, u32[]{:S(2)}) copy-start(bf16[384,4096]{1,0:T(8,128)(2,1)} %weight_ref.3) | copy-start | bytes 9437188
  51.2 4.6 %collective-permute-start.1 = (bf16[128,4096]{1,0:T(8,128)(2,1)S(1)}, bf16[128,4096]{1,0:T(8,128)(2,1)S(1)}, u32[]{:S(2)}, u32[]{:S(2)}) collective-permute-start(bf16[128,4096]{1,0:T(8,128)(2,1)S(1)} %get-tuple-element.14), channel_id=1, source_target_pairs={{0,1},{1,0},{2,3},{3,2},{4,5},{5,4},{6,7},{7,6},{8,9},{9,8},{10,11... | collective-permute-start | bytes 3145736 | tf_op jit(solution)/shard_map/ppermute | solution.py:290
  56.6 46.9 %copy-start.6 = (bf16[16,4096]{1,0:T(8,128)(2,1)S(1)}, bf16[16,4096]{1,0:T(8,128)(2,1)}, u32[]{:S(2)}) copy-start(bf16[16,4096]{1,0:T(8,128)(2,1)} %residual_ref.1) | copy-start | bytes 393220
  56.7 46.9 %copy-start.9 = (f32[4096]{0:T(1024)S(1)}, f32[4096]{0:T(1024)}, u32[]{:S(2)}) copy-start(f32[4096]{0:T(1024)} %param.15) | copy-start | bytes 49156
  56.7 25.6 %all-to-all-start.2 = ((bf16[4,16,4096]{2,1,0:T(8,128)(2,1)}), bf16[4,16,4096]{2,1,0:T(8,128)(2,1)}, u32[]{:S(2)}, u32[]{:S(2)}) async-start(bf16[4,16,4096]{2,1,0:T(8,128)(2,1)} %shard_map.102), calls=%async_computation.2 | async-start | bytes 1048576 | tf_op jit(solution)/shard_map/all_to_all | solution.py:297
  61.1 17.6 %collective-permute-start.2 = (bf16[32,4096]{1,0:T(8,128)(2,1)S(1)}, bf16[32,4096]{1,0:T(8,128)(2,1)S(1)}, u32[]{:S(2)}, u32[]{:S(2)}) collective-permute-start(bf16[32,4096]{1,0:T(8,128)(2,1)S(1)} %get-tuple-element.16), channel_id=1, source_target_pairs={{0,2},{1,3},{2,0},{3,1},{4,6},{5,7},{6,4},{7,5},{8,10},{9,11},{10,... | collective-permute-start | bytes 786440 | tf_op jit(solution)/shard_map/ppermute | solution.py:302
  78.7 14.0 %collective-permute-start.4 = (bf16[16,4096]{1,0:T(8,128)(2,1)S(1)}, bf16[16,4096]{1,0:T(8,128)(2,1)S(1)}, u32[]{:S(2)}, u32[]{:S(2)}) collective-permute-start(bf16[16,4096]{1,0:T(8,128)(2,1)S(1)} %shard_map.104), channel_id=1, source_target_pairs={{0,4},{1,5},{2,6},{3,7},{4,0},{5,1},{6,2},{7,3},{8,12},{9,13},{10,... | collective-permute-start | bytes 393224 | tf_op jit(solution)/shard_map/ppermute | solution.py:305
  83.4 20.1 %collective-permute-start.3 = (bf16[16,4096]{1,0:T(8,128)(2,1)S(1)}, bf16[16,4096]{1,0:T(8,128)(2,1)S(1)}, u32[]{:S(2)}, u32[]{:S(2)}) collective-permute-start(bf16[16,4096]{1,0:T(8,128)(2,1)S(1)} %shard_map.103), channel_id=1, source_target_pairs={{0,8},{1,9},{2,10},{3,11},{4,12},{5,13},{6,14},{7,15},{8,0},{9,1},... | collective-permute-start | bytes 393224 | tf_op jit(solution)/shard_map/ppermute | solution.py:306

commit v7 on v5

--- a/solution.py
+++ b/solution.py
@@ -80,7 +80,12 @@
         ).astype(BF16)
 
 
-def intra_kernel(starts_ref, decay_ref, query_ref, key_ref, value_ref, out_ref):
+def intra_kernel(
+    starts_ref, decay_ref, query_ref, key_ref, value_ref, weight_hbm,
+    out_ref, carry_ref, weight_ref, sem,
+):
+    copy = pltpu.make_async_copy(weight_hbm, weight_ref, sem)
+    copy.start()
     row, col = grid_iotas()
     lower = row >= col
     lower_f = lower.astype(F32)
@@ -90,6 +95,7 @@
     seg_col = segment_of(starts_ref, lax.broadcasted_iota(jnp.int32, (SPAN, 1), 0))
     seg_row = segment_of(starts_ref, lax.broadcasted_iota(jnp.int32, (1, SPAN), 1))
     same = lower & (seg_col == seg_row)
+    carry_ref[...] = jnp.exp(cum_col) * (seg_col == 0).astype(F32)
     for h in range(HEADS):
         cut = slice(h * HDIM, (h + 1) * HDIM)
         spread = cum_col[:, h : h + 1] - cum_row[h : h + 1, :]
@@ -99,6 +105,7 @@
         )
         weights = (scores * decay_mat).astype(BF16)
         out_ref[:, cut] = jnp.dot(weights, value_ref[:, cut], preferred_element_type=F32)
+    copy.wait()
 
 
 def decays(rows):
@@ -155,15 +162,11 @@
 
 
 def attend_kernel(
-    place_ref, starts_ref, decay_ref, query_ref, intra_ref, other_ref, row_ref, col_ref,
-    weight_ref, send_ref, keep_ref, mixed_ref, sibling_ref,
+    place_ref, query_ref, intra_ref, carry_ref, other_ref, row_ref, col_ref, weight_ref,
+    send_ref, keep_ref, mixed_ref, sibling_ref,
 ):
     odd = place_ref[0] & 1 == 1
-    row, col = grid_iotas()
-    lower_f = (row >= col).astype(F32)
-    cumulative = running_sums(lower_f, decay_ref[...], True)
-    segment = segment_of(starts_ref, lax.broadcasted_iota(jnp.int32, (SPAN, 1), 0))
-    carry = jnp.exp(cumulative) * (segment == 0).astype(F32)
+    carry = carry_ref[...]
     row_scale = [decays(row_ref[k, STATE:, :]) for k in range(3)]
     col_scale = [decays(col_ref[k, STATE:, :]) for k in range(3)]
     other_a = decays(other_ref[STATE:, :])
@@ -217,11 +220,13 @@
     out_ref[...] = total.astype(BF16)
 
 
-def finish_kernel(own_ref, *refs):
-    *part_refs, residual_ref, gain_ref, hidden_ref, normed_ref = refs
-    hidden = residual_ref[...].astype(F32) + own_ref[...]
-    for ref in part_refs:
-        hidden = hidden + ref[...].astype(F32)
+def fold_kernel(own_ref, a_ref, b_ref, c_ref, residual_ref, out_ref):
+    total = residual_ref[...].astype(F32) + own_ref[...]
+    out_ref[...] = total + a_ref[...].astype(F32) + b_ref[...].astype(F32) + c_ref[...].astype(F32)
+
+
+def finish_kernel(near_ref, far_ref, gain_ref, hidden_ref, normed_ref):
+    hidden = near_ref[...] + far_ref[...].astype(F32)
     scale = lax.rsqrt(jnp.mean(hidden * hidden, axis=1, keepdims=True) + 1e-05)
     hidden_ref[...] = hidden.astype(BF16)
     normed_ref[...] = (hidden * scale * gain_ref[...]).astype(BF16)
@@ -248,7 +253,7 @@
     place = jnp.stack([lax.axis_index("seq"), lax.axis_index("tp")]).astype(jnp.int32)
 
     local = call(
-        state_kernel, of((PAYLOAD, HDIM), BF16), [HBM] * 4,
+        state_kernel, pltpu.VMEM((PAYLOAD, HDIM), BF16), [HBM] * 4,
         *(
             pltpu.with_memory_space_constraint(a, pltpu.HBM)
             for a in (doc_starts, log_decay, key_rows, value_rows)
@@ -263,11 +268,15 @@
     )
     late_query = lax.optimization_barrier((local, query_rows))[1]
     other = lax.ppermute(local, "seq", FLIP_Z)
-    intra = call(
-        intra_kernel, of((SPAN, STATE), F32), [SMEM, VMEM, VMEM, VMEM, VMEM],
+    intra, carry, weight = call(
+        intra_kernel,
+        (of((SPAN, STATE), F32), of((SPAN, HEADS), F32), pltpu.VMEM((STATE, D), BF16)),
+        [SMEM, VMEM, VMEM, VMEM, VMEM, HBM],
         doc_starts, log_decay, late_query, key_rows, value_rows,
-    )
-    other, intra = lax.optimization_barrier((other, intra))
+        pltpu.with_memory_space_constraint(out_weight, pltpu.HBM),
+        scratch=[pltpu.SemaphoreType.DMA],
+    )
+    other, intra, carry = lax.optimization_barrier((other, intra, carry))
     four = of((4, PAYLOAD, HDIM), BF16)
     pairs = call(pair_kernel, four, [SMEM, VMEM, VMEM], place, local, other)
     rows = lax.all_to_all(pairs, "seq", 0, 0, axis_index_groups=ROW_Y)
@@ -275,12 +284,12 @@
     cols = lax.all_to_all(totals, "seq", 0, 0, axis_index_groups=ROW_X)
     send, keep = call(
         attend_kernel, (of((SPAN // 2, D), BF16), of((SPAN // 2, STATE), BF16)),
-        [SMEM, SMEM] + [VMEM] * 7,
-        place, doc_starts, log_decay, query_rows, intra, other, rows, cols, out_weight,
+        [SMEM] + [VMEM] * 7,
+        place, query_rows, intra, carry, other, rows, cols, weight,
         scratch=[pltpu.VMEM((SPAN, STATE), BF16), pltpu.VMEM((SPAN // 2, STATE), BF16)],
     )
     got = lax.ppermute(send, "tp", [(i, i ^ 1) for i in range(16)])
-    keep = call(keep_kernel, of((SPAN // 2, D), F32), [VMEM, VMEM], keep, out_weight)
+    keep = call(keep_kernel, of((SPAN // 2, D), F32), [VMEM, VMEM], keep, weight)
     full = of((16, D), BF16)
     away = call(
         far_kernel, pltpu.HBM((4, 16, D), BF16), [VMEM, VMEM], keep, got,
@@ -296,9 +305,8 @@
     ]
     away = call(sum_kernel, full, [VMEM], away)
     far = lax.ppermute(away, "tp", [(i, i ^ 8) for i in range(16)])
-    return call(
-        finish_kernel, (full, full), [VMEM] * 7, own, *near, far, residual_in, norm_gain[None, :]
-    )
+    folded = call(fold_kernel, of((16, D), F32), [VMEM] * 5, own, *near, residual_in)
+    return call(finish_kernel, (full, full), [VMEM] * 3, folded, far, norm_gain[None, :])
 
 
 def solution(mesh):

time: 99.9 us -> 97.2 us (0.973)
  starting transfers between devices: 40.7 us -> 39.4 us
    ppermute x1, waiting for transfers between devices: 11.8 us -> 8.26 us  [shards(): far = lax.ppermute(away, 'tp', [(i, i ^ 8) for i in range(16)])]
    ppermute x3, waiting for transfers between devices: 1.39 us -> 4.78 us  [shards(): lax.ppermute(sent, 'tp', [(i, i ^ 2 * k) for i in range(16)])]
    ppermute x1, starting transfers between devices: 9.97 us -> 8.65 us  [shards(): far = lax.ppermute(away, 'tp', [(i, i ^ 8) for i in range(16)])]
    pallas_call x10 -> x11, Pallas kernels: 11.9 us -> 11 us  [call(): pl.pallas_call(body, out_shape=shapes, in_specs=specs, out_specs=jax.tree...]
    unnamed x24 -> x16, local copies, waits for them, and re-layouts: 4.15 us -> 4.13 us
  transfers between devices with their start and end apart: 7 -> 7, of which waited for: 4 -> 4; matrix products, arithmetic and copies ran while one was open for 0% -> 0% of each run, Pallas kernels for 4% -> 5%
where the time goes in v7:
time: 97.2 us; the launch traced here: 96.6 us
  starting transfers between devices  39.4 us (41%)
  blocking collectives  23.7 us (24%)
  waiting for transfers between devices  17.6 us (18%)
  Pallas kernels  11 us (11%)
  local copies, waits for them, and re-layouts  4.13 us (4%)
    ppermute x1, starting transfers between devices, shards(): other = lax.ppermute(local, 'seq', FLIP_Z)  13.9 us
    all_to_all x1, blocking collectives, shards(): rows = lax.all_to_all(pairs, 'seq', 0, 0, axis_index_groups=ROW_Y)  12.1 us
    all_to_all x1, blocking collectives, shards(): cols = lax.all_to_all(totals, 'seq', 0, 0, axis_index_groups=ROW_X)  11.5 us
    pallas_call x11, Pallas kernels, call(): pl.pallas_call(body, out_shape=shapes, in_specs=specs, out_specs=jax.tree...  11 us
    ppermute x3, starting transfers between devices, shards(): lax.ppermute(sent, 'tp', [(i, i ^ 2 * k) for i in range(16)])  9.2 us
    ppermute x1, starting transfers between devices, shards(): far = lax.ppermute(away, 'tp', [(i, i ^ 8) for i in range(16)])  8.65 us
    ppermute x1, waiting for transfers between devices, shards(): far = lax.ppermute(away, 'tp', [(i, i ^ 8) for i in range(16)])  8.26 us
    all_to_all x1, starting transfers between devices, shards(): away = lax.all_to_all(away, 'tp', 0, 0, axis_index_groups=NEAR_CHIPS)  5.71 us
  transfers between devices with their start and end apart: 7, of which 4 were waited for; matrix products, arithmetic and copies ran while one was open for 0% of the time, Pallas kernels for 5%

profile of v7, /device:TPU:64, one launch (start us, length us, event | category | flops | bytes accessed | tf_op | source)
XLA Modules:
  0.0 96.6 jit_solution(16377278297175168766)
XLA Ops:
  0.6 1.7 %shard_map.95.own_ref = bf16[392,128]{1,0:T(8,128)(2,1)S(1)} custom-call(s32[1,3]{1,0:T(1,128)} %starts_ref.1, f32[3,256]{1,0:T(4,128)} %decay_ref.1, bf16[256,384]{1,0:T(8,128)(2,1)} %key_ref.1, bf16[256,384]{1,0:T(8,128)(2,1)} %value_ref.1), custom_call_target="tpu_custom_call" | custom-call | tf_op jit(solution)/shard_map/pallas_call | solution.py:236
  2.4 13.9 %collective-permute-start = (bf16[392,128]{1,0:T(8,128)(2,1)S(1)}, bf16[392,128]{1,0:T(8,128)(2,1)S(1)}, u32[]{:S(2)}, u32[]{:S(2)}) collective-permute-start(bf16[392,128]{1,0:T(8,128)(2,1)S(1)} %shard_map.95.own_ref), channel_id=1, source_target_pairs={{0,16},{16,0},{32,48},{48,32},{64,80},{80,64},{96,112},{112,96},{1... | collective-permute-start | bytes 301064 | tf_op jit(solution)/shard_map/ppermute | solution.py:270
  16.3 0.0 copy-start
  16.3 0.9 copy-done
  17.2 0.0 copy-start.2
  17.2 0.9 copy-done.2
  18.2 0.0 copy-start.3
  18.2 0.9 copy-done.3
  19.1 0.0 copy-start.5
  19.1 0.7 copy-done.5
  19.8 0.0 copy-start.7
  19.8 0.7 copy-done.7
  20.4 0.0 copy-start.1
  20.4 2.4 %shard_map.96 = (f32[256,384]{1,0:T(8,128)S(1)}, f32[256,3]{1,0:T(8,128)S(1)}, bf16[384,4096]{1,0:T(8,128)(2,1)S(1)}) custom-call(s32[1,3]{1,0:T(1,128)S(1)} %copy-done.7, f32[3,256]{1,0:T(4,128)S(1)} %copy-done.5, bf16[256,384]{1,0:T(8,128)(2,1)S(1)} %copy-done, bf16[256,384]{1,0:T(8,128)(2,1)S(1)} %copy-done.2, bf16[256,384]{1,0:T(8,128)(2,1)S(1)} %copy-done.3, ...), custom_call_target="tpu_custom_call" | custom-call | tf_op jit(solution)/shard_map/pallas_call | solution.py:236
  22.9 0.1 pad_add_fusion.place_ref
  23.0 0.0 collective-permute-done.other_ref
  23.0 0.6 shard_map.97
  23.6 12.1 %all_to_all.15.parts_ref.row_ref = bf16[4,392,128]{2,1,0:T(8,128)(2,1)S(1)} all-to-all(bf16[4,392,128]{2,1,0:T(8,128)(2,1)S(1)} %shard_map.97), channel_id=1, replica_groups={{0,32,64,96},{16,48,80,112},{128,160,192,224},{144,176,208,240},{256,28..., dimensions={0} | all-to-all | bytes 802816 | tf_op jit(solution)/shard_map/all_to_all | solution.py:282
  35.7 0.1 shard_map.98
  35.8 11.5 %all_to_all.16.col_ref = bf16[4,392,128]{2,1,0:T(8,128)(2,1)S(1)} all-to-all(bf16[4,392,128]{2,1,0:T(8,128)(2,1)S(1)} %shard_map.98), channel_id=1, replica_groups={{0,128,256,384},{16,144,272,400},{32,160,288,416},{48,176,304,432},{64,..., dimensions={0} | all-to-all | bytes 802816 | tf_op jit(solution)/shard_map/all_to_all | solution.py:284
  47.3 0.0 copy-done.1
  47.3 1.7 %shard_map.99 = (bf16[128,4096]{1,0:T(8,128)(2,1)S(1)}, bf16[128,384]{1,0:T(8,128)(2,1)S(1)}) custom-call(s32[2]{0:T(128)S(1)} %pad_add_fusion.place_ref, bf16[256,384]{1,0:T(8,128)(2,1)S(1)} %copy-done.1, f32[256,384]{1,0:T(8,128)S(1)} %get-tuple-element.18.intra_ref, f32[256,3]{1,0:T(8,128)S(1)} %get-tuple-element.19.carry_ref, ...), custom_call_target="tpu_custom_call" | custom-call | tf_op jit(solution)/shard_map/pallas_call | solution.py:236
  49.0 1.9 %collective-permute-start.1 = (bf16[128,4096]{1,0:T(8,128)(2,1)S(1)}, bf16[128,4096]{1,0:T(8,128)(2,1)S(1)}, u32[]{:S(2)}, u32[]{:S(2)}) collective-permute-start(bf16[128,4096]{1,0:T(8,128)(2,1)S(1)} %get-tuple-element.23), channel_id=1, source_target_pairs={{0,1},{1,0},{2,3},{3,2},{4,5},{5,4},{6,7},{7,6},{8,9},{9,8},{10,11... | collective-permute-start | bytes 3145736 | tf_op jit(solution)/shard_map/ppermute | solution.py:291
  51.0 0.7 shard_map.100.keep_ref
  51.7 1.9 %collective-permute-done.1.got_ref = bf16[128,4096]{1,0:T(8,128)(2,1)S(1)} collective-permute-done((bf16[128,4096]{1,0:T(8,128)(2,1)S(1)}, bf16[128,4096]{1,0:T(8,128)(2,1)S(1)}, u32[]{:S(2)}, u32[]{:S(2)}) %collective-permute-start.1) | collective-permute-done | bytes 1048608 | tf_op jit(solution)/shard_map/ppermute | solution.py:291
  53.6 0.9 shard_map.103
  54.5 0.0 copy-start.4
  54.5 0.0 copy-start.6
  54.5 5.7 %all-to-all-start.2 = ((bf16[4,16,4096]{2,1,0:T(8,128)(2,1)}), bf16[4,16,4096]{2,1,0:T(8,128)(2,1)}, u32[]{:S(2)}, u32[]{:S(2)}) async-start(bf16[4,16,4096]{2,1,0:T(8,128)(2,1)} %shard_map.103), calls=%async_computation.2 | async-start | bytes 1048576 | tf_op jit(solution)/shard_map/all_to_all | solution.py:298
  60.2 0.8 shard_map.101
  61.0 3.4 %collective-permute-start.2 = (bf16[16,4096]{1,0:T(8,128)(2,1)}, bf16[16,4096]{1,0:T(8,128)(2,1)S(1)}, u32[]{:S(2)}, u32[]{:S(2)}) collective-permute-start(bf16[16,4096]{1,0:T(8,128)(2,1)} %get-tuple-element.25), channel_id=1, source_target_pairs={{0,2},{1,3},{2,0},{3,1},{4,6},{5,7},{6,4},{7,5},{8,10},{9,11},{10,... | collective-permute-start | bytes 393224 | tf_op jit(solution)/shard_map/ppermute | solution.py:303
  64.4 2.5 %collective-permute-start.3 = (bf16[16,4096]{1,0:T(8,128)(2,1)}, bf16[16,4096]{1,0:T(8,128)(2,1)S(1)}, u32[]{:S(2)}, u32[]{:S(2)}) collective-permute-start(bf16[16,4096]{1,0:T(8,128)(2,1)} %get-tuple-element.26), channel_id=1, source_target_pairs={{0,4},{1,5},{2,6},{3,7},{4,0},{5,1},{6,2},{7,3},{8,12},{9,13},{10,... | collective-permute-start | bytes 393224 | tf_op jit(solution)/shard_map/ppermute | solution.py:303
  66.9 3.4 %collective-permute-start.4 = (bf16[16,4096]{1,0:T(8,128)(2,1)}, bf16[16,4096]{1,0:T(8,128)(2,1)S(1)}, u32[]{:S(2)}, u32[]{:S(2)}) collective-permute-start(bf16[16,4096]{1,0:T(8,128)(2,1)} %get-tuple-element.27), channel_id=1, source_target_pairs={{0,6},{1,7},{2,4},{3,5},{4,2},{5,3},{6,0},{7,1},{8,14},{9,15},{10,... | collective-permute-start | bytes 393224 | tf_op jit(solution)/shard_map/ppermute | solution.py:303
  70.2 2.7 %all-to-all-done.2.parts_ref = bf16[4,16,4096]{2,1,0:T(8,128)(2,1)} async-done(((bf16[4,16,4096]{2,1,0:T(8,128)(2,1)}), bf16[4,16,4096]{2,1,0:T(8,128)(2,1)}, u32[]{:S(2)}, u32[]{:S(2)}) %all-to-all-start.2) | async-done | bytes 524320 | tf_op jit(solution)/shard_map/all_to_all | solution.py:298
  72.9 1.1 %shard_map.104 = bf16[16,4096]{1,0:T(8,128)(2,1)S(1)} custom-call(bf16[4,16,4096]{2,1,0:T(8,128)(2,1)} %all-to-all-done.2.parts_ref), custom_call_target="tpu_custom_call" | custom-call | tf_op jit(solution)/shard_map/pallas_call | solution.py:236
  74.0 8.7 %collective-permute-start.5 = (bf16[16,4096]{1,0:T(8,128)(2,1)S(1)}, bf16[16,4096]{1,0:T(8,128)(2,1)S(1)}, u32[]{:S(2)}, u32[]{:S(2)}) collective-permute-start(bf16[16,4096]{1,0:T(8,128)(2,1)S(1)} %shard_map.104), channel_id=1, source_target_pairs={{0,8},{1,9},{2,10},{3,11},{4,12},{5,13},{6,14},{7,15},{8,0},{9,1},... | collective-permute-start | bytes 393224 | tf_op jit(solution)/shard_map/ppermute | solution.py:307
  82.7 0.0 collective-permute-done.2.a_ref
  82.7 0.0 collective-permute-done.3.b_ref
  82.7 4.8 %collective-permute-done.4.c_ref = bf16[16,4096]{1,0:T(8,128)(2,1)S(1)} collective-permute-done((bf16[16,4096]{1,0:T(8,128)(2,1)}, bf16[16,4096]{1,0:T(8,128)(2,1)S(1)}, u32[]{:S(2)}, u32[]{:S(2)}) %collective-permute-start.4) | collective-permute-done | bytes 131104 | tf_op jit(solution)/shard_map/ppermute | solution.py:303
  87.5 0.0 copy-done.4
  87.5 0.1 shard_map.102.near_ref
  87.6 8.3 %collective-permute-done.5.far_ref = bf16[16,4096]{1,0:T(8,128)(2,1)S(1)} collective-permute-done((bf16[16,4096]{1,0:T(8,128)(2,1)S(1)}, bf16[16,4096]{1,0:T(8,128)(2,1)S(1)}, u32[]{:S(2)}, u32[]{:S(2)}) %collective-permute-start.5) | collective-permute-done | bytes 131104 | tf_op jit(solution)/shard_map/ppermute | solution.py:307
  95.8 0.0 copy-done.6
  95.8 0.8 shard_map.105
Async XLA Ops:
  2.4 20.6 %collective-permute-start = (bf16[392,128]{1,0:T(8,128)(2,1)S(1)}, bf16[392,128]{1,0:T(8,128)(2,1)S(1)}, u32[]{:S(2)}, u32[]{:S(2)}) collective-permute-start(bf16[392,128]{1,0:T(8,128)(2,1)S(1)} %shard_map.95.own_ref), channel_id=1, source_target_pairs={{0,16},{16,0},{32,48},{48,32},{64,80},{80,64},{96,112},{112,96},{1... | collective-permute-start | bytes 301064 | tf_op jit(solution)/shard_map/ppermute | solution.py:270
  16.3 0.9 copy-start
  17.2 0.9 copy-start.2
  18.2 0.9 copy-start.3
  19.1 0.7 copy-start.5
  19.8 0.7 copy-start.7
  20.4 26.9 %copy-start.1 = (bf16[256,384]{1,0:T(8,128)(2,1)S(1)}, bf16[256,384]{1,0:T(8,128)(2,1)}, u32[]{:S(2)}) copy-start(bf16[256,384]{1,0:T(8,128)(2,1)} %query_ref.2) | copy-start | bytes 589828
  49.0 4.6 %collective-permute-start.1 = (bf16[128,4096]{1,0:T(8,128)(2,1)S(1)}, bf16[128,4096]{1,0:T(8,128)(2,1)S(1)}, u32[]{:S(2)}, u32[]{:S(2)}) collective-permute-start(bf16[128,4096]{1,0:T(8,128)(2,1)S(1)} %get-tuple-element.23), channel_id=1, source_target_pairs={{0,1},{1,0},{2,3},{3,2},{4,5},{5,4},{6,7},{7,6},{8,9},{9,8},{10,11... | collective-permute-start | bytes 3145736 | tf_op jit(solution)/shard_map/ppermute | solution.py:291
  54.5 33.0 %copy-start.4 = (bf16[16,4096]{1,0:T(8,128)(2,1)S(1)}, bf16[16,4096]{1,0:T(8,128)(2,1)}, u32[]{:S(2)}) copy-start(bf16[16,4096]{1,0:T(8,128)(2,1)} %residual_ref.1) | copy-start | bytes 393220
  54.5 41.4 %copy-start.6 = (f32[4096]{0:T(1024)S(1)}, f32[4096]{0:T(1024)}, u32[]{:S(2)}) copy-start(f32[4096]{0:T(1024)} %param.15) | copy-start | bytes 49156
  54.5 18.4 %all-to-all-start.2 = ((bf16[4,16,4096]{2,1,0:T(8,128)(2,1)}), bf16[4,16,4096]{2,1,0:T(8,128)(2,1)}, u32[]{:S(2)}, u32[]{:S(2)}) async-start(bf16[4,16,4096]{2,1,0:T(8,128)(2,1)} %shard_map.103), calls=%async_computation.2 | async-start | bytes 1048576 | tf_op jit(solution)/shard_map/all_to_all | solution.py:298
  61.0 21.7 %collective-permute-start.2 = (bf16[16,4096]{1,0:T(8,128)(2,1)}, bf16[16,4096]{1,0:T(8,128)(2,1)S(1)}, u32[]{:S(2)}, u32[]{:S(2)}) collective-permute-start(bf16[16,4096]{1,0:T(8,128)(2,1)} %get-tuple-element.25), channel_id=1, source_target_pairs={{0,2},{1,3},{2,0},{3,1},{4,6},{5,7},{6,4},{7,5},{8,10},{9,11},{10,... | collective-permute-start | bytes 393224 | tf_op jit(solution)/shard_map/ppermute | solution.py:303
  64.4 18.3 %collective-permute-start.3 = (bf16[16,4096]{1,0:T(8,128)(2,1)}, bf16[16,4096]{1,0:T(8,128)(2,1)S(1)}, u32[]{:S(2)}, u32[]{:S(2)}) collective-permute-start(bf16[16,4096]{1,0:T(8,128)(2,1)} %get-tuple-element.26), channel_id=1, source_target_pairs={{0,4},{1,5},{2,6},{3,7},{4,0},{5,1},{6,2},{7,3},{8,12},{9,13},{10,... | collective-permute-start | bytes 393224 | tf_op jit(solution)/shard_map/ppermute | solution.py:303
  66.9 20.6 %collective-permute-start.4 = (bf16[16,4096]{1,0:T(8,128)(2,1)}, bf16[16,4096]{1,0:T(8,128)(2,1)S(1)}, u32[]{:S(2)}, u32[]{:S(2)}) collective-permute-start(bf16[16,4096]{1,0:T(8,128)(2,1)} %get-tuple-element.27), channel_id=1, source_target_pairs={{0,6},{1,7},{2,4},{3,5},{4,2},{5,3},{6,0},{7,1},{8,14},{9,15},{10,... | collective-permute-start | bytes 393224 | tf_op jit(solution)/shard_map/ppermute | solution.py:303
  74.0 21.8 %collective-permute-start.5 = (bf16[16,4096]{1,0:T(8,128)(2,1)S(1)}, bf16[16,4096]{1,0:T(8,128)(2,1)S(1)}, u32[]{:S(2)}, u32[]{:S(2)}) collective-permute-start(bf16[16,4096]{1,0:T(8,128)(2,1)S(1)} %shard_map.104), channel_id=1, source_target_pairs={{0,8},{1,9},{2,10},{3,11},{4,12},{5,13},{6,14},{7,15},{8,0},{9,1},... | collective-permute-start | bytes 393224 | tf_op jit(solution)/shard_map/ppermute | solution.py:307

commit v8 on v7

--- a/solution.py
+++ b/solution.py
@@ -18,6 +18,7 @@
 FLIP_Z = [(i, i ^ 1) for i in range(SHARDS)]
 ROW_Y = [[g + 2 * k for k in range(4)] for g in range(SHARDS) if g & 6 == 0]
 ROW_X = [[g + 8 * k for k in range(4)] for g in range(8)]
+LONG = pl.CostEstimate(flops=10**11, bytes_accessed=0, transcendentals=0)
 NEAR_CHIPS = [[8 * g + 2 * k + core for k in range(4)] for g in range(2) for core in range(2)]
 
 VMEM = pl.BlockSpec(memory_space=pltpu.VMEM)
@@ -182,7 +183,7 @@
         mixed_ref[:, cut] = (mixed * scale).astype(BF16)
     core, chip = place_ref[1] & 1, place_ref[1] >> 1
     for k in range(8):
-        start = (chip ^ (k & 3) if k & 4 else ((chip & 4) ^ 4) + k) * 32
+        start = ((chip & 4) + (k & 3) if k & 4 else chip ^ 4 ^ k) * 32
         cut = slice(k * 16, (k + 1) * 16)
         own, sibling = start + core * 16, start + (1 - core) * 16
         keep_ref[cut, :] = mixed_ref[pl.ds(pl.multiple_of(own, 16), 16), :]
@@ -196,10 +197,16 @@
     out_ref[...] = jnp.dot(own_ref[...], weight_ref[...], preferred_element_type=F32)
 
 
-def far_kernel(keep_ref, got_ref, out_ref, sum_ref, sems):
+def far_kernel(keep_ref, got_ref, *out_refs):
+    for k, ref in enumerate(out_refs):
+        cut = slice(k * 16, (k + 1) * 16)
+        ref[...] = (keep_ref[cut, :] + got_ref[cut, :].astype(F32)).astype(ref.dtype)
+
+
+def near_kernel(keep_ref, got_ref, out_ref, sum_ref, sems):
     copies = []
     for k in range(4):
-        cut = slice(k * 16, (k + 1) * 16)
+        cut = slice(64 + k * 16, 80 + k * 16)
         sum_ref[k] = (keep_ref[cut, :] + got_ref[cut, :].astype(F32)).astype(BF16)
         copies.append(pltpu.make_async_copy(sum_ref.at[k], out_ref.at[k], sems.at[k]))
         copies[-1].start()
@@ -207,22 +214,16 @@
         copy.wait()
 
 
-def near_kernel(keep_ref, got_ref, *out_refs):
-    for k, ref in enumerate(out_refs):
-        cut = slice(64 + k * 16, 80 + k * 16)
-        ref[...] = (keep_ref[cut, :] + got_ref[cut, :].astype(F32)).astype(ref.dtype)
-
-
-def sum_kernel(parts_ref, out_ref):
-    total = parts_ref[0].astype(F32)
-    for k in range(1, 4):
+def sum_kernel(own_ref, a_ref, b_ref, c_ref, out_ref):
+    total = own_ref[...] + a_ref[...].astype(F32) + b_ref[...].astype(F32) + c_ref[...].astype(F32)
+    out_ref[...] = total.astype(BF16)
+
+
+def fold_kernel(parts_ref, residual_ref, out_ref):
+    total = residual_ref[...].astype(F32)
+    for k in range(4):
         total = total + parts_ref[k].astype(F32)
-    out_ref[...] = total.astype(BF16)
-
-
-def fold_kernel(own_ref, a_ref, b_ref, c_ref, residual_ref, out_ref):
-    total = residual_ref[...].astype(F32) + own_ref[...]
-    out_ref[...] = total + a_ref[...].astype(F32) + b_ref[...].astype(F32) + c_ref[...].astype(F32)
+    out_ref[...] = total
 
 
 def finish_kernel(near_ref, far_ref, gain_ref, hidden_ref, normed_ref):
@@ -232,13 +233,14 @@
     normed_ref[...] = (hidden * scale * gain_ref[...]).astype(BF16)
 
 
-def call(body, shapes, specs, *args, scratch=(), outs=VMEM):
+def call(body, shapes, specs, *args, scratch=(), outs=VMEM, cost=None):
     return pl.pallas_call(
         body,
         out_shape=shapes,
         in_specs=specs,
         out_specs=jax.tree.map(lambda _: outs, shapes),
         scratch_shapes=list(scratch),
+        cost_estimate=cost,
         compiler_params=pltpu.CompilerParams(vmem_limit_bytes=16 * 1024 * 1024),
     )(*args)
 
@@ -291,21 +293,21 @@
     got = lax.ppermute(send, "tp", [(i, i ^ 1) for i in range(16)])
     keep = call(keep_kernel, of((SPAN // 2, D), F32), [VMEM, VMEM], keep, weight)
     full = of((16, D), BF16)
-    away = call(
-        far_kernel, pltpu.HBM((4, 16, D), BF16), [VMEM, VMEM], keep, got,
-        scratch=[pltpu.VMEM((4, 16, D), BF16), pltpu.SemaphoreType.DMA((4,))], outs=HBM,
-    )
-    away = lax.all_to_all(away, "tp", 0, 0, axis_index_groups=NEAR_CHIPS)
     own, *parts = call(
-        near_kernel, (of((16, D), F32), full, full, full), [VMEM, VMEM], keep, got
-    )
-    near = [
+        far_kernel, (of((16, D), F32), full, full, full), [VMEM, VMEM], keep, got
+    )
+    parts = [
         lax.ppermute(sent, "tp", [(i, i ^ (2 * k)) for i in range(16)])
         for k, sent in enumerate(parts, 1)
     ]
-    away = call(sum_kernel, full, [VMEM], away)
+    near = call(
+        near_kernel, pltpu.HBM((4, 16, D), BF16), [VMEM, VMEM], keep, got,
+        scratch=[pltpu.VMEM((4, 16, D), BF16), pltpu.SemaphoreType.DMA((4,))], outs=HBM,
+    )
+    near = lax.all_to_all(near, "tp", 0, 0, axis_index_groups=NEAR_CHIPS)
+    away = call(sum_kernel, full, [VMEM] * 4, own, *parts, cost=LONG)
     far = lax.ppermute(away, "tp", [(i, i ^ 8) for i in range(16)])
-    folded = call(fold_kernel, of((16, D), F32), [VMEM] * 5, own, *near, residual_in)
+    folded = call(fold_kernel, of((16, D), F32), [VMEM] * 2, near, residual_in)
     return call(finish_kernel, (full, full), [VMEM] * 3, folded, far, norm_gain[None, :])
 
 

time: 97.2 us -> 99.2 us (1.021)
  the two profiles are of different devices: /device:TPU:64 before, /device:TPU:32 now
where the time goes in v8:
time: 99.2 us; the launch traced here: 98.6 us
  starting transfers between devices  40.2 us (41%)
  blocking collectives  23.2 us (23%)
  waiting for transfers between devices  21.1 us (21%)
  Pallas kernels  9.17 us (9%)
  local copies, waits for them, and re-layouts  4.13 us (4%)
    ppermute x1, starting transfers between devices, shards(): other = lax.ppermute(local, 'seq', FLIP_Z)  14.8 us
    all_to_all x1, blocking collectives, shards(): rows = lax.all_to_all(pairs, 'seq', 0, 0, axis_index_groups=ROW_Y)  11.7 us
    all_to_all x1, blocking collectives, shards(): cols = lax.all_to_all(totals, 'seq', 0, 0, axis_index_groups=ROW_X)  11.5 us
    ppermute x1, waiting for transfers between devices, shards(): far = lax.ppermute(away, 'tp', [(i, i ^ 8) for i in range(16)])  10.4 us
    ppermute x3, starting transfers between devices, shards(): lax.ppermute(sent, 'tp', [(i, i ^ 2 * k) for i in range(16)])  9.21 us
    pallas_call x11, Pallas kernels, call(): pl.pallas_call(body, out_shape=shapes, in_specs=specs, out_specs=jax.tree...  9.17 us
    ppermute x1, starting transfers between devices, shards(): far = lax.ppermute(away, 'tp', [(i, i ^ 8) for i in range(16)])  9.09 us
    ppermute x3, waiting for transfers between devices, shards(): lax.ppermute(sent, 'tp', [(i, i ^ 2 * k) for i in range(16)])  8.09 us
  transfers between devices with their start and end apart: 7, of which 4 were waited for; matrix products, arithmetic and copies ran while one was open for 0% of the time, Pallas kernels for 4%

profile of v8, /device:TPU:32, one launch (start us, length us, event | category | flops | bytes accessed | tf_op | source)
XLA Modules:
  0.0 98.6 jit_solution(5056221984548695152)
XLA Ops:
  0.6 1.7 %shard_map.95.own_ref = bf16[392,128]{1,0:T(8,128)(2,1)S(1)} custom-call(s32[1,3]{1,0:T(1,128)} %starts_ref.1, f32[3,256]{1,0:T(4,128)} %decay_ref.1, bf16[256,384]{1,0:T(8,128)(2,1)} %key_ref.1, bf16[256,384]{1,0:T(8,128)(2,1)} %value_ref.1), custom_call_target="tpu_custom_call" | custom-call | tf_op jit(solution)/shard_map/pallas_call | solution.py:237
  2.4 14.8 %collective-permute-start = (bf16[392,128]{1,0:T(8,128)(2,1)S(1)}, bf16[392,128]{1,0:T(8,128)(2,1)S(1)}, u32[]{:S(2)}, u32[]{:S(2)}) collective-permute-start(bf16[392,128]{1,0:T(8,128)(2,1)S(1)} %shard_map.95.own_ref), channel_id=1, source_target_pairs={{0,16},{16,0},{32,48},{48,32},{64,80},{80,64},{96,112},{112,96},{1... | collective-permute-start | bytes 301064 | tf_op jit(solution)/shard_map/ppermute | solution.py:272
  17.2 0.0 copy-start
  17.2 0.9 copy-done
  18.1 0.0 copy-start.2
  18.1 0.9 copy-done.2
  19.1 0.0 copy-start.3
  19.1 0.9 copy-done.3
  20.0 0.0 copy-start.5
  20.0 0.7 copy-done.5
  20.7 0.0 copy-start.7
  20.7 0.7 copy-done.7
  21.3 0.0 copy-start.1
  21.3 2.4 %shard_map.96 = (f32[256,384]{1,0:T(8,128)S(1)}, f32[256,3]{1,0:T(8,128)S(1)}, bf16[384,4096]{1,0:T(8,128)(2,1)S(1)}) custom-call(s32[1,3]{1,0:T(1,128)S(1)} %copy-done.7, f32[3,256]{1,0:T(4,128)S(1)} %copy-done.5, bf16[256,384]{1,0:T(8,128)(2,1)S(1)} %copy-done, bf16[256,384]{1,0:T(8,128)(2,1)S(1)} %copy-done.2, bf16[256,384]{1,0:T(8,128)(2,1)S(1)} %copy-done.3, ...), custom_call_target="tpu_custom_call" | custom-call | tf_op jit(solution)/shard_map/pallas_call | solution.py:237
  23.8 0.1 pad_add_fusion.place_ref
  23.9 0.7 collective-permute-done.other_ref
  24.5 0.6 shard_map.97
  25.1 11.7 %all_to_all.15.parts_ref.row_ref = bf16[4,392,128]{2,1,0:T(8,128)(2,1)S(1)} all-to-all(bf16[4,392,128]{2,1,0:T(8,128)(2,1)S(1)} %shard_map.97), channel_id=1, replica_groups={{0,32,64,96},{16,48,80,112},{128,160,192,224},{144,176,208,240},{256,28..., dimensions={0} | all-to-all | bytes 802816 | tf_op jit(solution)/shard_map/all_to_all | solution.py:284
  36.8 0.1 shard_map.98
  36.9 11.5 %all_to_all.16.col_ref = bf16[4,392,128]{2,1,0:T(8,128)(2,1)S(1)} all-to-all(bf16[4,392,128]{2,1,0:T(8,128)(2,1)S(1)} %shard_map.98), channel_id=1, replica_groups={{0,128,256,384},{16,144,272,400},{32,160,288,416},{48,176,304,432},{64,..., dimensions={0} | all-to-all | bytes 802816 | tf_op jit(solution)/shard_map/all_to_all | solution.py:286
  48.4 0.0 copy-done.1
  48.4 1.7 %shard_map.99 = (bf16[128,4096]{1,0:T(8,128)(2,1)S(1)}, bf16[128,384]{1,0:T(8,128)(2,1)S(1)}) custom-call(s32[2]{0:T(128)S(1)} %pad_add_fusion.place_ref, bf16[256,384]{1,0:T(8,128)(2,1)S(1)} %copy-done.1, f32[256,384]{1,0:T(8,128)S(1)} %get-tuple-element.18.intra_ref, f32[256,3]{1,0:T(8,128)S(1)} %get-tuple-element.19.carry_ref, ...), custom_call_target="tpu_custom_call" | custom-call | tf_op jit(solution)/shard_map/pallas_call | solution.py:237
  50.1 1.9 %collective-permute-start.1 = (bf16[128,4096]{1,0:T(8,128)(2,1)S(1)}, bf16[128,4096]{1,0:T(8,128)(2,1)S(1)}, u32[]{:S(2)}, u32[]{:S(2)}) collective-permute-start(bf16[128,4096]{1,0:T(8,128)(2,1)S(1)} %get-tuple-element.23), channel_id=1, source_target_pairs={{0,1},{1,0},{2,3},{3,2},{4,5},{5,4},{6,7},{7,6},{8,9},{9,8},{10,11... | collective-permute-start | bytes 3145736 | tf_op jit(solution)/shard_map/ppermute | solution.py:293
  52.1 0.7 shard_map.100.keep_ref
  52.8 1.9 %collective-permute-done.1.got_ref = bf16[128,4096]{1,0:T(8,128)(2,1)S(1)} collective-permute-done((bf16[128,4096]{1,0:T(8,128)(2,1)S(1)}, bf16[128,4096]{1,0:T(8,128)(2,1)S(1)}, u32[]{:S(2)}, u32[]{:S(2)}) %collective-permute-start.1) | collective-permute-done | bytes 1048608 | tf_op jit(solution)/shard_map/ppermute | solution.py:293
  54.7 0.1 shard_map.103
  54.8 2.7 %collective-permute-start.2 = (bf16[16,4096]{1,0:T(8,128)(2,1)S(1)}, bf16[16,4096]{1,0:T(8,128)(2,1)S(1)}, u32[]{:S(2)}, u32[]{:S(2)}) collective-permute-start(bf16[16,4096]{1,0:T(8,128)(2,1)S(1)} %get-tuple-element.25), channel_id=1, source_target_pairs={{0,2},{1,3},{2,0},{3,1},{4,6},{5,7},{6,4},{7,5},{8,10},{9,11},{10,... | collective-permute-start | bytes 393224 | tf_op jit(solution)/shard_map/ppermute | solution.py:300
  57.5 3.4 %collective-permute-start.3 = (bf16[16,4096]{1,0:T(8,128)(2,1)S(1)}, bf16[16,4096]{1,0:T(8,128)(2,1)S(1)}, u32[]{:S(2)}, u32[]{:S(2)}) collective-permute-start(bf16[16,4096]{1,0:T(8,128)(2,1)S(1)} %get-tuple-element.26), channel_id=1, source_target_pairs={{0,4},{1,5},{2,6},{3,7},{4,0},{5,1},{6,2},{7,3},{8,12},{9,13},{10,... | collective-permute-start | bytes 393224 | tf_op jit(solution)/shard_map/ppermute | solution.py:300
  60.9 3.1 %collective-permute-start.4 = (bf16[16,4096]{1,0:T(8,128)(2,1)S(1)}, bf16[16,4096]{1,0:T(8,128)(2,1)S(1)}, u32[]{:S(2)}, u32[]{:S(2)}) collective-permute-start(bf16[16,4096]{1,0:T(8,128)(2,1)S(1)} %get-tuple-element.27), channel_id=1, source_target_pairs={{0,6},{1,7},{2,4},{3,5},{4,2},{5,3},{6,0},{7,1},{8,14},{9,15},{10,... | collective-permute-start | bytes 393224 | tf_op jit(solution)/shard_map/ppermute | solution.py:300
  64.0 0.9 shard_map.101
  64.9 5.2 %all-to-all-start.2 = ((bf16[4,16,4096]{2,1,0:T(8,128)(2,1)}), bf16[4,16,4096]{2,1,0:T(8,128)(2,1)S(1)}, u32[]{:S(2)}, u32[]{:S(2)}) async-start(bf16[4,16,4096]{2,1,0:T(8,128)(2,1)} %shard_map.101), calls=%async_computation.2 | async-start | bytes 1048576 | tf_op jit(solution)/shard_map/all_to_all | solution.py:307
  70.1 0.0 collective-permute-done.2.a_ref
  70.1 0.0 collective-permute-done.3.b_ref
  70.1 8.1 %collective-permute-done.4.c_ref = bf16[16,4096]{1,0:T(8,128)(2,1)S(1)} collective-permute-done((bf16[16,4096]{1,0:T(8,128)(2,1)S(1)}, bf16[16,4096]{1,0:T(8,128)(2,1)S(1)}, u32[]{:S(2)}, u32[]{:S(2)}) %collective-permute-start.4) | collective-permute-done | bytes 131104 | tf_op jit(solution)/shard_map/ppermute | solution.py:300
  78.2 0.0 copy-start.4
  78.2 0.0 copy-start.6
  78.2 0.1 shard_map.104
  78.2 9.1 %collective-permute-start.5 = (bf16[16,4096]{1,0:T(8,128)(2,1)S(1)}, bf16[16,4096]{1,0:T(8,128)(2,1)S(1)}, u32[]{:S(2)}, u32[]{:S(2)}) collective-permute-start(bf16[16,4096]{1,0:T(8,128)(2,1)S(1)} %shard_map.104), channel_id=1, source_target_pairs={{0,8},{1,9},{2,10},{3,11},{4,12},{5,13},{6,14},{7,15},{8,0},{9,1},... | collective-permute-start | bytes 393224 | tf_op jit(solution)/shard_map/ppermute | solution.py:309
  87.3 0.0 all-to-all-done.2.parts_ref
  87.3 0.0 copy-done.4
  87.3 0.1 shard_map.102.near_ref
  87.4 10.4 %collective-permute-done.5.far_ref = bf16[16,4096]{1,0:T(8,128)(2,1)S(1)} collective-permute-done((bf16[16,4096]{1,0:T(8,128)(2,1)S(1)}, bf16[16,4096]{1,0:T(8,128)(2,1)S(1)}, u32[]{:S(2)}, u32[]{:S(2)}) %collective-permute-start.5) | collective-permute-done | bytes 131104 | tf_op jit(solution)/shard_map/ppermute | solution.py:309
  97.8 0.0 copy-done.6
  97.8 0.8 shard_map.105
Async XLA Ops:
  2.4 22.1 %collective-permute-start = (bf16[392,128]{1,0:T(8,128)(2,1)S(1)}, bf16[392,128]{1,0:T(8,128)(2,1)S(1)}, u32[]{:S(2)}, u32[]{:S(2)}) collective-permute-start(bf16[392,128]{1,0:T(8,128)(2,1)S(1)} %shard_map.95.own_ref), channel_id=1, source_target_pairs={{0,16},{16,0},{32,48},{48,32},{64,80},{80,64},{96,112},{112,96},{1... | collective-permute-start | bytes 301064 | tf_op jit(solution)/shard_map/ppermute | solution.py:272
  17.2 0.9 copy-start
  18.1 0.9 copy-start.2
  19.1 0.9 copy-start.3
  20.0 0.7 copy-start.5
  20.7 0.7 copy-start.7
  21.3 27.1 %copy-start.1 = (bf16[256,384]{1,0:T(8,128)(2,1)S(1)}, bf16[256,384]{1,0:T(8,128)(2,1)}, u32[]{:S(2)}) copy-start(bf16[256,384]{1,0:T(8,128)(2,1)} %query_ref.2) | copy-start | bytes 589828
  50.1 4.6 %collective-permute-start.1 = (bf16[128,4096]{1,0:T(8,128)(2,1)S(1)}, bf16[128,4096]{1,0:T(8,128)(2,1)S(1)}, u32[]{:S(2)}, u32[]{:S(2)}) collective-permute-start(bf16[128,4096]{1,0:T(8,128)(2,1)S(1)} %get-tuple-element.23), channel_id=1, source_target_pairs={{0,1},{1,0},{2,3},{3,2},{4,5},{5,4},{6,7},{7,6},{8,9},{9,8},{10,11... | collective-permute-start | bytes 3145736 | tf_op jit(solution)/shard_map/ppermute | solution.py:293
  54.8 15.3 %collective-permute-start.2 = (bf16[16,4096]{1,0:T(8,128)(2,1)S(1)}, bf16[16,4096]{1,0:T(8,128)(2,1)S(1)}, u32[]{:S(2)}, u32[]{:S(2)}) collective-permute-start(bf16[16,4096]{1,0:T(8,128)(2,1)S(1)} %get-tuple-element.25), channel_id=1, source_target_pairs={{0,2},{1,3},{2,0},{3,1},{4,6},{5,7},{6,4},{7,5},{8,10},{9,11},{10,... | collective-permute-start | bytes 393224 | tf_op jit(solution)/shard_map/ppermute | solution.py:300
  57.5 12.5 %collective-permute-start.3 = (bf16[16,4096]{1,0:T(8,128)(2,1)S(1)}, bf16[16,4096]{1,0:T(8,128)(2,1)S(1)}, u32[]{:S(2)}, u32[]{:S(2)}) collective-permute-start(bf16[16,4096]{1,0:T(8,128)(2,1)S(1)} %get-tuple-element.26), channel_id=1, source_target_pairs={{0,4},{1,5},{2,6},{3,7},{4,0},{5,1},{6,2},{7,3},{8,12},{9,13},{10,... | collective-permute-start | bytes 393224 | tf_op jit(solution)/shard_map/ppermute | solution.py:300
  60.9 17.2 %collective-permute-start.4 = (bf16[16,4096]{1,0:T(8,128)(2,1)S(1)}, bf16[16,4096]{1,0:T(8,128)(2,1)S(1)}, u32[]{:S(2)}, u32[]{:S(2)}) collective-permute-start(bf16[16,4096]{1,0:T(8,128)(2,1)S(1)} %get-tuple-element.27), channel_id=1, source_target_pairs={{0,6},{1,7},{2,4},{3,5},{4,2},{5,3},{6,0},{7,1},{8,14},{9,15},{10,... | collective-permute-start | bytes 393224 | tf_op jit(solution)/shard_map/ppermute | solution.py:300
  64.9 22.4 %all-to-all-start.2 = ((bf16[4,16,4096]{2,1,0:T(8,128)(2,1)}), bf16[4,16,4096]{2,1,0:T(8,128)(2,1)S(1)}, u32[]{:S(2)}, u32[]{:S(2)}) async-start(bf16[4,16,4096]{2,1,0:T(8,128)(2,1)} %shard_map.101), calls=%async_computation.2 | async-start | bytes 1048576 | tf_op jit(solution)/shard_map/all_to_all | solution.py:307
  78.2 9.2 %copy-start.4 = (bf16[16,4096]{1,0:T(8,128)(2,1)S(1)}, bf16[16,4096]{1,0:T(8,128)(2,1)}, u32[]{:S(2)}) copy-start(bf16[16,4096]{1,0:T(8,128)(2,1)} %residual_ref.1) | copy-start | bytes 393220
  78.2 19.7 %copy-start.6 = (f32[4096]{0:T(1024)S(1)}, f32[4096]{0:T(1024)}, u32[]{:S(2)}) copy-start(f32[4096]{0:T(1024)} %param.15) | copy-start | bytes 49156
  78.2 19.6 %collective-permute-start.5 = (bf16[16,4096]{1,0:T(8,128)(2,1)S(1)}, bf16[16,4096]{1,0:T(8,128)(2,1)S(1)}, u32[]{:S(2)}, u32[]{:S(2)}) collective-permute-start(bf16[16,4096]{1,0:T(8,128)(2,1)S(1)} %shard_map.104), channel_id=1, source_target_pairs={{0,8},{1,9},{2,10},{3,11},{4,12},{5,13},{6,14},{7,15},{8,0},{9,1},... | collective-permute-start | bytes 393224 | tf_op jit(solution)/shard_map/ppermute | solution.py:309

commit v9 on v8

--- a/solution.py
+++ b/solution.py
@@ -18,6 +18,7 @@
 FLIP_Z = [(i, i ^ 1) for i in range(SHARDS)]
 ROW_Y = [[g + 2 * k for k in range(4)] for g in range(SHARDS) if g & 6 == 0]
 ROW_X = [[g + 8 * k for k in range(4)] for g in range(8)]
+FAR_ORDER = (0, 3, 2, 1)
 LONG = pl.CostEstimate(flops=10**11, bytes_accessed=0, transcendentals=0)
 NEAR_CHIPS = [[8 * g + 2 * k + core for k in range(4)] for g in range(2) for core in range(2)]
 
@@ -183,7 +184,7 @@
         mixed_ref[:, cut] = (mixed * scale).astype(BF16)
     core, chip = place_ref[1] & 1, place_ref[1] >> 1
     for k in range(8):
-        start = ((chip & 4) + (k & 3) if k & 4 else chip ^ 4 ^ k) * 32
+        start = ((chip & 4) + (k & 3) if k & 4 else chip ^ 4 ^ FAR_ORDER[k]) * 32
         cut = slice(k * 16, (k + 1) * 16)
         own, sibling = start + core * 16, start + (1 - core) * 16
         keep_ref[cut, :] = mixed_ref[pl.ds(pl.multiple_of(own, 16), 16), :]
@@ -298,7 +299,7 @@
     )
     parts = [
         lax.ppermute(sent, "tp", [(i, i ^ (2 * k)) for i in range(16)])
-        for k, sent in enumerate(parts, 1)
+        for k, sent in zip(FAR_ORDER[1:], parts)
     ]
     near = call(
         near_kernel, pltpu.HBM((4, 16, D), BF16), [VMEM, VMEM], keep, got,

time: 99.2 us -> 93.8 us (0.946)
  the two profiles are of different devices: /device:TPU:32 before, /device:TPU:64 now
where the time goes in v9:
time: 93.8 us; the launch traced here: 93.3 us
  starting transfers between devices  39 us (42%)
  blocking collectives  23.7 us (25%)
  waiting for transfers between devices  16.5 us (18%)
  Pallas kernels  9.18 us (10%)
  local copies, waits for them, and re-layouts  4.13 us (4%)
    ppermute x1, starting transfers between devices, shards(): other = lax.ppermute(local, 'seq', FLIP_Z)  13.9 us
    all_to_all x1, blocking collectives, shards(): rows = lax.all_to_all(pairs, 'seq', 0, 0, axis_index_groups=ROW_Y)  12.1 us
    all_to_all x1, blocking collectives, shards(): cols = lax.all_to_all(totals, 'seq', 0, 0, axis_index_groups=ROW_X)  11.5 us
    ppermute x3, starting transfers between devices, shards(): lax.ppermute(sent, 'tp', [(i, i ^ 2 * k) for i in range(16)])  9.21 us
    pallas_call x11, Pallas kernels, call(): pl.pallas_call(body, out_shape=shapes, in_specs=specs, out_specs=jax.tree...  9.18 us
    all_to_all x1, waiting for transfers between devices, shards(): near = lax.all_to_all(near, 'tp', 0, 0, axis_index_groups=NEAR_CHIPS)  8.36 us
    ppermute x1, starting transfers between devices, shards(): far = lax.ppermute(away, 'tp', [(i, i ^ 8) for i in range(16)])  8.11 us
    ppermute x1, waiting for transfers between devices, shards(): far = lax.ppermute(away, 'tp', [(i, i ^ 8) for i in range(16)])  6.18 us
  transfers between devices with their start and end apart: 7, of which 3 were waited for; matrix products, arithmetic and copies ran while one was open for 0% of the time, Pallas kernels for 4%

profile of v9, /device:TPU:64, one launch (start us, length us, event | category | flops | bytes accessed | tf_op | source)
XLA Modules:
  0.0 93.3 jit_solution(4560861059651930085)
XLA Ops:
  0.6 1.7 %shard_map.95.own_ref = bf16[392,128]{1,0:T(8,128)(2,1)S(1)} custom-call(s32[1,3]{1,0:T(1,128)} %starts_ref.1, f32[3,256]{1,0:T(4,128)} %decay_ref.1, bf16[256,384]{1,0:T(8,128)(2,1)} %key_ref.1, bf16[256,384]{1,0:T(8,128)(2,1)} %value_ref.1), custom_call_target="tpu_custom_call" | custom-call | tf_op jit(solution)/shard_map/pallas_call | solution.py:238
  2.4 13.9 %collective-permute-start = (bf16[392,128]{1,0:T(8,128)(2,1)S(1)}, bf16[392,128]{1,0:T(8,128)(2,1)S(1)}, u32[]{:S(2)}, u32[]{:S(2)}) collective-permute-start(bf16[392,128]{1,0:T(8,128)(2,1)S(1)} %shard_map.95.own_ref), channel_id=1, source_target_pairs={{0,16},{16,0},{32,48},{48,32},{64,80},{80,64},{96,112},{112,96},{1... | collective-permute-start | bytes 301064 | tf_op jit(solution)/shard_map/ppermute | solution.py:273
  16.3 0.0 copy-start
  16.3 0.9 copy-done
  17.2 0.0 copy-start.2
  17.2 0.9 copy-done.2
  18.2 0.0 copy-start.3
  18.2 0.9 copy-done.3
  19.1 0.0 copy-start.5
  19.1 0.7 copy-done.5
  19.8 0.0 copy-start.7
  19.8 0.7 copy-done.7
  20.4 0.0 copy-start.1
  20.4 2.4 %shard_map.96 = (f32[256,384]{1,0:T(8,128)S(1)}, f32[256,3]{1,0:T(8,128)S(1)}, bf16[384,4096]{1,0:T(8,128)(2,1)S(1)}) custom-call(s32[1,3]{1,0:T(1,128)S(1)} %copy-done.7, f32[3,256]{1,0:T(4,128)S(1)} %copy-done.5, bf16[256,384]{1,0:T(8,128)(2,1)S(1)} %copy-done, bf16[256,384]{1,0:T(8,128)(2,1)S(1)} %copy-done.2, bf16[256,384]{1,0:T(8,128)(2,1)S(1)} %copy-done.3, ...), custom_call_target="tpu_custom_call" | custom-call | tf_op jit(solution)/shard_map/pallas_call | solution.py:238
  22.9 0.1 pad_add_fusion.place_ref
  23.0 0.0 collective-permute-done.other_ref
  23.0 0.6 shard_map.97
  23.6 12.1 %all_to_all.15.parts_ref.row_ref = bf16[4,392,128]{2,1,0:T(8,128)(2,1)S(1)} all-to-all(bf16[4,392,128]{2,1,0:T(8,128)(2,1)S(1)} %shard_map.97), channel_id=1, replica_groups={{0,32,64,96},{16,48,80,112},{128,160,192,224},{144,176,208,240},{256,28..., dimensions={0} | all-to-all | bytes 802816 | tf_op jit(solution)/shard_map/all_to_all | solution.py:285
  35.7 0.1 shard_map.98
  35.8 11.5 %all_to_all.16.col_ref = bf16[4,392,128]{2,1,0:T(8,128)(2,1)S(1)} all-to-all(bf16[4,392,128]{2,1,0:T(8,128)(2,1)S(1)} %shard_map.98), channel_id=1, replica_groups={{0,128,256,384},{16,144,272,400},{32,160,288,416},{48,176,304,432},{64,..., dimensions={0} | all-to-all | bytes 802816 | tf_op jit(solution)/shard_map/all_to_all | solution.py:287
  47.3 0.0 copy-done.1
  47.3 1.7 %shard_map.99 = (bf16[128,4096]{1,0:T(8,128)(2,1)S(1)}, bf16[128,384]{1,0:T(8,128)(2,1)S(1)}) custom-call(s32[2]{0:T(128)S(1)} %pad_add_fusion.place_ref, bf16[256,384]{1,0:T(8,128)(2,1)S(1)} %copy-done.1, f32[256,384]{1,0:T(8,128)S(1)} %get-tuple-element.18.intra_ref, f32[256,3]{1,0:T(8,128)S(1)} %get-tuple-element.19.carry_ref, ...), custom_call_target="tpu_custom_call" | custom-call | tf_op jit(solution)/shard_map/pallas_call | solution.py:238
  49.0 1.9 %collective-permute-start.1 = (bf16[128,4096]{1,0:T(8,128)(2,1)S(1)}, bf16[128,4096]{1,0:T(8,128)(2,1)S(1)}, u32[]{:S(2)}, u32[]{:S(2)}) collective-permute-start(bf16[128,4096]{1,0:T(8,128)(2,1)S(1)} %get-tuple-element.23), channel_id=1, source_target_pairs={{0,1},{1,0},{2,3},{3,2},{4,5},{5,4},{6,7},{7,6},{8,9},{9,8},{10,11... | collective-permute-start | bytes 3145736 | tf_op jit(solution)/shard_map/ppermute | solution.py:294
  51.0 0.7 shard_map.100.keep_ref
  51.7 1.9 %collective-permute-done.1.got_ref = bf16[128,4096]{1,0:T(8,128)(2,1)S(1)} collective-permute-done((bf16[128,4096]{1,0:T(8,128)(2,1)S(1)}, bf16[128,4096]{1,0:T(8,128)(2,1)S(1)}, u32[]{:S(2)}, u32[]{:S(2)}) %collective-permute-start.1) | collective-permute-done | bytes 1048608 | tf_op jit(solution)/shard_map/ppermute | solution.py:294
  53.6 0.1 shard_map.103
  53.7 3.1 %collective-permute-start.2 = (bf16[16,4096]{1,0:T(8,128)(2,1)S(1)}, bf16[16,4096]{1,0:T(8,128)(2,1)S(1)}, u32[]{:S(2)}, u32[]{:S(2)}) collective-permute-start(bf16[16,4096]{1,0:T(8,128)(2,1)S(1)} %get-tuple-element.25), channel_id=1, source_target_pairs={{0,6},{1,7},{2,4},{3,5},{4,2},{5,3},{6,0},{7,1},{8,14},{9,15},{10,... | collective-permute-start | bytes 393224 | tf_op jit(solution)/shard_map/ppermute | solution.py:301
  56.8 4.1 %collective-permute-start.3 = (bf16[16,4096]{1,0:T(8,128)(2,1)S(1)}, bf16[16,4096]{1,0:T(8,128)(2,1)S(1)}, u32[]{:S(2)}, u32[]{:S(2)}) collective-permute-start(bf16[16,4096]{1,0:T(8,128)(2,1)S(1)} %get-tuple-element.26), channel_id=1, source_target_pairs={{0,4},{1,5},{2,6},{3,7},{4,0},{5,1},{6,2},{7,3},{8,12},{9,13},{10,... | collective-permute-start | bytes 393224 | tf_op jit(solution)/shard_map/ppermute | solution.py:301
  60.9 2.0 %collective-permute-start.4 = (bf16[16,4096]{1,0:T(8,128)(2,1)S(1)}, bf16[16,4096]{1,0:T(8,128)(2,1)S(1)}, u32[]{:S(2)}, u32[]{:S(2)}) collective-permute-start(bf16[16,4096]{1,0:T(8,128)(2,1)S(1)} %get-tuple-element.27), channel_id=1, source_target_pairs={{0,2},{1,3},{2,0},{3,1},{4,6},{5,7},{6,4},{7,5},{8,10},{9,11},{10,... | collective-permute-start | bytes 393224 | tf_op jit(solution)/shard_map/ppermute | solution.py:301
  62.9 0.9 shard_map.101
  63.8 5.8 %all-to-all-start.2 = ((bf16[4,16,4096]{2,1,0:T(8,128)(2,1)}), bf16[4,16,4096]{2,1,0:T(8,128)(2,1)S(1)}, u32[]{:S(2)}, u32[]{:S(2)}) async-start(bf16[4,16,4096]{2,1,0:T(8,128)(2,1)} %shard_map.101), calls=%async_computation.2 | async-start | bytes 1048576 | tf_op jit(solution)/shard_map/all_to_all | solution.py:308
  69.6 0.0 collective-permute-done.2.a_ref
  69.6 0.0 collective-permute-done.3.b_ref
  69.6 0.0 collective-permute-done.4.c_ref
  69.6 0.0 copy-start.4
  69.6 0.0 copy-start.6
  69.6 0.1 shard_map.104
  69.7 8.1 %collective-permute-start.5 = (bf16[16,4096]{1,0:T(8,128)(2,1)S(1)}, bf16[16,4096]{1,0:T(8,128)(2,1)S(1)}, u32[]{:S(2)}, u32[]{:S(2)}) collective-permute-start(bf16[16,4096]{1,0:T(8,128)(2,1)S(1)} %shard_map.104), channel_id=1, source_target_pairs={{0,8},{1,9},{2,10},{3,11},{4,12},{5,13},{6,14},{7,15},{8,0},{9,1},... | collective-permute-start | bytes 393224 | tf_op jit(solution)/shard_map/ppermute | solution.py:310
  77.8 8.4 %all-to-all-done.2.parts_ref = bf16[4,16,4096]{2,1,0:T(8,128)(2,1)S(1)} async-done(((bf16[4,16,4096]{2,1,0:T(8,128)(2,1)}), bf16[4,16,4096]{2,1,0:T(8,128)(2,1)S(1)}, u32[]{:S(2)}, u32[]{:S(2)}) %all-to-all-start.2) | async-done | bytes 524320 | tf_op jit(solution)/shard_map/all_to_all | solution.py:308
  86.2 0.0 copy-done.4
  86.2 0.1 shard_map.102.near_ref
  86.3 6.2 %collective-permute-done.5.far_ref = bf16[16,4096]{1,0:T(8,128)(2,1)S(1)} collective-permute-done((bf16[16,4096]{1,0:T(8,128)(2,1)S(1)}, bf16[16,4096]{1,0:T(8,128)(2,1)S(1)}, u32[]{:S(2)}, u32[]{:S(2)}) %collective-permute-start.5) | collective-permute-done | bytes 131104 | tf_op jit(solution)/shard_map/ppermute | solution.py:310
  92.5 0.0 copy-done.6
  92.5 0.8 shard_map.105
Async XLA Ops:
  2.4 20.6 %collective-permute-start = (bf16[392,128]{1,0:T(8,128)(2,1)S(1)}, bf16[392,128]{1,0:T(8,128)(2,1)S(1)}, u32[]{:S(2)}, u32[]{:S(2)}) collective-permute-start(bf16[392,128]{1,0:T(8,128)(2,1)S(1)} %shard_map.95.own_ref), channel_id=1, source_target_pairs={{0,16},{16,0},{32,48},{48,32},{64,80},{80,64},{96,112},{112,96},{1... | collective-permute-start | bytes 301064 | tf_op jit(solution)/shard_map/ppermute | solution.py:273
  16.3 0.9 copy-start
  17.2 0.9 copy-start.2
  18.2 0.9 copy-start.3
  19.1 0.7 copy-start.5
  19.8 0.7 copy-start.7
  20.4 26.9 %copy-start.1 = (bf16[256,384]{1,0:T(8,128)(2,1)S(1)}, bf16[256,384]{1,0:T(8,128)(2,1)}, u32[]{:S(2)}) copy-start(bf16[256,384]{1,0:T(8,128)(2,1)} %query_ref.2) | copy-start | bytes 589828
  49.0 4.6 %collective-permute-start.1 = (bf16[128,4096]{1,0:T(8,128)(2,1)S(1)}, bf16[128,4096]{1,0:T(8,128)(2,1)S(1)}, u32[]{:S(2)}, u32[]{:S(2)}) collective-permute-start(bf16[128,4096]{1,0:T(8,128)(2,1)S(1)} %get-tuple-element.23), channel_id=1, source_target_pairs={{0,1},{1,0},{2,3},{3,2},{4,5},{5,4},{6,7},{7,6},{8,9},{9,8},{10,11... | collective-permute-start | bytes 3145736 | tf_op jit(solution)/shard_map/ppermute | solution.py:294
  53.7 15.9 %collective-permute-start.2 = (bf16[16,4096]{1,0:T(8,128)(2,1)S(1)}, bf16[16,4096]{1,0:T(8,128)(2,1)S(1)}, u32[]{:S(2)}, u32[]{:S(2)}) collective-permute-start(bf16[16,4096]{1,0:T(8,128)(2,1)S(1)} %get-tuple-element.25), channel_id=1, source_target_pairs={{0,6},{1,7},{2,4},{3,5},{4,2},{5,3},{6,0},{7,1},{8,14},{9,15},{10,... | collective-permute-start | bytes 393224 | tf_op jit(solution)/shard_map/ppermute | solution.py:301
  56.8 12.8 %collective-permute-start.3 = (bf16[16,4096]{1,0:T(8,128)(2,1)S(1)}, bf16[16,4096]{1,0:T(8,128)(2,1)S(1)}, u32[]{:S(2)}, u32[]{:S(2)}) collective-permute-start(bf16[16,4096]{1,0:T(8,128)(2,1)S(1)} %get-tuple-element.26), channel_id=1, source_target_pairs={{0,4},{1,5},{2,6},{3,7},{4,0},{5,1},{6,2},{7,3},{8,12},{9,13},{10,... | collective-permute-start | bytes 393224 | tf_op jit(solution)/shard_map/ppermute | solution.py:301
  60.9 8.7 %collective-permute-start.4 = (bf16[16,4096]{1,0:T(8,128)(2,1)S(1)}, bf16[16,4096]{1,0:T(8,128)(2,1)S(1)}, u32[]{:S(2)}, u32[]{:S(2)}) collective-permute-start(bf16[16,4096]{1,0:T(8,128)(2,1)S(1)} %get-tuple-element.27), channel_id=1, source_target_pairs={{0,2},{1,3},{2,0},{3,1},{4,6},{5,7},{6,4},{7,5},{8,10},{9,11},{10,... | collective-permute-start | bytes 393224 | tf_op jit(solution)/shard_map/ppermute | solution.py:301
  63.8 22.4 %all-to-all-start.2 = ((bf16[4,16,4096]{2,1,0:T(8,128)(2,1)}), bf16[4,16,4096]{2,1,0:T(8,128)(2,1)S(1)}, u32[]{:S(2)}, u32[]{:S(2)}) async-start(bf16[4,16,4096]{2,1,0:T(8,128)(2,1)} %shard_map.101), calls=%async_computation.2 | async-start | bytes 1048576 | tf_op jit(solution)/shard_map/all_to_all | solution.py:308
  69.6 16.6 %copy-start.4 = (bf16[16,4096]{1,0:T(8,128)(2,1)S(1)}, bf16[16,4096]{1,0:T(8,128)(2,1)}, u32[]{:S(2)}) copy-start(bf16[16,4096]{1,0:T(8,128)(2,1)} %residual_ref.1) | copy-start | bytes 393220
  69.6 22.8 %copy-start.6 = (f32[4096]{0:T(1024)S(1)}, f32[4096]{0:T(1024)}, u32[]{:S(2)}) copy-start(f32[4096]{0:T(1024)} %param.15) | copy-start | bytes 49156
  69.7 22.7 %collective-permute-start.5 = (bf16[16,4096]{1,0:T(8,128)(2,1)S(1)}, bf16[16,4096]{1,0:T(8,128)(2,1)S(1)}, u32[]{:S(2)}, u32[]{:S(2)}) collective-permute-start(bf16[16,4096]{1,0:T(8,128)(2,1)S(1)} %shard_map.104), channel_id=1, source_target_pairs={{0,8},{1,9},{2,10},{3,11},{4,12},{5,13},{6,14},{7,15},{8,0},{9,1},... | collective-permute-start | bytes 393224 | tf_op jit(solution)/shard_map/ppermute | solution.py:310

commit v10 on v9

--- a/solution.py
+++ b/solution.py
@@ -18,9 +18,8 @@
 FLIP_Z = [(i, i ^ 1) for i in range(SHARDS)]
 ROW_Y = [[g + 2 * k for k in range(4)] for g in range(SHARDS) if g & 6 == 0]
 ROW_X = [[g + 8 * k for k in range(4)] for g in range(8)]
-FAR_ORDER = (0, 3, 2, 1)
+FAR_ORDER, NEAR_ORDER = (0, 3, 2, 1), (0, 2, 1, 3)
 LONG = pl.CostEstimate(flops=10**11, bytes_accessed=0, transcendentals=0)
-NEAR_CHIPS = [[8 * g + 2 * k + core for k in range(4)] for g in range(2) for core in range(2)]
 
 VMEM = pl.BlockSpec(memory_space=pltpu.VMEM)
 HBM = pl.BlockSpec(memory_space=pltpu.HBM)
@@ -184,7 +183,7 @@
         mixed_ref[:, cut] = (mixed * scale).astype(BF16)
     core, chip = place_ref[1] & 1, place_ref[1] >> 1
     for k in range(8):
-        start = ((chip & 4) + (k & 3) if k & 4 else chip ^ 4 ^ FAR_ORDER[k]) * 32
+        start = (chip ^ NEAR_ORDER[k - 4] if k & 4 else chip ^ 4 ^ FAR_ORDER[k]) * 32
         cut = slice(k * 16, (k + 1) * 16)
         own, sibling = start + core * 16, start + (1 - core) * 16
         keep_ref[cut, :] = mixed_ref[pl.ds(pl.multiple_of(own, 16), 16), :]
@@ -204,15 +203,19 @@
         ref[...] = (keep_ref[cut, :] + got_ref[cut, :].astype(F32)).astype(ref.dtype)
 
 
-def near_kernel(keep_ref, got_ref, out_ref, sum_ref, sems):
-    copies = []
-    for k in range(4):
-        cut = slice(64 + k * 16, 80 + k * 16)
-        sum_ref[k] = (keep_ref[cut, :] + got_ref[cut, :].astype(F32)).astype(BF16)
-        copies.append(pltpu.make_async_copy(sum_ref.at[k], out_ref.at[k], sems.at[k]))
-        copies[-1].start()
-    for copy in copies:
-        copy.wait()
+def near_kernel(keep_ref, got_ref, own_ref, next_ref, sent_ref):
+    def rows(start, stop):
+        return keep_ref[start:stop, :] + got_ref[start:stop, :].astype(F32)
+
+    sent_ref[...] = rows(96, 128).astype(BF16)
+    own_ref[...] = rows(64, 80)
+    next_ref[...] = rows(80, 96)
+
+
+def next_kernel(own_ref, next_ref, got_ref, residual_ref, folded_ref, out_ref):
+    out_ref[...] = (next_ref[...] + got_ref[16:, :].astype(F32)).astype(BF16)
+    folded = residual_ref[...].astype(F32) + own_ref[...]
+    folded_ref[...] = folded + got_ref[:16, :].astype(F32)
 
 
 def sum_kernel(own_ref, a_ref, b_ref, c_ref, out_ref):
@@ -220,15 +223,8 @@
     out_ref[...] = total.astype(BF16)
 
 
-def fold_kernel(parts_ref, residual_ref, out_ref):
-    total = residual_ref[...].astype(F32)
-    for k in range(4):
-        total = total + parts_ref[k].astype(F32)
-    out_ref[...] = total
-
-
-def finish_kernel(near_ref, far_ref, gain_ref, hidden_ref, normed_ref):
-    hidden = near_ref[...] + far_ref[...].astype(F32)
+def finish_kernel(folded_ref, near_ref, far_ref, gain_ref, hidden_ref, normed_ref):
+    hidden = folded_ref[...] + near_ref[...].astype(F32) + far_ref[...].astype(F32)
     scale = lax.rsqrt(jnp.mean(hidden * hidden, axis=1, keepdims=True) + 1e-05)
     hidden_ref[...] = hidden.astype(BF16)
     normed_ref[...] = (hidden * scale * gain_ref[...]).astype(BF16)
@@ -301,15 +297,18 @@
         lax.ppermute(sent, "tp", [(i, i ^ (2 * k)) for i in range(16)])
         for k, sent in zip(FAR_ORDER[1:], parts)
     ]
-    near = call(
-        near_kernel, pltpu.HBM((4, 16, D), BF16), [VMEM, VMEM], keep, got,
-        scratch=[pltpu.VMEM((4, 16, D), BF16), pltpu.SemaphoreType.DMA((4,))], outs=HBM,
-    )
-    near = lax.all_to_all(near, "tp", 0, 0, axis_index_groups=NEAR_CHIPS)
+    wide = of((16, D), F32)
+    mine, following, sent = call(
+        near_kernel, (wide, wide, of((32, D), BF16)), [VMEM, VMEM], keep, got
+    )
+    first = lax.ppermute(sent, "tp", [(i, i ^ 2) for i in range(16)])
     away = call(sum_kernel, full, [VMEM] * 4, own, *parts, cost=LONG)
     far = lax.ppermute(away, "tp", [(i, i ^ 8) for i in range(16)])
-    folded = call(fold_kernel, of((16, D), F32), [VMEM] * 2, near, residual_in)
-    return call(finish_kernel, (full, full), [VMEM] * 3, folded, far, norm_gain[None, :])
+    folded, following = call(
+        next_kernel, (wide, full), [VMEM] * 4, mine, following, first, residual_in
+    )
+    second = lax.ppermute(following, "tp", [(i, i ^ 4) for i in range(16)])
+    return call(finish_kernel, (full, full), [VMEM] * 4, folded, second, far, norm_gain[None, :])
 
 
 def solution(mesh):

time: 93.8 us -> 96.5 us (1.029)
  the two profiles are of different devices: /device:TPU:64 before, /device:TPU:1 now
where the time goes in v10:
time: 96.5 us; the launch traced here: 95.9 us
  starting transfers between devices  42.8 us (44%)
  blocking collectives  21 us (22%)
  waiting for transfers between devices  18.6 us (19%)
  Pallas kernels  8.44 us (9%)
  local copies, waits for them, and re-layouts  4.13 us (4%)
    ppermute x1, starting transfers between devices, shards(): other = lax.ppermute(local, 'seq', FLIP_Z)  16.3 us
    all_to_all x1, blocking collectives, shards(): rows = lax.all_to_all(pairs, 'seq', 0, 0, axis_index_groups=ROW_Y)  10.9 us
    all_to_all x1, blocking collectives, shards(): cols = lax.all_to_all(totals, 'seq', 0, 0, axis_index_groups=ROW_X)  10.1 us
    ppermute x3, starting transfers between devices, shards(): lax.ppermute(sent, 'tp', [(i, i ^ 2 * k) for i in range(16)])  9.27 us
    pallas_call x11, Pallas kernels, call(): pl.pallas_call(body, out_shape=shapes, in_specs=specs, out_specs=jax.tree...  8.44 us
    ppermute x1, starting transfers between devices, shards(): far = lax.ppermute(away, 'tp', [(i, i ^ 8) for i in range(16)])  7.67 us
    ppermute x1, waiting for transfers between devices, shards(): far = lax.ppermute(away, 'tp', [(i, i ^ 8) for i in range(16)])  6.49 us
    ppermute x1, waiting for transfers between devices, shards(): second = lax.ppermute(following, 'tp', [(i, i ^ 4) for i in range(16)])  6.23 us
  transfers between devices with their start and end apart: 8, of which 4 were waited for; matrix products, arithmetic and copies ran while one was open for 0% of the time, Pallas kernels for 4%

profile of v10, /device:TPU:1, one launch (start us, length us, event | category | flops | bytes accessed | tf_op | source)
XLA Modules:
  0.0 95.9 jit_solution(6670160339440041507)
XLA Ops:
  0.6 1.7 %shard_map.95.own_ref = bf16[392,128]{1,0:T(8,128)(2,1)S(1)} custom-call(s32[1,3]{1,0:T(1,128)} %starts_ref.1, f32[3,256]{1,0:T(4,128)} %decay_ref.1, bf16[256,384]{1,0:T(8,128)(2,1)} %key_ref.1, bf16[256,384]{1,0:T(8,128)(2,1)} %value_ref.1), custom_call_target="tpu_custom_call" | custom-call | tf_op jit(solution)/shard_map/pallas_call | solution.py:234
  2.4 16.3 %collective-permute-start = (bf16[392,128]{1,0:T(8,128)(2,1)S(1)}, bf16[392,128]{1,0:T(8,128)(2,1)S(1)}, u32[]{:S(2)}, u32[]{:S(2)}) collective-permute-start(bf16[392,128]{1,0:T(8,128)(2,1)S(1)} %shard_map.95.own_ref), channel_id=1, source_target_pairs={{0,16},{16,0},{32,48},{48,32},{64,80},{80,64},{96,112},{112,96},{1... | collective-permute-start | bytes 301064 | tf_op jit(solution)/shard_map/ppermute | solution.py:269
  18.7 0.0 copy-start
  18.7 0.9 copy-done
  19.6 0.0 copy-start.2
  19.6 0.9 copy-done.2
  20.5 0.0 copy-start.3
  20.5 0.9 copy-done.3
  21.4 0.0 copy-start.5
  21.4 0.7 copy-done.5
  22.1 0.0 copy-start.7
  22.1 0.7 copy-done.7
  22.8 0.0 copy-start.1
  22.8 2.4 %shard_map.96 = (f32[256,384]{1,0:T(8,128)S(1)}, f32[256,3]{1,0:T(8,128)S(1)}, bf16[384,4096]{1,0:T(8,128)(2,1)S(1)}) custom-call(s32[1,3]{1,0:T(1,128)S(1)} %copy-done.7, f32[3,256]{1,0:T(4,128)S(1)} %copy-done.5, bf16[256,384]{1,0:T(8,128)(2,1)S(1)} %copy-done, bf16[256,384]{1,0:T(8,128)(2,1)S(1)} %copy-done.2, bf16[256,384]{1,0:T(8,128)(2,1)S(1)} %copy-done.3, ...), custom_call_target="tpu_custom_call" | custom-call | tf_op jit(solution)/shard_map/pallas_call | solution.py:234
  25.2 0.1 pad_add_fusion.place_ref
  25.3 0.0 collective-permute-done.other_ref
  25.3 0.6 shard_map.97
  25.9 10.9 %all_to_all.10.parts_ref.row_ref = bf16[4,392,128]{2,1,0:T(8,128)(2,1)S(1)} all-to-all(bf16[4,392,128]{2,1,0:T(8,128)(2,1)S(1)} %shard_map.97), channel_id=1, replica_groups={{0,32,64,96},{16,48,80,112},{128,160,192,224},{144,176,208,240},{256,28..., dimensions={0} | all-to-all | bytes 802816 | tf_op jit(solution)/shard_map/all_to_all | solution.py:281
  36.9 0.1 shard_map.98
  36.9 10.1 %all_to_all.11.col_ref = bf16[4,392,128]{2,1,0:T(8,128)(2,1)S(1)} all-to-all(bf16[4,392,128]{2,1,0:T(8,128)(2,1)S(1)} %shard_map.98), channel_id=1, replica_groups={{0,128,256,384},{16,144,272,400},{32,160,288,416},{48,176,304,432},{64,..., dimensions={0} | all-to-all | bytes 802816 | tf_op jit(solution)/shard_map/all_to_all | solution.py:283
  47.0 0.0 copy-done.1
  47.0 1.8 %shard_map.99 = (bf16[128,4096]{1,0:T(8,128)(2,1)S(1)}, bf16[128,384]{1,0:T(8,128)(2,1)S(1)}) custom-call(s32[2]{0:T(128)S(1)} %pad_add_fusion.place_ref, bf16[256,384]{1,0:T(8,128)(2,1)S(1)} %copy-done.1, f32[256,384]{1,0:T(8,128)S(1)} %get-tuple-element.23.intra_ref, f32[256,3]{1,0:T(8,128)S(1)} %get-tuple-element.24.carry_ref, ...), custom_call_target="tpu_custom_call" | custom-call | tf_op jit(solution)/shard_map/pallas_call | solution.py:234
  48.8 5.5 %collective-permute-start.1 = (bf16[128,4096]{1,0:T(8,128)(2,1)S(1)}, bf16[128,4096]{1,0:T(8,128)(2,1)S(1)}, u32[]{:S(2)}, u32[]{:S(2)}) collective-permute-start(bf16[128,4096]{1,0:T(8,128)(2,1)S(1)} %get-tuple-element.28), channel_id=1, source_target_pairs={{0,1},{1,0},{2,3},{3,2},{4,5},{5,4},{6,7},{7,6},{8,9},{9,8},{10,11... | collective-permute-start | bytes 3145736 | tf_op jit(solution)/shard_map/ppermute | solution.py:290
  54.3 0.7 shard_map.100.keep_ref
  55.0 1.5 %collective-permute-done.1.got_ref = bf16[128,4096]{1,0:T(8,128)(2,1)S(1)} collective-permute-done((bf16[128,4096]{1,0:T(8,128)(2,1)S(1)}, bf16[128,4096]{1,0:T(8,128)(2,1)S(1)}, u32[]{:S(2)}, u32[]{:S(2)}) %collective-permute-start.1) | collective-permute-done | bytes 1048608 | tf_op jit(solution)/shard_map/ppermute | solution.py:290
  56.5 0.1 shard_map.103
  56.6 3.6 %collective-permute-start.4 = (bf16[16,4096]{1,0:T(8,128)(2,1)S(1)}, bf16[16,4096]{1,0:T(8,128)(2,1)S(1)}, u32[]{:S(2)}, u32[]{:S(2)}) collective-permute-start(bf16[16,4096]{1,0:T(8,128)(2,1)S(1)} %get-tuple-element.35), channel_id=1, source_target_pairs={{0,6},{1,7},{2,4},{3,5},{4,2},{5,3},{6,0},{7,1},{8,14},{9,15},{10,... | collective-permute-start | bytes 393224 | tf_op jit(solution)/shard_map/ppermute | solution.py:297
  60.2 2.4 %collective-permute-start.5 = (bf16[16,4096]{1,0:T(8,128)(2,1)S(1)}, bf16[16,4096]{1,0:T(8,128)(2,1)S(1)}, u32[]{:S(2)}, u32[]{:S(2)}) collective-permute-start(bf16[16,4096]{1,0:T(8,128)(2,1)S(1)} %get-tuple-element.36), channel_id=1, source_target_pairs={{0,4},{1,5},{2,6},{3,7},{4,0},{5,1},{6,2},{7,3},{8,12},{9,13},{10,... | collective-permute-start | bytes 393224 | tf_op jit(solution)/shard_map/ppermute | solution.py:297
  62.6 3.4 %collective-permute-start.6 = (bf16[16,4096]{1,0:T(8,128)(2,1)S(1)}, bf16[16,4096]{1,0:T(8,128)(2,1)S(1)}, u32[]{:S(2)}, u32[]{:S(2)}) collective-permute-start(bf16[16,4096]{1,0:T(8,128)(2,1)S(1)} %get-tuple-element.37), channel_id=1, source_target_pairs={{0,2},{1,3},{2,0},{3,1},{4,6},{5,7},{6,4},{7,5},{8,10},{9,11},{10,... | collective-permute-start | bytes 393224 | tf_op jit(solution)/shard_map/ppermute | solution.py:297
  65.9 0.1 shard_map.101
  66.0 1.9 %collective-permute-start.2 = (bf16[32,4096]{1,0:T(8,128)(2,1)S(1)}, bf16[32,4096]{1,0:T(8,128)(2,1)S(1)}, u32[]{:S(2)}, u32[]{:S(2)}) collective-permute-start(bf16[32,4096]{1,0:T(8,128)(2,1)S(1)} %get-tuple-element.31), channel_id=1, source_target_pairs={{0,2},{1,3},{2,0},{3,1},{4,6},{5,7},{6,4},{7,5},{8,10},{9,11},{10,... | collective-permute-start | bytes 786440 | tf_op jit(solution)/shard_map/ppermute | solution.py:304
  68.0 0.0 collective-permute-done.4.a_ref
  68.0 4.4 %collective-permute-done.5.b_ref = bf16[16,4096]{1,0:T(8,128)(2,1)S(1)} collective-permute-done((bf16[16,4096]{1,0:T(8,128)(2,1)S(1)}, bf16[16,4096]{1,0:T(8,128)(2,1)S(1)}, u32[]{:S(2)}, u32[]{:S(2)}) %collective-permute-start.5) | collective-permute-done | bytes 131104 | tf_op jit(solution)/shard_map/ppermute | solution.py:297
  72.4 0.0 collective-permute-done.6.c_ref
  72.4 0.0 copy-start.4
  72.4 0.0 copy-start.6
  72.4 0.1 shard_map.104
  72.4 7.7 %collective-permute-start.7 = (bf16[16,4096]{1,0:T(8,128)(2,1)S(1)}, bf16[16,4096]{1,0:T(8,128)(2,1)S(1)}, u32[]{:S(2)}, u32[]{:S(2)}) collective-permute-start(bf16[16,4096]{1,0:T(8,128)(2,1)S(1)} %shard_map.104), channel_id=1, source_target_pairs={{0,8},{1,9},{2,10},{3,11},{4,12},{5,13},{6,14},{7,15},{8,0},{9,1},... | collective-permute-start | bytes 393224 | tf_op jit(solution)/shard_map/ppermute | solution.py:306
  80.1 0.0 collective-permute-done.2.got_ref
  80.1 0.0 copy-done.4
  80.1 0.1 shard_map.102
  80.2 2.2 %collective-permute-start.3 = (bf16[16,4096]{1,0:T(8,128)(2,1)S(1)}, bf16[16,4096]{1,0:T(8,128)(2,1)S(1)}, u32[]{:S(2)}, u32[]{:S(2)}) collective-permute-start(bf16[16,4096]{1,0:T(8,128)(2,1)S(1)} %get-tuple-element.33), channel_id=1, source_target_pairs={{0,4},{1,5},{2,6},{3,7},{4,0},{5,1},{6,2},{7,3},{8,12},{9,13},{10,... | collective-permute-start | bytes 393224 | tf_op jit(solution)/shard_map/ppermute | solution.py:310
  82.4 6.5 %collective-permute-done.7.far_ref = bf16[16,4096]{1,0:T(8,128)(2,1)S(1)} collective-permute-done((bf16[16,4096]{1,0:T(8,128)(2,1)S(1)}, bf16[16,4096]{1,0:T(8,128)(2,1)S(1)}, u32[]{:S(2)}, u32[]{:S(2)}) %collective-permute-start.7) | collective-permute-done | bytes 131104 | tf_op jit(solution)/shard_map/ppermute | solution.py:306
  88.9 6.2 %collective-permute-done.3.near_ref = bf16[16,4096]{1,0:T(8,128)(2,1)S(1)} collective-permute-done((bf16[16,4096]{1,0:T(8,128)(2,1)S(1)}, bf16[16,4096]{1,0:T(8,128)(2,1)S(1)}, u32[]{:S(2)}, u32[]{:S(2)}) %collective-permute-start.3) | collective-permute-done | bytes 131104 | tf_op jit(solution)/shard_map/ppermute | solution.py:310
  95.1 0.0 copy-done.6
  95.1 0.8 shard_map.105
Async XLA Ops:
  2.4 22.9 %collective-permute-start = (bf16[392,128]{1,0:T(8,128)(2,1)S(1)}, bf16[392,128]{1,0:T(8,128)(2,1)S(1)}, u32[]{:S(2)}, u32[]{:S(2)}) collective-permute-start(bf16[392,128]{1,0:T(8,128)(2,1)S(1)} %shard_map.95.own_ref), channel_id=1, source_target_pairs={{0,16},{16,0},{32,48},{48,32},{64,80},{80,64},{96,112},{112,96},{1... | collective-permute-start | bytes 301064 | tf_op jit(solution)/shard_map/ppermute | solution.py:269
  18.7 0.9 copy-start
  19.6 0.9 copy-start.2
  20.5 0.9 copy-start.3
  21.4 0.7 copy-start.5
  22.1 0.7 copy-start.7
  22.8 24.3 %copy-start.1 = (bf16[256,384]{1,0:T(8,128)(2,1)S(1)}, bf16[256,384]{1,0:T(8,128)(2,1)}, u32[]{:S(2)}) copy-start(bf16[256,384]{1,0:T(8,128)(2,1)} %query_ref.2) | copy-start | bytes 589828
  48.8 7.7 %collective-permute-start.1 = (bf16[128,4096]{1,0:T(8,128)(2,1)S(1)}, bf16[128,4096]{1,0:T(8,128)(2,1)S(1)}, u32[]{:S(2)}, u32[]{:S(2)}) collective-permute-start(bf16[128,4096]{1,0:T(8,128)(2,1)S(1)} %get-tuple-element.28), channel_id=1, source_target_pairs={{0,1},{1,0},{2,3},{3,2},{4,5},{5,4},{6,7},{7,6},{8,9},{9,8},{10,11... | collective-permute-start | bytes 3145736 | tf_op jit(solution)/shard_map/ppermute | solution.py:290
  56.6 11.3 %collective-permute-start.4 = (bf16[16,4096]{1,0:T(8,128)(2,1)S(1)}, bf16[16,4096]{1,0:T(8,128)(2,1)S(1)}, u32[]{:S(2)}, u32[]{:S(2)}) collective-permute-start(bf16[16,4096]{1,0:T(8,128)(2,1)S(1)} %get-tuple-element.35), channel_id=1, source_target_pairs={{0,6},{1,7},{2,4},{3,5},{4,2},{5,3},{6,0},{7,1},{8,14},{9,15},{10,... | collective-permute-start | bytes 393224 | tf_op jit(solution)/shard_map/ppermute | solution.py:297
  60.2 12.1 %collective-permute-start.5 = (bf16[16,4096]{1,0:T(8,128)(2,1)S(1)}, bf16[16,4096]{1,0:T(8,128)(2,1)S(1)}, u32[]{:S(2)}, u32[]{:S(2)}) collective-permute-start(bf16[16,4096]{1,0:T(8,128)(2,1)S(1)} %get-tuple-element.36), channel_id=1, source_target_pairs={{0,4},{1,5},{2,6},{3,7},{4,0},{5,1},{6,2},{7,3},{8,12},{9,13},{10,... | collective-permute-start | bytes 393224 | tf_op jit(solution)/shard_map/ppermute | solution.py:297
  62.6 9.8 %collective-permute-start.6 = (bf16[16,4096]{1,0:T(8,128)(2,1)S(1)}, bf16[16,4096]{1,0:T(8,128)(2,1)S(1)}, u32[]{:S(2)}, u32[]{:S(2)}) collective-permute-start(bf16[16,4096]{1,0:T(8,128)(2,1)S(1)} %get-tuple-element.37), channel_id=1, source_target_pairs={{0,2},{1,3},{2,0},{3,1},{4,6},{5,7},{6,4},{7,5},{8,10},{9,11},{10,... | collective-permute-start | bytes 393224 | tf_op jit(solution)/shard_map/ppermute | solution.py:297
  66.0 14.1 %collective-permute-start.2 = (bf16[32,4096]{1,0:T(8,128)(2,1)S(1)}, bf16[32,4096]{1,0:T(8,128)(2,1)S(1)}, u32[]{:S(2)}, u32[]{:S(2)}) collective-permute-start(bf16[32,4096]{1,0:T(8,128)(2,1)S(1)} %get-tuple-element.31), channel_id=1, source_target_pairs={{0,2},{1,3},{2,0},{3,1},{4,6},{5,7},{6,4},{7,5},{8,10},{9,11},{10,... | collective-permute-start | bytes 786440 | tf_op jit(solution)/shard_map/ppermute | solution.py:304
  72.4 7.8 %copy-start.4 = (bf16[16,4096]{1,0:T(8,128)(2,1)S(1)}, bf16[16,4096]{1,0:T(8,128)(2,1)}, u32[]{:S(2)}) copy-start(bf16[16,4096]{1,0:T(8,128)(2,1)} %residual_ref.1) | copy-start | bytes 393220
  72.4 22.7 %copy-start.6 = (f32[4096]{0:T(1024)S(1)}, f32[4096]{0:T(1024)}, u32[]{:S(2)}) copy-start(f32[4096]{0:T(1024)} %param.15) | copy-start | bytes 49156
  72.4 16.4 %collective-permute-start.7 = (bf16[16,4096]{1,0:T(8,128)(2,1)S(1)}, bf16[16,4096]{1,0:T(8,128)(2,1)S(1)}, u32[]{:S(2)}, u32[]{:S(2)}) collective-permute-start(bf16[16,4096]{1,0:T(8,128)(2,1)S(1)} %shard_map.104), channel_id=1, source_target_pairs={{0,8},{1,9},{2,10},{3,11},{4,12},{5,13},{6,14},{7,15},{8,0},{9,1},... | collective-permute-start | bytes 393224 | tf_op jit(solution)/shard_map/ppermute | solution.py:306
  80.2 14.9 %collective-permute-start.3 = (bf16[16,4096]{1,0:T(8,128)(2,1)S(1)}, bf16[16,4096]{1,0:T(8,128)(2,1)S(1)}, u32[]{:S(2)}, u32[]{:S(2)}) collective-permute-start(bf16[16,4096]{1,0:T(8,128)(2,1)S(1)} %get-tuple-element.33), channel_id=1, source_target_pairs={{0,4},{1,5},{2,6},{3,7},{4,0},{5,1},{6,2},{7,3},{8,12},{9,13},{10,... | collective-permute-start | bytes 393224 | tf_op jit(solution)/shard_map/ppermute | solution.py:310

commit v11 on v9

--- a/solution.py
+++ b/solution.py
@@ -15,7 +15,20 @@
 BF16 = jnp.bfloat16
 
 SHARDS = 32
-FLIP_Z = [(i, i ^ 1) for i in range(SHARDS)]
+TP = 16
+
+
+def hop_z(core, steps):
+    pairs = []
+    for place in range(SHARDS // 2):
+        for z in range(TP):
+            to = (z + steps) % TP
+            pairs.append(
+                tuple((place * 2 + a // 8) * TP + a % 8 * 2 + core for a in (z, to))
+            )
+    return pairs
+
+
 ROW_Y = [[g + 2 * k for k in range(4)] for g in range(SHARDS) if g & 6 == 0]
 ROW_X = [[g + 8 * k for k in range(4)] for g in range(8)]
 FAR_ORDER = (0, 3, 2, 1)
@@ -121,7 +134,8 @@
     return jnp.concatenate([high, low, jnp.zeros((2, HDIM), F32)], axis=0).astype(BF16)
 
 
-def pair_kernel(place_ref, own_ref, other_ref, out_ref):
+def pair_kernel(place_ref, own_ref, straight_ref, around_ref, out_ref, other_ref):
+    other_ref[...] = jnp.where(place_ref[1] & 1 == 1, around_ref[...], straight_ref[...])
     odd = place_ref[0] & 1 == 1
     own_a, other_a = decays(own_ref[STATE:, :]), decays(other_ref[STATE:, :])
     later_a = jnp.where(odd, own_a, other_a)
@@ -270,7 +284,9 @@
         ],
     )
     late_query = lax.optimization_barrier((local, query_rows))[1]
-    other = lax.ppermute(local, "seq", FLIP_Z)
+    straight = lax.ppermute(local, ("seq", "tp"), hop_z(0, 8))
+    halfway = lax.ppermute(local, ("seq", "tp"), hop_z(1, -4))
+    around = lax.ppermute(halfway, ("seq", "tp"), hop_z(1, -4))
     intra, carry, weight = call(
         intra_kernel,
         (of((SPAN, STATE), F32), of((SPAN, HEADS), F32), pltpu.VMEM((STATE, D), BF16)),
@@ -279,9 +295,12 @@
         pltpu.with_memory_space_constraint(out_weight, pltpu.HBM),
         scratch=[pltpu.SemaphoreType.DMA],
     )
-    other, intra, carry = lax.optimization_barrier((other, intra, carry))
+    straight, around, intra, carry = lax.optimization_barrier((straight, around, intra, carry))
     four = of((4, PAYLOAD, HDIM), BF16)
-    pairs = call(pair_kernel, four, [SMEM, VMEM, VMEM], place, local, other)
+    pairs, other = call(
+        pair_kernel, (four, of((PAYLOAD, HDIM), BF16)), [SMEM] + [VMEM] * 3,
+        place, local, straight, around,
+    )
     rows = lax.all_to_all(pairs, "seq", 0, 0, axis_index_groups=ROW_Y)
     totals = call(row_kernel, four, [VMEM], rows)
     cols = lax.all_to_all(totals, "seq", 0, 0, axis_index_groups=ROW_X)

time: 93.8 us -> 97.6 us (1.041)
  the two profiles are of different devices: /device:TPU:64 before, /device:TPU:1 now
where the time goes in v11:
time: 97.6 us; the launch traced here: 97 us
  starting transfers between devices  37.7 us (39%)
  waiting for transfers between devices  24.7 us (25%)
  blocking collectives  20.3 us (21%)
  Pallas kernels  9.22 us (9%)
  local copies, waits for them, and re-layouts  4.13 us (4%)
    all_to_all x1, waiting for transfers between devices, shards(): near = lax.all_to_all(near, 'tp', 0, 0, axis_index_groups=NEAR_CHIPS)  14.4 us
    ppermute x1, starting transfers between devices, shards(): halfway = lax.ppermute(local, ('seq', 'tp'), hop_z(1, -4))  13.3 us
    all_to_all x1, blocking collectives, shards(): rows = lax.all_to_all(pairs, 'seq', 0, 0, axis_index_groups=ROW_Y)  10.3 us
    all_to_all x1, blocking collectives, shards(): cols = lax.all_to_all(totals, 'seq', 0, 0, axis_index_groups=ROW_X)  10.1 us
    ppermute x3, starting transfers between devices, shards(): lax.ppermute(sent, 'tp', [(i, i ^ 2 * k) for i in range(16)])  9.27 us
    pallas_call x11, Pallas kernels, call(): pl.pallas_call(body, out_shape=shapes, in_specs=specs, out_specs=jax.tree...  9.22 us
    ppermute x1, waiting for transfers between devices, shards(): around = lax.ppermute(halfway, ('seq', 'tp'), hop_z(1, -4))  6.99 us
    ppermute x1, starting transfers between devices, shards(): around = lax.ppermute(halfway, ('seq', 'tp'), hop_z(1, -4))  5.43 us
  transfers between devices with their start and end apart: 9, of which 4 were waited for; matrix products, arithmetic and copies ran while one was open for 0% of the time, Pallas kernels for 4%

profile of v11, /device:TPU:1, one launch (start us, length us, event | category | flops | bytes accessed | tf_op | source)
XLA Modules:
  0.0 97.0 jit_solution(16604180379551736791)
XLA Ops:
  0.6 1.7 %shard_map.95.own_ref = bf16[392,128]{1,0:T(8,128)(2,1)S(1)} custom-call(s32[1,3]{1,0:T(1,128)} %starts_ref.1, f32[3,256]{1,0:T(4,128)} %decay_ref.1, bf16[256,384]{1,0:T(8,128)(2,1)} %key_ref.1, bf16[256,384]{1,0:T(8,128)(2,1)} %value_ref.1), custom_call_target="tpu_custom_call" | custom-call | tf_op jit(solution)/shard_map/pallas_call | solution.py:252
  2.4 13.3 %collective-permute-start.1 = (bf16[392,128]{1,0:T(8,128)(2,1)S(1)}, bf16[392,128]{1,0:T(8,128)(2,1)S(1)}, u32[]{:S(2)}, u32[]{:S(2)}) collective-permute-start(bf16[392,128]{1,0:T(8,128)(2,1)S(1)} %shard_map.95.own_ref), channel_id=1, source_target_pairs={{1,25},{3,27},{5,29},{7,31},{9,1},{11,3},{13,5},{15,7},{17,9},{19,... | collective-permute-start | bytes 301064 | tf_op jit(solution)/shard_map/ppermute | solution.py:288
  15.7 0.7 collective-permute-start
  16.3 0.0 copy-start
  16.4 0.9 copy-done
  17.3 0.0 copy-start.2
  17.3 0.9 copy-done.2
  18.2 0.0 copy-start.3
  18.2 0.9 copy-done.3
  19.1 0.0 copy-start.5
  19.1 0.7 copy-done.5
  19.8 0.0 copy-start.7
  19.8 0.7 copy-done.7
  20.5 0.0 copy-start.1
  20.5 2.4 %shard_map.96 = (f32[256,384]{1,0:T(8,128)S(1)}, f32[256,3]{1,0:T(8,128)S(1)}, bf16[384,4096]{1,0:T(8,128)(2,1)S(1)}) custom-call(s32[1,3]{1,0:T(1,128)S(1)} %copy-done.7, f32[3,256]{1,0:T(4,128)S(1)} %copy-done.5, bf16[256,384]{1,0:T(8,128)(2,1)S(1)} %copy-done, bf16[256,384]{1,0:T(8,128)(2,1)S(1)} %copy-done.2, bf16[256,384]{1,0:T(8,128)(2,1)S(1)} %copy-done.3, ...), custom_call_target="tpu_custom_call" | custom-call | tf_op jit(solution)/shard_map/pallas_call | solution.py:252
  22.9 0.0 collective-permute-done.1
  22.9 5.4 %collective-permute-start.2 = (bf16[392,128]{1,0:T(8,128)(2,1)S(1)}, bf16[392,128]{1,0:T(8,128)(2,1)S(1)}, u32[]{:S(2)}, u32[]{:S(2)}) collective-permute-start(bf16[392,128]{1,0:T(8,128)(2,1)S(1)} %collective-permute-done.1), channel_id=1, source_target_pairs={{1,25},{3,27},{5,29},{7,31},{9,1},{11,3},{13,5},{15,7},{17,9},{19,... | collective-permute-start | bytes 301064 | tf_op jit(solution)/shard_map/ppermute | solution.py:289
  28.4 0.1 pad_add_fusion.place_ref
  28.4 0.0 collective-permute-done.straight_ref
  28.5 7.0 %collective-permute-done.2.around_ref = bf16[392,128]{1,0:T(8,128)(2,1)S(1)} collective-permute-done((bf16[392,128]{1,0:T(8,128)(2,1)S(1)}, bf16[392,128]{1,0:T(8,128)(2,1)S(1)}, u32[]{:S(2)}, u32[]{:S(2)}) %collective-permute-start.2) | collective-permute-done | bytes 100384 | tf_op jit(solution)/shard_map/ppermute | solution.py:289
  35.4 0.6 shard_map.97
  36.1 10.3 %all_to_all.15.parts_ref.row_ref = bf16[4,392,128]{2,1,0:T(8,128)(2,1)S(1)} all-to-all(bf16[4,392,128]{2,1,0:T(8,128)(2,1)S(1)} %get-tuple-element.26), channel_id=1, replica_groups={{0,32,64,96},{16,48,80,112},{128,160,192,224},{144,176,208,240},{256,28..., dimensions={0} | all-to-all | bytes 802816 | tf_op jit(solution)/shard_map/all_to_all | solution.py:304
  46.3 0.1 shard_map.98
  46.4 10.1 %all_to_all.16.col_ref = bf16[4,392,128]{2,1,0:T(8,128)(2,1)S(1)} all-to-all(bf16[4,392,128]{2,1,0:T(8,128)(2,1)S(1)} %shard_map.98), channel_id=1, replica_groups={{0,128,256,384},{16,144,272,400},{32,160,288,416},{48,176,304,432},{64,..., dimensions={0} | all-to-all | bytes 802816 | tf_op jit(solution)/shard_map/all_to_all | solution.py:306
  56.5 0.0 copy-done.1
  56.5 1.7 %shard_map.99 = (bf16[128,4096]{1,0:T(8,128)(2,1)S(1)}, bf16[128,384]{1,0:T(8,128)(2,1)S(1)}) custom-call(s32[2]{0:T(128)S(1)} %pad_add_fusion.place_ref, bf16[256,384]{1,0:T(8,128)(2,1)S(1)} %copy-done.1, f32[256,384]{1,0:T(8,128)S(1)} %get-tuple-element.21.intra_ref, f32[256,3]{1,0:T(8,128)S(1)} %get-tuple-element.22.carry_ref, ...), custom_call_target="tpu_custom_call" | custom-call | tf_op jit(solution)/shard_map/pallas_call | solution.py:252
  58.3 1.9 %collective-permute-start.3 = (bf16[128,4096]{1,0:T(8,128)(2,1)S(1)}, bf16[128,4096]{1,0:T(8,128)(2,1)S(1)}, u32[]{:S(2)}, u32[]{:S(2)}) collective-permute-start(bf16[128,4096]{1,0:T(8,128)(2,1)S(1)} %get-tuple-element.29), channel_id=1, source_target_pairs={{0,1},{1,0},{2,3},{3,2},{4,5},{5,4},{6,7},{7,6},{8,9},{9,8},{10,11... | collective-permute-start | bytes 3145736 | tf_op jit(solution)/shard_map/ppermute | solution.py:313
  60.2 0.7 shard_map.100.keep_ref
  60.9 1.9 %collective-permute-done.3.got_ref = bf16[128,4096]{1,0:T(8,128)(2,1)S(1)} collective-permute-done((bf16[128,4096]{1,0:T(8,128)(2,1)S(1)}, bf16[128,4096]{1,0:T(8,128)(2,1)S(1)}, u32[]{:S(2)}, u32[]{:S(2)}) %collective-permute-start.3) | collective-permute-done | bytes 1048608 | tf_op jit(solution)/shard_map/ppermute | solution.py:313
  62.8 0.1 shard_map.103
  62.9 1.9 %collective-permute-start.4 = (bf16[16,4096]{1,0:T(8,128)(2,1)S(1)}, bf16[16,4096]{1,0:T(8,128)(2,1)S(1)}, u32[]{:S(2)}, u32[]{:S(2)}) collective-permute-start(bf16[16,4096]{1,0:T(8,128)(2,1)S(1)} %get-tuple-element.31), channel_id=1, source_target_pairs={{0,6},{1,7},{2,4},{3,5},{4,2},{5,3},{6,0},{7,1},{8,14},{9,15},{10,... | collective-permute-start | bytes 393224 | tf_op jit(solution)/shard_map/ppermute | solution.py:320
  64.8 2.8 %collective-permute-start.5 = (bf16[16,4096]{1,0:T(8,128)(2,1)S(1)}, bf16[16,4096]{1,0:T(8,128)(2,1)S(1)}, u32[]{:S(2)}, u32[]{:S(2)}) collective-permute-start(bf16[16,4096]{1,0:T(8,128)(2,1)S(1)} %get-tuple-element.32), channel_id=1, source_target_pairs={{0,4},{1,5},{2,6},{3,7},{4,0},{5,1},{6,2},{7,3},{8,12},{9,13},{10,... | collective-permute-start | bytes 393224 | tf_op jit(solution)/shard_map/ppermute | solution.py:320
  67.7 4.5 %collective-permute-start.6 = (bf16[16,4096]{1,0:T(8,128)(2,1)S(1)}, bf16[16,4096]{1,0:T(8,128)(2,1)S(1)}, u32[]{:S(2)}, u32[]{:S(2)}) collective-permute-start(bf16[16,4096]{1,0:T(8,128)(2,1)S(1)} %get-tuple-element.33), channel_id=1, source_target_pairs={{0,2},{1,3},{2,0},{3,1},{4,6},{5,7},{6,4},{7,5},{8,10},{9,11},{10,... | collective-permute-start | bytes 393224 | tf_op jit(solution)/shard_map/ppermute | solution.py:320
  72.2 0.9 shard_map.101
  73.1 3.5 %all-to-all-start.2 = ((bf16[4,16,4096]{2,1,0:T(8,128)(2,1)}), bf16[4,16,4096]{2,1,0:T(8,128)(2,1)S(1)}, u32[]{:S(2)}, u32[]{:S(2)}) async-start(bf16[4,16,4096]{2,1,0:T(8,128)(2,1)} %shard_map.101), calls=%async_computation.2 | async-start | bytes 1048576 | tf_op jit(solution)/shard_map/all_to_all | solution.py:327
  76.6 0.0 collective-permute-done.4.a_ref
  76.6 1.4 %collective-permute-done.5.b_ref = bf16[16,4096]{1,0:T(8,128)(2,1)S(1)} collective-permute-done((bf16[16,4096]{1,0:T(8,128)(2,1)S(1)}, bf16[16,4096]{1,0:T(8,128)(2,1)S(1)}, u32[]{:S(2)}, u32[]{:S(2)}) %collective-permute-start.5) | collective-permute-done | bytes 131104 | tf_op jit(solution)/shard_map/ppermute | solution.py:320
  77.9 0.0 collective-permute-done.6.c_ref
  77.9 0.0 copy-start.4
  77.9 0.0 copy-start.6
  77.9 0.1 shard_map.104
  78.0 3.7 %collective-permute-start.7 = (bf16[16,4096]{1,0:T(8,128)(2,1)S(1)}, bf16[16,4096]{1,0:T(8,128)(2,1)S(1)}, u32[]{:S(2)}, u32[]{:S(2)}) collective-permute-start(bf16[16,4096]{1,0:T(8,128)(2,1)S(1)} %shard_map.104), channel_id=1, source_target_pairs={{0,8},{1,9},{2,10},{3,11},{4,12},{5,13},{6,14},{7,15},{8,0},{9,1},... | collective-permute-start | bytes 393224 | tf_op jit(solution)/shard_map/ppermute | solution.py:329
  81.7 14.4 %all-to-all-done.2.parts_ref = bf16[4,16,4096]{2,1,0:T(8,128)(2,1)S(1)} async-done(((bf16[4,16,4096]{2,1,0:T(8,128)(2,1)}), bf16[4,16,4096]{2,1,0:T(8,128)(2,1)S(1)}, u32[]{:S(2)}, u32[]{:S(2)}) %all-to-all-start.2) | async-done | bytes 524320 | tf_op jit(solution)/shard_map/all_to_all | solution.py:327
  96.1 0.0 copy-done.4
  96.1 0.1 shard_map.102.near_ref
  96.2 0.0 collective-permute-done.7.far_ref
  96.2 0.0 copy-done.6
  96.2 0.8 shard_map.105
Async XLA Ops:
  2.4 20.6 %collective-permute-start.1 = (bf16[392,128]{1,0:T(8,128)(2,1)S(1)}, bf16[392,128]{1,0:T(8,128)(2,1)S(1)}, u32[]{:S(2)}, u32[]{:S(2)}) collective-permute-start(bf16[392,128]{1,0:T(8,128)(2,1)S(1)} %shard_map.95.own_ref), channel_id=1, source_target_pairs={{1,25},{3,27},{5,29},{7,31},{9,1},{11,3},{13,5},{15,7},{17,9},{19,... | collective-permute-start | bytes 301064 | tf_op jit(solution)/shard_map/ppermute | solution.py:288
  15.7 12.8 %collective-permute-start = (bf16[392,128]{1,0:T(8,128)(2,1)S(1)}, bf16[392,128]{1,0:T(8,128)(2,1)S(1)}, u32[]{:S(2)}, u32[]{:S(2)}) collective-permute-start(bf16[392,128]{1,0:T(8,128)(2,1)S(1)} %shard_map.95.own_ref), channel_id=1, source_target_pairs={{0,16},{2,18},{4,20},{6,22},{8,24},{10,26},{12,28},{14,30},{16,0},... | collective-permute-start | bytes 301064 | tf_op jit(solution)/shard_map/ppermute | solution.py:287
  16.3 0.9 copy-start
  17.3 0.9 copy-start.2
  18.2 0.9 copy-start.3
  19.1 0.7 copy-start.5
  19.8 0.7 copy-start.7
  20.5 36.0 %copy-start.1 = (bf16[256,384]{1,0:T(8,128)(2,1)S(1)}, bf16[256,384]{1,0:T(8,128)(2,1)}, u32[]{:S(2)}) copy-start(bf16[256,384]{1,0:T(8,128)(2,1)} %query_ref.2) | copy-start | bytes 589828
  22.9 12.5 %collective-permute-start.2 = (bf16[392,128]{1,0:T(8,128)(2,1)S(1)}, bf16[392,128]{1,0:T(8,128)(2,1)S(1)}, u32[]{:S(2)}, u32[]{:S(2)}) collective-permute-start(bf16[392,128]{1,0:T(8,128)(2,1)S(1)} %collective-permute-done.1), channel_id=1, source_target_pairs={{1,25},{3,27},{5,29},{7,31},{9,1},{11,3},{13,5},{15,7},{17,9},{19,... | collective-permute-start | bytes 301064 | tf_op jit(solution)/shard_map/ppermute | solution.py:289
  58.3 4.6 %collective-permute-start.3 = (bf16[128,4096]{1,0:T(8,128)(2,1)S(1)}, bf16[128,4096]{1,0:T(8,128)(2,1)S(1)}, u32[]{:S(2)}, u32[]{:S(2)}) collective-permute-start(bf16[128,4096]{1,0:T(8,128)(2,1)S(1)} %get-tuple-element.29), channel_id=1, source_target_pairs={{0,1},{1,0},{2,3},{3,2},{4,5},{5,4},{6,7},{7,6},{8,9},{9,8},{10,11... | collective-permute-start | bytes 3145736 | tf_op jit(solution)/shard_map/ppermute | solution.py:313
  62.9 13.7 %collective-permute-start.4 = (bf16[16,4096]{1,0:T(8,128)(2,1)S(1)}, bf16[16,4096]{1,0:T(8,128)(2,1)S(1)}, u32[]{:S(2)}, u32[]{:S(2)}) collective-permute-start(bf16[16,4096]{1,0:T(8,128)(2,1)S(1)} %get-tuple-element.31), channel_id=1, source_target_pairs={{0,6},{1,7},{2,4},{3,5},{4,2},{5,3},{6,0},{7,1},{8,14},{9,15},{10,... | collective-permute-start | bytes 393224 | tf_op jit(solution)/shard_map/ppermute | solution.py:320
  64.8 13.1 %collective-permute-start.5 = (bf16[16,4096]{1,0:T(8,128)(2,1)S(1)}, bf16[16,4096]{1,0:T(8,128)(2,1)S(1)}, u32[]{:S(2)}, u32[]{:S(2)}) collective-permute-start(bf16[16,4096]{1,0:T(8,128)(2,1)S(1)} %get-tuple-element.32), channel_id=1, source_target_pairs={{0,4},{1,5},{2,6},{3,7},{4,0},{5,1},{6,2},{7,3},{8,12},{9,13},{10,... | collective-permute-start | bytes 393224 | tf_op jit(solution)/shard_map/ppermute | solution.py:320
  67.7 10.3 %collective-permute-start.6 = (bf16[16,4096]{1,0:T(8,128)(2,1)S(1)}, bf16[16,4096]{1,0:T(8,128)(2,1)S(1)}, u32[]{:S(2)}, u32[]{:S(2)}) collective-permute-start(bf16[16,4096]{1,0:T(8,128)(2,1)S(1)} %get-tuple-element.33), channel_id=1, source_target_pairs={{0,2},{1,3},{2,0},{3,1},{4,6},{5,7},{6,4},{7,5},{8,10},{9,11},{10,... | collective-permute-start | bytes 393224 | tf_op jit(solution)/shard_map/ppermute | solution.py:320
  73.1 23.1 %all-to-all-start.2 = ((bf16[4,16,4096]{2,1,0:T(8,128)(2,1)}), bf16[4,16,4096]{2,1,0:T(8,128)(2,1)S(1)}, u32[]{:S(2)}, u32[]{:S(2)}) async-start(bf16[4,16,4096]{2,1,0:T(8,128)(2,1)} %shard_map.101), calls=%async_computation.2 | async-start | bytes 1048576 | tf_op jit(solution)/shard_map/all_to_all | solution.py:327
  77.9 18.2 %copy-start.4 = (bf16[16,4096]{1,0:T(8,128)(2,1)S(1)}, bf16[16,4096]{1,0:T(8,128)(2,1)}, u32[]{:S(2)}) copy-start(bf16[16,4096]{1,0:T(8,128)(2,1)} %residual_ref.1) | copy-start | bytes 393220
  77.9 18.3 %copy-start.6 = (f32[4096]{0:T(1024)S(1)}, f32[4096]{0:T(1024)}, u32[]{:S(2)}) copy-start(f32[4096]{0:T(1024)} %param.15) | copy-start | bytes 49156
  78.0 18.2 %collective-permute-start.7 = (bf16[16,4096]{1,0:T(8,128)(2,1)S(1)}, bf16[16,4096]{1,0:T(8,128)(2,1)S(1)}, u32[]{:S(2)}, u32[]{:S(2)}) collective-permute-start(bf16[16,4096]{1,0:T(8,128)(2,1)S(1)} %shard_map.104), channel_id=1, source_target_pairs={{0,8},{1,9},{2,10},{3,11},{4,12},{5,13},{6,14},{7,15},{8,0},{9,1},... | collective-permute-start | bytes 393224 | tf_op jit(solution)/shard_map/ppermute | solution.py:329

commit v12 on v8

--- a/solution.py
+++ b/solution.py
@@ -1,3 +1,5 @@
+import functools
+
 import jax
 import jax.numpy as jnp
 from jax import lax
@@ -18,8 +20,8 @@
 FLIP_Z = [(i, i ^ 1) for i in range(SHARDS)]
 ROW_Y = [[g + 2 * k for k in range(4)] for g in range(SHARDS) if g & 6 == 0]
 ROW_X = [[g + 8 * k for k in range(4)] for g in range(8)]
+FAR_ORDER, NEAR_ORDER = (0, 3, 2, 1), (1, 3, 2, 0)
 LONG = pl.CostEstimate(flops=10**11, bytes_accessed=0, transcendentals=0)
-NEAR_CHIPS = [[8 * g + 2 * k + core for k in range(4)] for g in range(2) for core in range(2)]
 
 VMEM = pl.BlockSpec(memory_space=pltpu.VMEM)
 HBM = pl.BlockSpec(memory_space=pltpu.HBM)
@@ -183,7 +185,7 @@
         mixed_ref[:, cut] = (mixed * scale).astype(BF16)
     core, chip = place_ref[1] & 1, place_ref[1] >> 1
     for k in range(8):
-        start = ((chip & 4) + (k & 3) if k & 4 else chip ^ 4 ^ k) * 32
+        start = (chip ^ NEAR_ORDER[k - 4] if k & 4 else chip ^ 4 ^ FAR_ORDER[k]) * 32
         cut = slice(k * 16, (k + 1) * 16)
         own, sibling = start + core * 16, start + (1 - core) * 16
         keep_ref[cut, :] = mixed_ref[pl.ds(pl.multiple_of(own, 16), 16), :]
@@ -197,33 +199,21 @@
     out_ref[...] = jnp.dot(own_ref[...], weight_ref[...], preferred_element_type=F32)
 
 
-def far_kernel(keep_ref, got_ref, *out_refs):
-    for k, ref in enumerate(out_refs):
-        cut = slice(k * 16, (k + 1) * 16)
+def slab_kernel(slabs, keep_ref, got_ref, *out_refs):
+    for (start, stop), ref in zip(slabs, out_refs):
+        cut = slice(start, stop)
         ref[...] = (keep_ref[cut, :] + got_ref[cut, :].astype(F32)).astype(ref.dtype)
 
 
-def near_kernel(keep_ref, got_ref, out_ref, sum_ref, sems):
-    copies = []
-    for k in range(4):
-        cut = slice(64 + k * 16, 80 + k * 16)
-        sum_ref[k] = (keep_ref[cut, :] + got_ref[cut, :].astype(F32)).astype(BF16)
-        copies.append(pltpu.make_async_copy(sum_ref.at[k], out_ref.at[k], sems.at[k]))
-        copies[-1].start()
-    for copy in copies:
-        copy.wait()
-
-
 def sum_kernel(own_ref, a_ref, b_ref, c_ref, out_ref):
-    total = own_ref[...] + a_ref[...].astype(F32) + b_ref[...].astype(F32) + c_ref[...].astype(F32)
-    out_ref[...] = total.astype(BF16)
-
-
-def fold_kernel(parts_ref, residual_ref, out_ref):
-    total = residual_ref[...].astype(F32)
-    for k in range(4):
-        total = total + parts_ref[k].astype(F32)
-    out_ref[...] = total
+    total = own_ref[...] + a_ref[...].astype(F32) + b_ref[...].astype(F32)
+    out_ref[...] = (total + c_ref[:16, :].astype(F32)).astype(BF16)
+
+
+def fold_kernel(own_ref, a_ref, b_ref, c_ref, residual_ref, out_ref):
+    total = residual_ref[...].astype(F32) + own_ref[...]
+    total = total + a_ref[...].astype(F32) + b_ref[...].astype(F32)
+    out_ref[...] = total + c_ref[16:, :].astype(F32)
 
 
 def finish_kernel(near_ref, far_ref, gain_ref, hidden_ref, normed_ref):
@@ -293,21 +283,24 @@
     got = lax.ppermute(send, "tp", [(i, i ^ 1) for i in range(16)])
     keep = call(keep_kernel, of((SPAN // 2, D), F32), [VMEM, VMEM], keep, weight)
     full = of((16, D), BF16)
-    own, *parts = call(
-        far_kernel, (of((16, D), F32), full, full, full), [VMEM, VMEM], keep, got
-    )
-    parts = [
-        lax.ppermute(sent, "tp", [(i, i ^ (2 * k)) for i in range(16)])
-        for k, sent in enumerate(parts, 1)
-    ]
-    near = call(
-        near_kernel, pltpu.HBM((4, 16, D), BF16), [VMEM, VMEM], keep, got,
-        scratch=[pltpu.VMEM((4, 16, D), BF16), pltpu.SemaphoreType.DMA((4,))], outs=HBM,
-    )
-    near = lax.all_to_all(near, "tp", 0, 0, axis_index_groups=NEAR_CHIPS)
-    away = call(sum_kernel, full, [VMEM] * 4, own, *parts, cost=LONG)
+    wide = of((16, D), F32)
+
+    def to_chip(sent, k):
+        return lax.ppermute(sent, "tp", [(i, i ^ (2 * k)) for i in range(16)])
+
+    own, far_c, far_b, both = call(
+        functools.partial(slab_kernel, ((0, 16), (16, 32), (32, 48), (48, 80))),
+        (wide, full, full, of((32, D), BF16)), [VMEM, VMEM], keep, got,
+    )
+    far_c, far_b, both = to_chip(far_c, 3), to_chip(far_b, 2), to_chip(both, 1)
+    near_c, near_b, mine = call(
+        functools.partial(slab_kernel, ((80, 96), (96, 112), (112, 128))),
+        (full, full, wide), [VMEM, VMEM], keep, got, cost=LONG,
+    )
+    near_c, near_b = to_chip(near_c, 3), to_chip(near_b, 2)
+    away = call(sum_kernel, full, [VMEM] * 4, own, far_c, far_b, both, cost=LONG)
     far = lax.ppermute(away, "tp", [(i, i ^ 8) for i in range(16)])
-    folded = call(fold_kernel, of((16, D), F32), [VMEM] * 2, near, residual_in)
+    folded = call(fold_kernel, wide, [VMEM] * 5, mine, near_c, near_b, both, residual_in)
     return call(finish_kernel, (full, full), [VMEM] * 3, folded, far, norm_gain[None, :])
 
 

time: 99.2 us -> 96.7 us (0.975)
  the two profiles are of different devices: /device:TPU:32 before, /device:TPU:2 now
where the time goes in v12:
time: 96.7 us; the launch traced here: 96.2 us
  starting transfers between devices  43.5 us (45%)
  blocking collectives  22.7 us (23%)
  waiting for transfers between devices  16.5 us (17%)
  Pallas kernels  8.45 us (9%)
  local copies, waits for them, and re-layouts  4.13 us (4%)
    ppermute x5, starting transfers between devices, to_chip(): return lax.ppermute(sent, 'tp', [(i, i ^ 2 * k) for i in range(16)])  15.9 us
    ppermute x1, starting transfers between devices, shards(): other = lax.ppermute(local, 'seq', FLIP_Z)  15.7 us
    all_to_all x1, blocking collectives, shards(): rows = lax.all_to_all(pairs, 'seq', 0, 0, axis_index_groups=ROW_Y)  12.1 us
    all_to_all x1, blocking collectives, shards(): cols = lax.all_to_all(totals, 'seq', 0, 0, axis_index_groups=ROW_X)  10.6 us
    ppermute x1, starting transfers between devices, shards(): far = lax.ppermute(away, 'tp', [(i, i ^ 8) for i in range(16)])  9.94 us
    ppermute x1, waiting for transfers between devices, shards(): far = lax.ppermute(away, 'tp', [(i, i ^ 8) for i in range(16)])  9.17 us
    pallas_call x11, Pallas kernels, call(): pl.pallas_call(body, out_shape=shapes, in_specs=specs, out_specs=jax.tree...  8.45 us
    ppermute x5, waiting for transfers between devices, to_chip(): return lax.ppermute(sent, 'tp', [(i, i ^ 2 * k) for i in range(16)])  5.42 us
  transfers between devices with their start and end apart: 8, of which 4 were waited for; matrix products, arithmetic and copies ran while one was open for 0% of the time, Pallas kernels for 3%

profile of v12, /device:TPU:2, one launch (start us, length us, event | category | flops | bytes accessed | tf_op | source)
XLA Modules:
  0.0 96.2 jit_solution(11359404257900205348)
XLA Ops:
  0.6 1.7 %shard_map.95.own_ref = bf16[392,128]{1,0:T(8,128)(2,1)S(1)} custom-call(s32[1,3]{1,0:T(1,128)} %starts_ref.1, f32[3,256]{1,0:T(4,128)} %decay_ref.1, bf16[256,384]{1,0:T(8,128)(2,1)} %key_ref.1, bf16[256,384]{1,0:T(8,128)(2,1)} %value_ref.1), custom_call_target="tpu_custom_call" | custom-call | tf_op jit(solution)/shard_map/pallas_call | solution.py:227
  2.4 15.7 %collective-permute-start = (bf16[392,128]{1,0:T(8,128)(2,1)S(1)}, bf16[392,128]{1,0:T(8,128)(2,1)S(1)}, u32[]{:S(2)}, u32[]{:S(2)}) collective-permute-start(bf16[392,128]{1,0:T(8,128)(2,1)S(1)} %shard_map.95.own_ref), channel_id=1, source_target_pairs={{0,16},{16,0},{32,48},{48,32},{64,80},{80,64},{96,112},{112,96},{1... | collective-permute-start | bytes 301064 | tf_op jit(solution)/shard_map/ppermute | solution.py:262
  18.1 0.0 copy-start
  18.1 0.9 copy-done
  19.0 0.0 copy-start.2
  19.0 0.9 copy-done.2
  20.0 0.0 copy-start.3
  20.0 0.9 copy-done.3
  20.9 0.0 copy-start.5
  20.9 0.7 copy-done.5
  21.6 0.0 copy-start.7
  21.6 0.7 copy-done.7
  22.2 0.0 copy-start.1
  22.2 2.4 %shard_map.96 = (f32[256,384]{1,0:T(8,128)S(1)}, f32[256,3]{1,0:T(8,128)S(1)}, bf16[384,4096]{1,0:T(8,128)(2,1)S(1)}) custom-call(s32[1,3]{1,0:T(1,128)S(1)} %copy-done.7, f32[3,256]{1,0:T(4,128)S(1)} %copy-done.5, bf16[256,384]{1,0:T(8,128)(2,1)S(1)} %copy-done, bf16[256,384]{1,0:T(8,128)(2,1)S(1)} %copy-done.2, bf16[256,384]{1,0:T(8,128)(2,1)S(1)} %copy-done.3, ...), custom_call_target="tpu_custom_call" | custom-call | tf_op jit(solution)/shard_map/pallas_call | solution.py:227
  24.7 0.1 pad_add_fusion.place_ref
  24.8 0.0 collective-permute-done.other_ref
  24.8 0.6 shard_map.97
  25.4 12.1 %all_to_all.10.parts_ref.row_ref = bf16[4,392,128]{2,1,0:T(8,128)(2,1)S(1)} all-to-all(bf16[4,392,128]{2,1,0:T(8,128)(2,1)S(1)} %shard_map.97), channel_id=1, replica_groups={{0,32,64,96},{16,48,80,112},{128,160,192,224},{144,176,208,240},{256,28..., dimensions={0} | all-to-all | bytes 802816 | tf_op jit(solution)/shard_map/all_to_all | solution.py:274
  37.5 0.1 shard_map.98
  37.6 10.6 %all_to_all.11.col_ref = bf16[4,392,128]{2,1,0:T(8,128)(2,1)S(1)} all-to-all(bf16[4,392,128]{2,1,0:T(8,128)(2,1)S(1)} %shard_map.98), channel_id=1, replica_groups={{0,128,256,384},{16,144,272,400},{32,160,288,416},{48,176,304,432},{64,..., dimensions={0} | all-to-all | bytes 802816 | tf_op jit(solution)/shard_map/all_to_all | solution.py:276
  48.2 0.0 copy-done.1
  48.2 1.7 %shard_map.99 = (bf16[128,4096]{1,0:T(8,128)(2,1)S(1)}, bf16[128,384]{1,0:T(8,128)(2,1)S(1)}) custom-call(s32[2]{0:T(128)S(1)} %pad_add_fusion.place_ref, bf16[256,384]{1,0:T(8,128)(2,1)S(1)} %copy-done.1, f32[256,384]{1,0:T(8,128)S(1)} %get-tuple-element.21.intra_ref, f32[256,3]{1,0:T(8,128)S(1)} %get-tuple-element.22.carry_ref, ...), custom_call_target="tpu_custom_call" | custom-call | tf_op jit(solution)/shard_map/pallas_call | solution.py:227
  49.9 1.9 %collective-permute-start.1 = (bf16[128,4096]{1,0:T(8,128)(2,1)S(1)}, bf16[128,4096]{1,0:T(8,128)(2,1)S(1)}, u32[]{:S(2)}, u32[]{:S(2)}) collective-permute-start(bf16[128,4096]{1,0:T(8,128)(2,1)S(1)} %get-tuple-element.26), channel_id=1, source_target_pairs={{0,1},{1,0},{2,3},{3,2},{4,5},{5,4},{6,7},{7,6},{8,9},{9,8},{10,11... | collective-permute-start | bytes 3145736 | tf_op jit(solution)/shard_map/ppermute | solution.py:283
  51.9 0.7 shard_map.100.keep_ref
  52.6 1.9 %collective-permute-done.1.got_ref = bf16[128,4096]{1,0:T(8,128)(2,1)S(1)} collective-permute-done((bf16[128,4096]{1,0:T(8,128)(2,1)S(1)}, bf16[128,4096]{1,0:T(8,128)(2,1)S(1)}, u32[]{:S(2)}, u32[]{:S(2)}) %collective-permute-start.1) | collective-permute-done | bytes 1048608 | tf_op jit(solution)/shard_map/ppermute | solution.py:283
  54.5 0.1 shard_map.102
  54.6 3.8 %collective-permute-start.5 = (bf16[16,4096]{1,0:T(8,128)(2,1)S(1)}, bf16[16,4096]{1,0:T(8,128)(2,1)S(1)}, u32[]{:S(2)}, u32[]{:S(2)}) collective-permute-start(bf16[16,4096]{1,0:T(8,128)(2,1)S(1)} %get-tuple-element.32), channel_id=1, source_target_pairs={{0,6},{1,7},{2,4},{3,5},{4,2},{5,3},{6,0},{7,1},{8,14},{9,15},{10,... | collective-permute-start | bytes 393224 | tf_op jit(solution)/shard_map/ppermute | solution.py:289
  58.5 2.6 %collective-permute-start.6 = (bf16[16,4096]{1,0:T(8,128)(2,1)S(1)}, bf16[16,4096]{1,0:T(8,128)(2,1)S(1)}, u32[]{:S(2)}, u32[]{:S(2)}) collective-permute-start(bf16[16,4096]{1,0:T(8,128)(2,1)S(1)} %get-tuple-element.33), channel_id=1, source_target_pairs={{0,4},{1,5},{2,6},{3,7},{4,0},{5,1},{6,2},{7,3},{8,12},{9,13},{10,... | collective-permute-start | bytes 393224 | tf_op jit(solution)/shard_map/ppermute | solution.py:289
  61.1 3.6 %collective-permute-start.4 = (bf16[32,4096]{1,0:T(8,128)(2,1)S(1)}, bf16[32,4096]{1,0:T(8,128)(2,1)S(1)}, u32[]{:S(2)}, u32[]{:S(2)}) collective-permute-start(bf16[32,4096]{1,0:T(8,128)(2,1)S(1)} %get-tuple-element.30), channel_id=1, source_target_pairs={{0,2},{1,3},{2,0},{3,1},{4,6},{5,7},{6,4},{7,5},{8,10},{9,11},{10,... | collective-permute-start | bytes 786440 | tf_op jit(solution)/shard_map/ppermute | solution.py:289
  64.8 0.1 shard_map.101
  64.9 3.8 %collective-permute-start.2 = (bf16[16,4096]{1,0:T(8,128)(2,1)S(1)}, bf16[16,4096]{1,0:T(8,128)(2,1)S(1)}, u32[]{:S(2)}, u32[]{:S(2)}) collective-permute-start(bf16[16,4096]{1,0:T(8,128)(2,1)S(1)} %get-tuple-element.28), channel_id=1, source_target_pairs={{0,6},{1,7},{2,4},{3,5},{4,2},{5,3},{6,0},{7,1},{8,14},{9,15},{10,... | collective-permute-start | bytes 393224 | tf_op jit(solution)/shard_map/ppermute | solution.py:289
  68.7 1.9 %collective-permute-start.3 = (bf16[16,4096]{1,0:T(8,128)(2,1)S(1)}, bf16[16,4096]{1,0:T(8,128)(2,1)S(1)}, u32[]{:S(2)}, u32[]{:S(2)}) collective-permute-start(bf16[16,4096]{1,0:T(8,128)(2,1)S(1)} %get-tuple-element.29), channel_id=1, source_target_pairs={{0,4},{1,5},{2,6},{3,7},{4,0},{5,1},{6,2},{7,3},{8,12},{9,13},{10,... | collective-permute-start | bytes 393224 | tf_op jit(solution)/shard_map/ppermute | solution.py:289
  70.6 0.0 collective-permute-done.5.a_ref
  70.7 2.3 %collective-permute-done.6.b_ref = bf16[16,4096]{1,0:T(8,128)(2,1)S(1)} collective-permute-done((bf16[16,4096]{1,0:T(8,128)(2,1)S(1)}, bf16[16,4096]{1,0:T(8,128)(2,1)S(1)}, u32[]{:S(2)}, u32[]{:S(2)}) %collective-permute-start.6) | collective-permute-done | bytes 131104 | tf_op jit(solution)/shard_map/ppermute | solution.py:289
  73.0 3.1 %collective-permute-done.4.c_ref = bf16[32,4096]{1,0:T(8,128)(2,1)S(1)} collective-permute-done((bf16[32,4096]{1,0:T(8,128)(2,1)S(1)}, bf16[32,4096]{1,0:T(8,128)(2,1)S(1)}, u32[]{:S(2)}, u32[]{:S(2)}) %collective-permute-start.4) | collective-permute-done | bytes 262176 | tf_op jit(solution)/shard_map/ppermute | solution.py:289
  76.1 0.0 copy-start.4
  76.1 0.0 copy-start.6
  76.1 0.1 shard_map.104
  76.1 9.9 %collective-permute-start.7 = (bf16[16,4096]{1,0:T(8,128)(2,1)S(1)}, bf16[16,4096]{1,0:T(8,128)(2,1)S(1)}, u32[]{:S(2)}, u32[]{:S(2)}) collective-permute-start(bf16[16,4096]{1,0:T(8,128)(2,1)S(1)} %shard_map.104), channel_id=1, source_target_pairs={{0,8},{1,9},{2,10},{3,11},{4,12},{5,13},{6,14},{7,15},{8,0},{9,1},... | collective-permute-start | bytes 393224 | tf_op jit(solution)/shard_map/ppermute | solution.py:302
  86.1 0.0 collective-permute-done.2.a_ref
  86.1 0.0 collective-permute-done.3.b_ref
  86.1 0.0 copy-done.4
  86.1 0.1 shard_map.103.near_ref
  86.2 9.2 %collective-permute-done.7.far_ref = bf16[16,4096]{1,0:T(8,128)(2,1)S(1)} collective-permute-done((bf16[16,4096]{1,0:T(8,128)(2,1)S(1)}, bf16[16,4096]{1,0:T(8,128)(2,1)S(1)}, u32[]{:S(2)}, u32[]{:S(2)}) %collective-permute-start.7) | collective-permute-done | bytes 131104 | tf_op jit(solution)/shard_map/ppermute | solution.py:302
  95.4 0.0 copy-done.6
  95.4 0.8 shard_map.105
Async XLA Ops:
  2.4 22.4 %collective-permute-start = (bf16[392,128]{1,0:T(8,128)(2,1)S(1)}, bf16[392,128]{1,0:T(8,128)(2,1)S(1)}, u32[]{:S(2)}, u32[]{:S(2)}) collective-permute-start(bf16[392,128]{1,0:T(8,128)(2,1)S(1)} %shard_map.95.own_ref), channel_id=1, source_target_pairs={{0,16},{16,0},{32,48},{48,32},{64,80},{80,64},{96,112},{112,96},{1... | collective-permute-start | bytes 301064 | tf_op jit(solution)/shard_map/ppermute | solution.py:262
  18.1 0.9 copy-start
  19.0 0.9 copy-start.2
  20.0 0.9 copy-start.3
  20.9 0.7 copy-start.5
  21.6 0.7 copy-start.7
  22.2 26.0 %copy-start.1 = (bf16[256,384]{1,0:T(8,128)(2,1)S(1)}, bf16[256,384]{1,0:T(8,128)(2,1)}, u32[]{:S(2)}) copy-start(bf16[256,384]{1,0:T(8,128)(2,1)} %query_ref.2) | copy-start | bytes 589828
  49.9 4.6 %collective-permute-start.1 = (bf16[128,4096]{1,0:T(8,128)(2,1)S(1)}, bf16[128,4096]{1,0:T(8,128)(2,1)S(1)}, u32[]{:S(2)}, u32[]{:S(2)}) collective-permute-start(bf16[128,4096]{1,0:T(8,128)(2,1)S(1)} %get-tuple-element.26), channel_id=1, source_target_pairs={{0,1},{1,0},{2,3},{3,2},{4,5},{5,4},{6,7},{7,6},{8,9},{9,8},{10,11... | collective-permute-start | bytes 3145736 | tf_op jit(solution)/shard_map/ppermute | solution.py:283
  54.6 16.0 %collective-permute-start.5 = (bf16[16,4096]{1,0:T(8,128)(2,1)S(1)}, bf16[16,4096]{1,0:T(8,128)(2,1)S(1)}, u32[]{:S(2)}, u32[]{:S(2)}) collective-permute-start(bf16[16,4096]{1,0:T(8,128)(2,1)S(1)} %get-tuple-element.32), channel_id=1, source_target_pairs={{0,6},{1,7},{2,4},{3,5},{4,2},{5,3},{6,0},{7,1},{8,14},{9,15},{10,... | collective-permute-start | bytes 393224 | tf_op jit(solution)/shard_map/ppermute | solution.py:289
  58.5 14.5 %collective-permute-start.6 = (bf16[16,4096]{1,0:T(8,128)(2,1)S(1)}, bf16[16,4096]{1,0:T(8,128)(2,1)S(1)}, u32[]{:S(2)}, u32[]{:S(2)}) collective-permute-start(bf16[16,4096]{1,0:T(8,128)(2,1)S(1)} %get-tuple-element.33), channel_id=1, source_target_pairs={{0,4},{1,5},{2,6},{3,7},{4,0},{5,1},{6,2},{7,3},{8,12},{9,13},{10,... | collective-permute-start | bytes 393224 | tf_op jit(solution)/shard_map/ppermute | solution.py:289
  61.1 14.9 %collective-permute-start.4 = (bf16[32,4096]{1,0:T(8,128)(2,1)S(1)}, bf16[32,4096]{1,0:T(8,128)(2,1)S(1)}, u32[]{:S(2)}, u32[]{:S(2)}) collective-permute-start(bf16[32,4096]{1,0:T(8,128)(2,1)S(1)} %get-tuple-element.30), channel_id=1, source_target_pairs={{0,2},{1,3},{2,0},{3,1},{4,6},{5,7},{6,4},{7,5},{8,10},{9,11},{10,... | collective-permute-start | bytes 786440 | tf_op jit(solution)/shard_map/ppermute | solution.py:289
  64.9 21.2 %collective-permute-start.2 = (bf16[16,4096]{1,0:T(8,128)(2,1)S(1)}, bf16[16,4096]{1,0:T(8,128)(2,1)S(1)}, u32[]{:S(2)}, u32[]{:S(2)}) collective-permute-start(bf16[16,4096]{1,0:T(8,128)(2,1)S(1)} %get-tuple-element.28), channel_id=1, source_target_pairs={{0,6},{1,7},{2,4},{3,5},{4,2},{5,3},{6,0},{7,1},{8,14},{9,15},{10,... | collective-permute-start | bytes 393224 | tf_op jit(solution)/shard_map/ppermute | solution.py:289
  68.7 17.4 %collective-permute-start.3 = (bf16[16,4096]{1,0:T(8,128)(2,1)S(1)}, bf16[16,4096]{1,0:T(8,128)(2,1)S(1)}, u32[]{:S(2)}, u32[]{:S(2)}) collective-permute-start(bf16[16,4096]{1,0:T(8,128)(2,1)S(1)} %get-tuple-element.29), channel_id=1, source_target_pairs={{0,4},{1,5},{2,6},{3,7},{4,0},{5,1},{6,2},{7,3},{8,12},{9,13},{10,... | collective-permute-start | bytes 393224 | tf_op jit(solution)/shard_map/ppermute | solution.py:289
  76.1 10.0 %copy-start.4 = (bf16[16,4096]{1,0:T(8,128)(2,1)S(1)}, bf16[16,4096]{1,0:T(8,128)(2,1)}, u32[]{:S(2)}) copy-start(bf16[16,4096]{1,0:T(8,128)(2,1)} %residual_ref.1) | copy-start | bytes 393220
  76.1 19.3 %copy-start.6 = (f32[4096]{0:T(1024)S(1)}, f32[4096]{0:T(1024)}, u32[]{:S(2)}) copy-start(f32[4096]{0:T(1024)} %param.15) | copy-start | bytes 49156
  76.1 19.2 %collective-permute-start.7 = (bf16[16,4096]{1,0:T(8,128)(2,1)S(1)}, bf16[16,4096]{1,0:T(8,128)(2,1)S(1)}, u32[]{:S(2)}, u32[]{:S(2)}) collective-permute-start(bf16[16,4096]{1,0:T(8,128)(2,1)S(1)} %shard_map.104), channel_id=1, source_target_pairs={{0,8},{1,9},{2,10},{3,11},{4,12},{5,13},{6,14},{7,15},{8,0},{9,1},... | collective-permute-start | bytes 393224 | tf_op jit(solution)/shard_map/ppermute | solution.py:302

commit v13 on v9

--- a/solution.py
+++ b/solution.py
@@ -18,7 +18,7 @@
 FLIP_Z = [(i, i ^ 1) for i in range(SHARDS)]
 ROW_Y = [[g + 2 * k for k in range(4)] for g in range(SHARDS) if g & 6 == 0]
 ROW_X = [[g + 8 * k for k in range(4)] for g in range(8)]
-FAR_ORDER = (0, 3, 2, 1)
+FAR_ORDER = (0, 2, 3, 1)
 LONG = pl.CostEstimate(flops=10**11, bytes_accessed=0, transcendentals=0)
 NEAR_CHIPS = [[8 * g + 2 * k + core for k in range(4)] for g in range(2) for core in range(2)]
 

time: 93.8 us -> 94.7 us (level)
  waiting for transfers between devices: 16.5 us -> 17.9 us
    all_to_all x1, waiting for transfers between devices: 8.36 us -> 6.18 us  [shards(): near = lax.all_to_all(near, 'tp', 0, 0, axis_index_groups=NEAR_CHIPS)]
    ppermute x1, waiting for transfers between devices: 6.18 us -> 8.36 us  [shards(): far = lax.ppermute(away, 'tp', [(i, i ^ 8) for i in range(16)])]
    all_to_all x1, starting transfers between devices: 5.8 us -> 4.2 us  [shards(): near = lax.all_to_all(near, 'tp', 0, 0, axis_index_groups=NEAR_CHIPS)]
    ppermute x3, waiting for transfers between devices: 0.01 us -> 1.42 us  [shards(): lax.ppermute(sent, 'tp', [(i, i ^ 2 * k) for i in range(16)])]
  transfers between devices with their start and end apart: 7 -> 7, of which waited for: 3 -> 4; matrix products, arithmetic and copies ran while one was open for 0% -> 0% of each run, Pallas kernels for 4% -> 4%
where the time goes in v13:
time: 94.7 us; the launch traced here: 94.2 us
  starting transfers between devices  38.5 us (41%)
  blocking collectives  23.7 us (25%)
  waiting for transfers between devices  17.9 us (19%)
  Pallas kernels  9.17 us (10%)
  local copies, waits for them, and re-layouts  4.13 us (4%)
    ppermute x1, starting transfers between devices, shards(): other = lax.ppermute(local, 'seq', FLIP_Z)  13.9 us
    all_to_all x1, blocking collectives, shards(): rows = lax.all_to_all(pairs, 'seq', 0, 0, axis_index_groups=ROW_Y)  12.1 us
    all_to_all x1, blocking collectives, shards(): cols = lax.all_to_all(totals, 'seq', 0, 0, axis_index_groups=ROW_X)  11.5 us
    ppermute x3, starting transfers between devices, shards(): lax.ppermute(sent, 'tp', [(i, i ^ 2 * k) for i in range(16)])  10.1 us
    pallas_call x11, Pallas kernels, call(): pl.pallas_call(body, out_shape=shapes, in_specs=specs, out_specs=jax.tree...  9.17 us
    ppermute x1, waiting for transfers between devices, shards(): far = lax.ppermute(away, 'tp', [(i, i ^ 8) for i in range(16)])  8.36 us
    ppermute x1, starting transfers between devices, shards(): far = lax.ppermute(away, 'tp', [(i, i ^ 8) for i in range(16)])  8.32 us
    all_to_all x1, waiting for transfers between devices, shards(): near = lax.all_to_all(near, 'tp', 0, 0, axis_index_groups=NEAR_CHIPS)  6.18 us
  transfers between devices with their start and end apart: 7, of which 4 were waited for; matrix products, arithmetic and copies ran while one was open for 0% of the time, Pallas kernels for 4%

profile of v13, /device:TPU:64, one launch (start us, length us, event | category | flops | bytes accessed | tf_op | source)
XLA Modules:
  0.0 94.2 jit_solution(1202031862442440288)
XLA Ops:
  0.6 1.7 %shard_map.95.own_ref = bf16[392,128]{1,0:T(8,128)(2,1)S(1)} custom-call(s32[1,3]{1,0:T(1,128)} %starts_ref.1, f32[3,256]{1,0:T(4,128)} %decay_ref.1, bf16[256,384]{1,0:T(8,128)(2,1)} %key_ref.1, bf16[256,384]{1,0:T(8,128)(2,1)} %value_ref.1), custom_call_target="tpu_custom_call" | custom-call | tf_op jit(solution)/shard_map/pallas_call | solution.py:238
  2.4 13.9 %collective-permute-start = (bf16[392,128]{1,0:T(8,128)(2,1)S(1)}, bf16[392,128]{1,0:T(8,128)(2,1)S(1)}, u32[]{:S(2)}, u32[]{:S(2)}) collective-permute-start(bf16[392,128]{1,0:T(8,128)(2,1)S(1)} %shard_map.95.own_ref), channel_id=1, source_target_pairs={{0,16},{16,0},{32,48},{48,32},{64,80},{80,64},{96,112},{112,96},{1... | collective-permute-start | bytes 301064 | tf_op jit(solution)/shard_map/ppermute | solution.py:273
  16.3 0.0 copy-start
  16.3 0.9 copy-done
  17.2 0.0 copy-start.2
  17.2 0.9 copy-done.2
  18.2 0.0 copy-start.3
  18.2 0.9 copy-done.3
  19.1 0.0 copy-start.5
  19.1 0.7 copy-done.5
  19.8 0.0 copy-start.7
  19.8 0.7 copy-done.7
  20.4 0.0 copy-start.1
  20.4 2.4 %shard_map.96 = (f32[256,384]{1,0:T(8,128)S(1)}, f32[256,3]{1,0:T(8,128)S(1)}, bf16[384,4096]{1,0:T(8,128)(2,1)S(1)}) custom-call(s32[1,3]{1,0:T(1,128)S(1)} %copy-done.7, f32[3,256]{1,0:T(4,128)S(1)} %copy-done.5, bf16[256,384]{1,0:T(8,128)(2,1)S(1)} %copy-done, bf16[256,384]{1,0:T(8,128)(2,1)S(1)} %copy-done.2, bf16[256,384]{1,0:T(8,128)(2,1)S(1)} %copy-done.3, ...), custom_call_target="tpu_custom_call" | custom-call | tf_op jit(solution)/shard_map/pallas_call | solution.py:238
  22.9 0.1 pad_add_fusion.place_ref
  23.0 0.0 collective-permute-done.other_ref
  23.0 0.6 shard_map.97
  23.6 12.1 %all_to_all.15.parts_ref.row_ref = bf16[4,392,128]{2,1,0:T(8,128)(2,1)S(1)} all-to-all(bf16[4,392,128]{2,1,0:T(8,128)(2,1)S(1)} %shard_map.97), channel_id=1, replica_groups={{0,32,64,96},{16,48,80,112},{128,160,192,224},{144,176,208,240},{256,28..., dimensions={0} | all-to-all | bytes 802816 | tf_op jit(solution)/shard_map/all_to_all | solution.py:285
  35.7 0.1 shard_map.98
  35.8 11.5 %all_to_all.16.col_ref = bf16[4,392,128]{2,1,0:T(8,128)(2,1)S(1)} all-to-all(bf16[4,392,128]{2,1,0:T(8,128)(2,1)S(1)} %shard_map.98), channel_id=1, replica_groups={{0,128,256,384},{16,144,272,400},{32,160,288,416},{48,176,304,432},{64,..., dimensions={0} | all-to-all | bytes 802816 | tf_op jit(solution)/shard_map/all_to_all | solution.py:287
  47.3 0.0 copy-done.1
  47.3 1.7 %shard_map.99 = (bf16[128,4096]{1,0:T(8,128)(2,1)S(1)}, bf16[128,384]{1,0:T(8,128)(2,1)S(1)}) custom-call(s32[2]{0:T(128)S(1)} %pad_add_fusion.place_ref, bf16[256,384]{1,0:T(8,128)(2,1)S(1)} %copy-done.1, f32[256,384]{1,0:T(8,128)S(1)} %get-tuple-element.18.intra_ref, f32[256,3]{1,0:T(8,128)S(1)} %get-tuple-element.19.carry_ref, ...), custom_call_target="tpu_custom_call" | custom-call | tf_op jit(solution)/shard_map/pallas_call | solution.py:238
  49.0 1.9 %collective-permute-start.1 = (bf16[128,4096]{1,0:T(8,128)(2,1)S(1)}, bf16[128,4096]{1,0:T(8,128)(2,1)S(1)}, u32[]{:S(2)}, u32[]{:S(2)}) collective-permute-start(bf16[128,4096]{1,0:T(8,128)(2,1)S(1)} %get-tuple-element.23), channel_id=1, source_target_pairs={{0,1},{1,0},{2,3},{3,2},{4,5},{5,4},{6,7},{7,6},{8,9},{9,8},{10,11... | collective-permute-start | bytes 3145736 | tf_op jit(solution)/shard_map/ppermute | solution.py:294
  51.0 0.7 shard_map.100.keep_ref
  51.7 1.9 %collective-permute-done.1.got_ref = bf16[128,4096]{1,0:T(8,128)(2,1)S(1)} collective-permute-done((bf16[128,4096]{1,0:T(8,128)(2,1)S(1)}, bf16[128,4096]{1,0:T(8,128)(2,1)S(1)}, u32[]{:S(2)}, u32[]{:S(2)}) %collective-permute-start.1) | collective-permute-done | bytes 1048608 | tf_op jit(solution)/shard_map/ppermute | solution.py:294
  53.6 0.1 shard_map.103
  53.7 3.4 %collective-permute-start.2 = (bf16[16,4096]{1,0:T(8,128)(2,1)S(1)}, bf16[16,4096]{1,0:T(8,128)(2,1)S(1)}, u32[]{:S(2)}, u32[]{:S(2)}) collective-permute-start(bf16[16,4096]{1,0:T(8,128)(2,1)S(1)} %get-tuple-element.25), channel_id=1, source_target_pairs={{0,4},{1,5},{2,6},{3,7},{4,0},{5,1},{6,2},{7,3},{8,12},{9,13},{10,... | collective-permute-start | bytes 393224 | tf_op jit(solution)/shard_map/ppermute | solution.py:301
  57.1 2.9 %collective-permute-start.3 = (bf16[16,4096]{1,0:T(8,128)(2,1)S(1)}, bf16[16,4096]{1,0:T(8,128)(2,1)S(1)}, u32[]{:S(2)}, u32[]{:S(2)}) collective-permute-start(bf16[16,4096]{1,0:T(8,128)(2,1)S(1)} %get-tuple-element.26), channel_id=1, source_target_pairs={{0,6},{1,7},{2,4},{3,5},{4,2},{5,3},{6,0},{7,1},{8,14},{9,15},{10,... | collective-permute-start | bytes 393224 | tf_op jit(solution)/shard_map/ppermute | solution.py:301
  60.0 3.8 %collective-permute-start.4 = (bf16[16,4096]{1,0:T(8,128)(2,1)S(1)}, bf16[16,4096]{1,0:T(8,128)(2,1)S(1)}, u32[]{:S(2)}, u32[]{:S(2)}) collective-permute-start(bf16[16,4096]{1,0:T(8,128)(2,1)S(1)} %get-tuple-element.27), channel_id=1, source_target_pairs={{0,2},{1,3},{2,0},{3,1},{4,6},{5,7},{6,4},{7,5},{8,10},{9,11},{10,... | collective-permute-start | bytes 393224 | tf_op jit(solution)/shard_map/ppermute | solution.py:301
  63.8 0.9 shard_map.101
  64.7 4.2 %all-to-all-start.2 = ((bf16[4,16,4096]{2,1,0:T(8,128)(2,1)}), bf16[4,16,4096]{2,1,0:T(8,128)(2,1)S(1)}, u32[]{:S(2)}, u32[]{:S(2)}) async-start(bf16[4,16,4096]{2,1,0:T(8,128)(2,1)} %shard_map.101), calls=%async_computation.2 | async-start | bytes 1048576 | tf_op jit(solution)/shard_map/all_to_all | solution.py:308
  68.9 0.0 collective-permute-done.2.a_ref
  68.9 1.4 %collective-permute-done.3.b_ref = bf16[16,4096]{1,0:T(8,128)(2,1)S(1)} collective-permute-done((bf16[16,4096]{1,0:T(8,128)(2,1)S(1)}, bf16[16,4096]{1,0:T(8,128)(2,1)S(1)}, u32[]{:S(2)}, u32[]{:S(2)}) %collective-permute-start.3) | collective-permute-done | bytes 131104 | tf_op jit(solution)/shard_map/ppermute | solution.py:301
  70.3 0.0 collective-permute-done.4.c_ref
  70.3 0.0 copy-start.4
  70.3 0.0 copy-start.6
  70.3 0.1 shard_map.104
  70.4 8.3 %collective-permute-start.5 = (bf16[16,4096]{1,0:T(8,128)(2,1)S(1)}, bf16[16,4096]{1,0:T(8,128)(2,1)S(1)}, u32[]{:S(2)}, u32[]{:S(2)}) collective-permute-start(bf16[16,4096]{1,0:T(8,128)(2,1)S(1)} %shard_map.104), channel_id=1, source_target_pairs={{0,8},{1,9},{2,10},{3,11},{4,12},{5,13},{6,14},{7,15},{8,0},{9,1},... | collective-permute-start | bytes 393224 | tf_op jit(solution)/shard_map/ppermute | solution.py:310
  78.7 6.2 %all-to-all-done.2.parts_ref = bf16[4,16,4096]{2,1,0:T(8,128)(2,1)S(1)} async-done(((bf16[4,16,4096]{2,1,0:T(8,128)(2,1)}), bf16[4,16,4096]{2,1,0:T(8,128)(2,1)S(1)}, u32[]{:S(2)}, u32[]{:S(2)}) %all-to-all-start.2) | async-done | bytes 524320 | tf_op jit(solution)/shard_map/all_to_all | solution.py:308
  84.9 0.0 copy-done.4
  84.9 0.1 shard_map.102.near_ref
  85.0 8.4 %collective-permute-done.5.far_ref = bf16[16,4096]{1,0:T(8,128)(2,1)S(1)} collective-permute-done((bf16[16,4096]{1,0:T(8,128)(2,1)S(1)}, bf16[16,4096]{1,0:T(8,128)(2,1)S(1)}, u32[]{:S(2)}, u32[]{:S(2)}) %collective-permute-start.5) | collective-permute-done | bytes 131104 | tf_op jit(solution)/shard_map/ppermute | solution.py:310
  93.4 0.0 copy-done.6
  93.4 0.8 shard_map.105
Async XLA Ops:
  2.4 20.6 %collective-permute-start = (bf16[392,128]{1,0:T(8,128)(2,1)S(1)}, bf16[392,128]{1,0:T(8,128)(2,1)S(1)}, u32[]{:S(2)}, u32[]{:S(2)}) collective-permute-start(bf16[392,128]{1,0:T(8,128)(2,1)S(1)} %shard_map.95.own_ref), channel_id=1, source_target_pairs={{0,16},{16,0},{32,48},{48,32},{64,80},{80,64},{96,112},{112,96},{1... | collective-permute-start | bytes 301064 | tf_op jit(solution)/shard_map/ppermute | solution.py:273
  16.3 0.9 copy-start
  17.2 0.9 copy-start.2
  18.2 0.9 copy-start.3
  19.1 0.7 copy-start.5
  19.8 0.7 copy-start.7
  20.4 26.9 %copy-start.1 = (bf16[256,384]{1,0:T(8,128)(2,1)S(1)}, bf16[256,384]{1,0:T(8,128)(2,1)}, u32[]{:S(2)}) copy-start(bf16[256,384]{1,0:T(8,128)(2,1)} %query_ref.2) | copy-start | bytes 589828
  49.0 4.6 %collective-permute-start.1 = (bf16[128,4096]{1,0:T(8,128)(2,1)S(1)}, bf16[128,4096]{1,0:T(8,128)(2,1)S(1)}, u32[]{:S(2)}, u32[]{:S(2)}) collective-permute-start(bf16[128,4096]{1,0:T(8,128)(2,1)S(1)} %get-tuple-element.23), channel_id=1, source_target_pairs={{0,1},{1,0},{2,3},{3,2},{4,5},{5,4},{6,7},{7,6},{8,9},{9,8},{10,11... | collective-permute-start | bytes 3145736 | tf_op jit(solution)/shard_map/ppermute | solution.py:294
  53.7 15.2 %collective-permute-start.2 = (bf16[16,4096]{1,0:T(8,128)(2,1)S(1)}, bf16[16,4096]{1,0:T(8,128)(2,1)S(1)}, u32[]{:S(2)}, u32[]{:S(2)}) collective-permute-start(bf16[16,4096]{1,0:T(8,128)(2,1)S(1)} %get-tuple-element.25), channel_id=1, source_target_pairs={{0,4},{1,5},{2,6},{3,7},{4,0},{5,1},{6,2},{7,3},{8,12},{9,13},{10,... | collective-permute-start | bytes 393224 | tf_op jit(solution)/shard_map/ppermute | solution.py:301
  57.1 13.3 %collective-permute-start.3 = (bf16[16,4096]{1,0:T(8,128)(2,1)S(1)}, bf16[16,4096]{1,0:T(8,128)(2,1)S(1)}, u32[]{:S(2)}, u32[]{:S(2)}) collective-permute-start(bf16[16,4096]{1,0:T(8,128)(2,1)S(1)} %get-tuple-element.26), channel_id=1, source_target_pairs={{0,6},{1,7},{2,4},{3,5},{4,2},{5,3},{6,0},{7,1},{8,14},{9,15},{10,... | collective-permute-start | bytes 393224 | tf_op jit(solution)/shard_map/ppermute | solution.py:301
  60.0 10.3 %collective-permute-start.4 = (bf16[16,4096]{1,0:T(8,128)(2,1)S(1)}, bf16[16,4096]{1,0:T(8,128)(2,1)S(1)}, u32[]{:S(2)}, u32[]{:S(2)}) collective-permute-start(bf16[16,4096]{1,0:T(8,128)(2,1)S(1)} %get-tuple-element.27), channel_id=1, source_target_pairs={{0,2},{1,3},{2,0},{3,1},{4,6},{5,7},{6,4},{7,5},{8,10},{9,11},{10,... | collective-permute-start | bytes 393224 | tf_op jit(solution)/shard_map/ppermute | solution.py:301
  64.7 20.2 %all-to-all-start.2 = ((bf16[4,16,4096]{2,1,0:T(8,128)(2,1)}), bf16[4,16,4096]{2,1,0:T(8,128)(2,1)S(1)}, u32[]{:S(2)}, u32[]{:S(2)}) async-start(bf16[4,16,4096]{2,1,0:T(8,128)(2,1)} %shard_map.101), calls=%async_computation.2 | async-start | bytes 1048576 | tf_op jit(solution)/shard_map/all_to_all | solution.py:308
  70.3 14.6 %copy-start.4 = (bf16[16,4096]{1,0:T(8,128)(2,1)S(1)}, bf16[16,4096]{1,0:T(8,128)(2,1)}, u32[]{:S(2)}) copy-start(bf16[16,4096]{1,0:T(8,128)(2,1)} %residual_ref.1) | copy-start | bytes 393220
  70.3 23.0 %copy-start.6 = (f32[4096]{0:T(1024)S(1)}, f32[4096]{0:T(1024)}, u32[]{:S(2)}) copy-start(f32[4096]{0:T(1024)} %param.15) | copy-start | bytes 49156
  70.4 23.0 %collective-permute-start.5 = (bf16[16,4096]{1,0:T(8,128)(2,1)S(1)}, bf16[16,4096]{1,0:T(8,128)(2,1)S(1)}, u32[]{:S(2)}, u32[]{:S(2)}) collective-permute-start(bf16[16,4096]{1,0:T(8,128)(2,1)S(1)} %shard_map.104), channel_id=1, source_target_pairs={{0,8},{1,9},{2,10},{3,11},{4,12},{5,13},{6,14},{7,15},{8,0},{9,1},... | collective-permute-start | bytes 393224 | tf_op jit(solution)/shard_map/ppermute | solution.py:310

commit v14 on v9

--- a/solution.py
+++ b/solution.py
@@ -165,7 +165,7 @@
 
 def attend_kernel(
     place_ref, query_ref, intra_ref, carry_ref, other_ref, row_ref, col_ref, weight_ref,
-    send_ref, keep_ref, mixed_ref, sibling_ref,
+    far_ref, near_ref, keep_ref, mixed_ref, sibling_ref,
 ):
     odd = place_ref[0] & 1 == 1
     carry = carry_ref[...]
@@ -189,9 +189,9 @@
         own, sibling = start + core * 16, start + (1 - core) * 16
         keep_ref[cut, :] = mixed_ref[pl.ds(pl.multiple_of(own, 16), 16), :]
         sibling_ref[cut, :] = mixed_ref[pl.ds(pl.multiple_of(sibling, 16), 16), :]
-    send_ref[...] = jnp.dot(
-        sibling_ref[...], weight_ref[...], preferred_element_type=F32
-    ).astype(BF16)
+    send = jnp.dot(sibling_ref[...], weight_ref[...], preferred_element_type=F32).astype(BF16)
+    far_ref[...] = send[:64]
+    near_ref[...] = send[64:]
 
 
 def keep_kernel(own_ref, weight_ref, out_ref):
@@ -208,7 +208,8 @@
     copies = []
     for k in range(4):
         cut = slice(64 + k * 16, 80 + k * 16)
-        sum_ref[k] = (keep_ref[cut, :] + got_ref[cut, :].astype(F32)).astype(BF16)
+        got = got_ref[k * 16 : (k + 1) * 16, :]
+        sum_ref[k] = (keep_ref[cut, :] + got.astype(F32)).astype(BF16)
         copies.append(pltpu.make_async_copy(sum_ref.at[k], out_ref.at[k], sems.at[k]))
         copies[-1].start()
     for copy in copies:
@@ -285,24 +286,26 @@
     rows = lax.all_to_all(pairs, "seq", 0, 0, axis_index_groups=ROW_Y)
     totals = call(row_kernel, four, [VMEM], rows)
     cols = lax.all_to_all(totals, "seq", 0, 0, axis_index_groups=ROW_X)
-    send, keep = call(
-        attend_kernel, (of((SPAN // 2, D), BF16), of((SPAN // 2, STATE), BF16)),
+    quarter = of((SPAN // 4, D), BF16)
+    far, near, keep = call(
+        attend_kernel, (quarter, quarter, of((SPAN // 2, STATE), BF16)),
         [SMEM] + [VMEM] * 7,
         place, query_rows, intra, carry, other, rows, cols, weight,
         scratch=[pltpu.VMEM((SPAN, STATE), BF16), pltpu.VMEM((SPAN // 2, STATE), BF16)],
     )
-    got = lax.ppermute(send, "tp", [(i, i ^ 1) for i in range(16)])
+    got_far = lax.ppermute(far, "tp", [(i, i ^ 1) for i in range(16)])
+    got_near = lax.ppermute(near, "tp", [(i, i ^ 1) for i in range(16)])
     keep = call(keep_kernel, of((SPAN // 2, D), F32), [VMEM, VMEM], keep, weight)
     full = of((16, D), BF16)
     own, *parts = call(
-        far_kernel, (of((16, D), F32), full, full, full), [VMEM, VMEM], keep, got
+        far_kernel, (of((16, D), F32), full, full, full), [VMEM, VMEM], keep, got_far
     )
     parts = [
         lax.ppermute(sent, "tp", [(i, i ^ (2 * k)) for i in range(16)])
         for k, sent in zip(FAR_ORDER[1:], parts)
     ]
     near = call(
-        near_kernel, pltpu.HBM((4, 16, D), BF16), [VMEM, VMEM], keep, got,
+        near_kernel, pltpu.HBM((4, 16, D), BF16), [VMEM, VMEM], keep, got_near,
         scratch=[pltpu.VMEM((4, 16, D), BF16), pltpu.SemaphoreType.DMA((4,))], outs=HBM,
     )
     near = lax.all_to_all(near, "tp", 0, 0, axis_index_groups=NEAR_CHIPS)

time: 93.8 us -> 94.2 us (level)
  starting transfers between devices: 39 us -> 41.3 us
  waiting for transfers between devices: 16.5 us -> 14.4 us
    ppermute x1 -> x2, starting transfers between devices: 1.92 us -> 4.33 us  [the longest x1 2.41 us: shards(): got_near = lax.ppermute(near, 'tp', [(i, i ^ 1) for i in range(16)])]
    ppermute x1 -> x2, waiting for transfers between devices: 1.91 us -> 0.01 us  [the longest x1 0.01 us: shards(): got_far = lax.ppermute(far, 'tp', [(i, i ^ 1) for i in range(16)])]
  transfers between devices with their start and end apart: 7 -> 8, of which waited for: 3 -> 2; matrix products, arithmetic and copies ran while one was open for 0% -> 0% of each run, Pallas kernels for 4% -> 5%
where the time goes in v14:
time: 94.2 us; the launch traced here: 93.6 us
  starting transfers between devices  41.3 us (44%)
  blocking collectives  23.7 us (25%)
  waiting for transfers between devices  14.4 us (15%)
  Pallas kernels  9.19 us (10%)
  local copies, waits for them, and re-layouts  4.13 us (4%)
    ppermute x1, starting transfers between devices, shards(): other = lax.ppermute(local, 'seq', FLIP_Z)  13.9 us
    all_to_all x1, blocking collectives, shards(): rows = lax.all_to_all(pairs, 'seq', 0, 0, axis_index_groups=ROW_Y)  12.1 us
    all_to_all x1, blocking collectives, shards(): cols = lax.all_to_all(totals, 'seq', 0, 0, axis_index_groups=ROW_X)  11.5 us
    ppermute x3, starting transfers between devices, shards(): lax.ppermute(sent, 'tp', [(i, i ^ 2 * k) for i in range(16)])  9.21 us
    pallas_call x11, Pallas kernels, call(): pl.pallas_call(body, out_shape=shapes, in_specs=specs, out_specs=jax.tree...  9.19 us
    all_to_all x1, waiting for transfers between devices, shards(): near = lax.all_to_all(near, 'tp', 0, 0, axis_index_groups=NEAR_CHIPS)  8.26 us
    ppermute x1, starting transfers between devices, shards(): far = lax.ppermute(away, 'tp', [(i, i ^ 8) for i in range(16)])  8.07 us
    ppermute x1, waiting for transfers between devices, shards(): far = lax.ppermute(away, 'tp', [(i, i ^ 8) for i in range(16)])  6.15 us
  transfers between devices with their start and end apart: 8, of which 2 were waited for; matrix products, arithmetic and copies ran while one was open for 0% of the time, Pallas kernels for 5%

profile of v14, /device:TPU:64, one launch (start us, length us, event | category | flops | bytes accessed | tf_op | source)
XLA Modules:
  0.0 93.6 jit_solution(1226468262773788864)
XLA Ops:
  0.6 1.7 %shard_map.95.own_ref = bf16[392,128]{1,0:T(8,128)(2,1)S(1)} custom-call(s32[1,3]{1,0:T(1,128)} %starts_ref.1, f32[3,256]{1,0:T(4,128)} %decay_ref.1, bf16[256,384]{1,0:T(8,128)(2,1)} %key_ref.1, bf16[256,384]{1,0:T(8,128)(2,1)} %value_ref.1), custom_call_target="tpu_custom_call" | custom-call | tf_op jit(solution)/shard_map/pallas_call | solution.py:239
  2.4 13.9 %collective-permute-start = (bf16[392,128]{1,0:T(8,128)(2,1)S(1)}, bf16[392,128]{1,0:T(8,128)(2,1)S(1)}, u32[]{:S(2)}, u32[]{:S(2)}) collective-permute-start(bf16[392,128]{1,0:T(8,128)(2,1)S(1)} %shard_map.95.own_ref), channel_id=1, source_target_pairs={{0,16},{16,0},{32,48},{48,32},{64,80},{80,64},{96,112},{112,96},{1... | collective-permute-start | bytes 301064 | tf_op jit(solution)/shard_map/ppermute | solution.py:274
  16.3 0.0 copy-start
  16.3 0.9 copy-done
  17.2 0.0 copy-start.2
  17.2 0.9 copy-done.2
  18.2 0.0 copy-start.3
  18.2 0.9 copy-done.3
  19.1 0.0 copy-start.5
  19.1 0.7 copy-done.5
  19.8 0.0 copy-start.7
  19.8 0.7 copy-done.7
  20.4 0.0 copy-start.1
  20.4 2.4 %shard_map.96 = (f32[256,384]{1,0:T(8,128)S(1)}, f32[256,3]{1,0:T(8,128)S(1)}, bf16[384,4096]{1,0:T(8,128)(2,1)S(1)}) custom-call(s32[1,3]{1,0:T(1,128)S(1)} %copy-done.7, f32[3,256]{1,0:T(4,128)S(1)} %copy-done.5, bf16[256,384]{1,0:T(8,128)(2,1)S(1)} %copy-done, bf16[256,384]{1,0:T(8,128)(2,1)S(1)} %copy-done.2, bf16[256,384]{1,0:T(8,128)(2,1)S(1)} %copy-done.3, ...), custom_call_target="tpu_custom_call" | custom-call | tf_op jit(solution)/shard_map/pallas_call | solution.py:239
  22.9 0.1 pad_add_fusion.place_ref
  23.0 0.0 collective-permute-done.other_ref
  23.0 0.6 shard_map.97
  23.6 12.1 %all_to_all.15.parts_ref.row_ref = bf16[4,392,128]{2,1,0:T(8,128)(2,1)S(1)} all-to-all(bf16[4,392,128]{2,1,0:T(8,128)(2,1)S(1)} %shard_map.97), channel_id=1, replica_groups={{0,32,64,96},{16,48,80,112},{128,160,192,224},{144,176,208,240},{256,28..., dimensions={0} | all-to-all | bytes 802816 | tf_op jit(solution)/shard_map/all_to_all | solution.py:286
  35.7 0.1 shard_map.98
  35.8 11.5 %all_to_all.16.col_ref = bf16[4,392,128]{2,1,0:T(8,128)(2,1)S(1)} all-to-all(bf16[4,392,128]{2,1,0:T(8,128)(2,1)S(1)} %shard_map.98), channel_id=1, replica_groups={{0,128,256,384},{16,144,272,400},{32,160,288,416},{48,176,304,432},{64,..., dimensions={0} | all-to-all | bytes 802816 | tf_op jit(solution)/shard_map/all_to_all | solution.py:288
  47.3 0.0 copy-done.1
  47.3 1.7 %shard_map.99 = (bf16[64,4096]{1,0:T(8,128)(2,1)S(1)}, bf16[64,4096]{1,0:T(8,128)(2,1)S(1)}, bf16[128,384]{1,0:T(8,128)(2,1)S(1)}) custom-call(s32[2]{0:T(128)S(1)} %pad_add_fusion.place_ref, bf16[256,384]{1,0:T(8,128)(2,1)S(1)} %copy-done.1, f32[256,384]{1,0:T(8,128)S(1)} %get-tuple-element.19.intra_ref, f32[256,3]{1,0:T(8,128)S(1)} %get-tuple-element.20.carry_ref, ...), custom_call_target="tpu_custom_call" | custom-call | tf_op jit(solution)/shard_map/pallas_call | solution.py:239
  49.1 1.9 %collective-permute-start.2 = (bf16[64,4096]{1,0:T(8,128)(2,1)S(1)}, bf16[64,4096]{1,0:T(8,128)(2,1)S(1)}, u32[]{:S(2)}, u32[]{:S(2)}) collective-permute-start(bf16[64,4096]{1,0:T(8,128)(2,1)S(1)} %get-tuple-element.25), channel_id=1, source_target_pairs={{0,1},{1,0},{2,3},{3,2},{4,5},{5,4},{6,7},{7,6},{8,9},{9,8},{10,11... | collective-permute-start | bytes 1572872 | tf_op jit(solution)/shard_map/ppermute | solution.py:296
  51.0 2.4 %collective-permute-start.1 = (bf16[64,4096]{1,0:T(8,128)(2,1)S(1)}, bf16[64,4096]{1,0:T(8,128)(2,1)S(1)}, u32[]{:S(2)}, u32[]{:S(2)}) collective-permute-start(bf16[64,4096]{1,0:T(8,128)(2,1)S(1)} %get-tuple-element.24), channel_id=1, source_target_pairs={{0,1},{1,0},{2,3},{3,2},{4,5},{5,4},{6,7},{7,6},{8,9},{9,8},{10,11... | collective-permute-start | bytes 1572872 | tf_op jit(solution)/shard_map/ppermute | solution.py:297
  53.4 0.7 shard_map.100.keep_ref
  54.1 0.0 collective-permute-done.2.got_ref
  54.1 0.1 shard_map.103
  54.2 3.1 %collective-permute-start.3 = (bf16[16,4096]{1,0:T(8,128)(2,1)S(1)}, bf16[16,4096]{1,0:T(8,128)(2,1)S(1)}, u32[]{:S(2)}, u32[]{:S(2)}) collective-permute-start(bf16[16,4096]{1,0:T(8,128)(2,1)S(1)} %get-tuple-element.27), channel_id=1, source_target_pairs={{0,6},{1,7},{2,4},{3,5},{4,2},{5,3},{6,0},{7,1},{8,14},{9,15},{10,... | collective-permute-start | bytes 393224 | tf_op jit(solution)/shard_map/ppermute | solution.py:304
  57.3 4.1 %collective-permute-start.4 = (bf16[16,4096]{1,0:T(8,128)(2,1)S(1)}, bf16[16,4096]{1,0:T(8,128)(2,1)S(1)}, u32[]{:S(2)}, u32[]{:S(2)}) collective-permute-start(bf16[16,4096]{1,0:T(8,128)(2,1)S(1)} %get-tuple-element.28), channel_id=1, source_target_pairs={{0,4},{1,5},{2,6},{3,7},{4,0},{5,1},{6,2},{7,3},{8,12},{9,13},{10,... | collective-permute-start | bytes 393224 | tf_op jit(solution)/shard_map/ppermute | solution.py:304
  61.4 2.0 %collective-permute-start.5 = (bf16[16,4096]{1,0:T(8,128)(2,1)S(1)}, bf16[16,4096]{1,0:T(8,128)(2,1)S(1)}, u32[]{:S(2)}, u32[]{:S(2)}) collective-permute-start(bf16[16,4096]{1,0:T(8,128)(2,1)S(1)} %get-tuple-element.29), channel_id=1, source_target_pairs={{0,2},{1,3},{2,0},{3,1},{4,6},{5,7},{6,4},{7,5},{8,10},{9,11},{10,... | collective-permute-start | bytes 393224 | tf_op jit(solution)/shard_map/ppermute | solution.py:304
  63.5 0.0 collective-permute-done.1.got_ref
  63.5 0.9 shard_map.101
  64.3 5.8 %all-to-all-start.2 = ((bf16[4,16,4096]{2,1,0:T(8,128)(2,1)}), bf16[4,16,4096]{2,1,0:T(8,128)(2,1)S(1)}, u32[]{:S(2)}, u32[]{:S(2)}) async-start(bf16[4,16,4096]{2,1,0:T(8,128)(2,1)} %shard_map.101), calls=%async_computation.2 | async-start | bytes 1048576 | tf_op jit(solution)/shard_map/all_to_all | solution.py:311
  70.2 0.0 collective-permute-done.3.a_ref
  70.2 0.0 collective-permute-done.4.b_ref
  70.2 0.0 collective-permute-done.5.c_ref
  70.2 0.0 copy-start.4
  70.2 0.0 copy-start.6
  70.2 0.1 shard_map.104
  70.3 8.1 %collective-permute-start.6 = (bf16[16,4096]{1,0:T(8,128)(2,1)S(1)}, bf16[16,4096]{1,0:T(8,128)(2,1)S(1)}, u32[]{:S(2)}, u32[]{:S(2)}) collective-permute-start(bf16[16,4096]{1,0:T(8,128)(2,1)S(1)} %shard_map.104), channel_id=1, source_target_pairs={{0,8},{1,9},{2,10},{3,11},{4,12},{5,13},{6,14},{7,15},{8,0},{9,1},... | collective-permute-start | bytes 393224 | tf_op jit(solution)/shard_map/ppermute | solution.py:313
  78.3 8.3 %all-to-all-done.2.parts_ref = bf16[4,16,4096]{2,1,0:T(8,128)(2,1)S(1)} async-done(((bf16[4,16,4096]{2,1,0:T(8,128)(2,1)}), bf16[4,16,4096]{2,1,0:T(8,128)(2,1)S(1)}, u32[]{:S(2)}, u32[]{:S(2)}) %all-to-all-start.2) | async-done | bytes 524320 | tf_op jit(solution)/shard_map/all_to_all | solution.py:311
  86.6 0.0 copy-done.4
  86.6 0.1 shard_map.102.near_ref
  86.7 6.1 %collective-permute-done.6.far_ref = bf16[16,4096]{1,0:T(8,128)(2,1)S(1)} collective-permute-done((bf16[16,4096]{1,0:T(8,128)(2,1)S(1)}, bf16[16,4096]{1,0:T(8,128)(2,1)S(1)}, u32[]{:S(2)}, u32[]{:S(2)}) %collective-permute-start.6) | collective-permute-done | bytes 131104 | tf_op jit(solution)/shard_map/ppermute | solution.py:313
  92.8 0.0 copy-done.6
  92.8 0.8 shard_map.105
Async XLA Ops:
  2.4 20.6 %collective-permute-start = (bf16[392,128]{1,0:T(8,128)(2,1)S(1)}, bf16[392,128]{1,0:T(8,128)(2,1)S(1)}, u32[]{:S(2)}, u32[]{:S(2)}) collective-permute-start(bf16[392,128]{1,0:T(8,128)(2,1)S(1)} %shard_map.95.own_ref), channel_id=1, source_target_pairs={{0,16},{16,0},{32,48},{48,32},{64,80},{80,64},{96,112},{112,96},{1... | collective-permute-start | bytes 301064 | tf_op jit(solution)/shard_map/ppermute | solution.py:274
  16.3 0.9 copy-start
  17.2 0.9 copy-start.2
  18.2 0.9 copy-start.3
  19.1 0.7 copy-start.5
  19.8 0.7 copy-start.7
  20.4 26.9 %copy-start.1 = (bf16[256,384]{1,0:T(8,128)(2,1)S(1)}, bf16[256,384]{1,0:T(8,128)(2,1)}, u32[]{:S(2)}) copy-start(bf16[256,384]{1,0:T(8,128)(2,1)} %query_ref.2) | copy-start | bytes 589828
  49.1 5.1 %collective-permute-start.2 = (bf16[64,4096]{1,0:T(8,128)(2,1)S(1)}, bf16[64,4096]{1,0:T(8,128)(2,1)S(1)}, u32[]{:S(2)}, u32[]{:S(2)}) collective-permute-start(bf16[64,4096]{1,0:T(8,128)(2,1)S(1)} %get-tuple-element.25), channel_id=1, source_target_pairs={{0,1},{1,0},{2,3},{3,2},{4,5},{5,4},{6,7},{7,6},{8,9},{9,8},{10,11... | collective-permute-start | bytes 1572872 | tf_op jit(solution)/shard_map/ppermute | solution.py:296
  51.0 12.5 %collective-permute-start.1 = (bf16[64,4096]{1,0:T(8,128)(2,1)S(1)}, bf16[64,4096]{1,0:T(8,128)(2,1)S(1)}, u32[]{:S(2)}, u32[]{:S(2)}) collective-permute-start(bf16[64,4096]{1,0:T(8,128)(2,1)S(1)} %get-tuple-element.24), channel_id=1, source_target_pairs={{0,1},{1,0},{2,3},{3,2},{4,5},{5,4},{6,7},{7,6},{8,9},{9,8},{10,11... | collective-permute-start | bytes 1572872 | tf_op jit(solution)/shard_map/ppermute | solution.py:297
  54.2 15.9 %collective-permute-start.3 = (bf16[16,4096]{1,0:T(8,128)(2,1)S(1)}, bf16[16,4096]{1,0:T(8,128)(2,1)S(1)}, u32[]{:S(2)}, u32[]{:S(2)}) collective-permute-start(bf16[16,4096]{1,0:T(8,128)(2,1)S(1)} %get-tuple-element.27), channel_id=1, source_target_pairs={{0,6},{1,7},{2,4},{3,5},{4,2},{5,3},{6,0},{7,1},{8,14},{9,15},{10,... | collective-permute-start | bytes 393224 | tf_op jit(solution)/shard_map/ppermute | solution.py:304
  57.3 12.8 %collective-permute-start.4 = (bf16[16,4096]{1,0:T(8,128)(2,1)S(1)}, bf16[16,4096]{1,0:T(8,128)(2,1)S(1)}, u32[]{:S(2)}, u32[]{:S(2)}) collective-permute-start(bf16[16,4096]{1,0:T(8,128)(2,1)S(1)} %get-tuple-element.28), channel_id=1, source_target_pairs={{0,4},{1,5},{2,6},{3,7},{4,0},{5,1},{6,2},{7,3},{8,12},{9,13},{10,... | collective-permute-start | bytes 393224 | tf_op jit(solution)/shard_map/ppermute | solution.py:304
  61.4 8.7 %collective-permute-start.5 = (bf16[16,4096]{1,0:T(8,128)(2,1)S(1)}, bf16[16,4096]{1,0:T(8,128)(2,1)S(1)}, u32[]{:S(2)}, u32[]{:S(2)}) collective-permute-start(bf16[16,4096]{1,0:T(8,128)(2,1)S(1)} %get-tuple-element.29), channel_id=1, source_target_pairs={{0,2},{1,3},{2,0},{3,1},{4,6},{5,7},{6,4},{7,5},{8,10},{9,11},{10,... | collective-permute-start | bytes 393224 | tf_op jit(solution)/shard_map/ppermute | solution.py:304
  64.3 22.3 %all-to-all-start.2 = ((bf16[4,16,4096]{2,1,0:T(8,128)(2,1)}), bf16[4,16,4096]{2,1,0:T(8,128)(2,1)S(1)}, u32[]{:S(2)}, u32[]{:S(2)}) async-start(bf16[4,16,4096]{2,1,0:T(8,128)(2,1)} %shard_map.101), calls=%async_computation.2 | async-start | bytes 1048576 | tf_op jit(solution)/shard_map/all_to_all | solution.py:311
  70.2 16.4 %copy-start.4 = (bf16[16,4096]{1,0:T(8,128)(2,1)S(1)}, bf16[16,4096]{1,0:T(8,128)(2,1)}, u32[]{:S(2)}) copy-start(bf16[16,4096]{1,0:T(8,128)(2,1)} %residual_ref.1) | copy-start | bytes 393220
  70.2 22.7 %copy-start.6 = (f32[4096]{0:T(1024)S(1)}, f32[4096]{0:T(1024)}, u32[]{:S(2)}) copy-start(f32[4096]{0:T(1024)} %param.15) | copy-start | bytes 49156
  70.3 22.6 %collective-permute-start.6 = (bf16[16,4096]{1,0:T(8,128)(2,1)S(1)}, bf16[16,4096]{1,0:T(8,128)(2,1)S(1)}, u32[]{:S(2)}, u32[]{:S(2)}) collective-permute-start(bf16[16,4096]{1,0:T(8,128)(2,1)S(1)} %shard_map.104), channel_id=1, source_target_pairs={{0,8},{1,9},{2,10},{3,11},{4,12},{5,13},{6,14},{7,15},{8,0},{9,1},... | collective-permute-start | bytes 393224 | tf_op jit(solution)/shard_map/ppermute | solution.py:313
